TPU v7x, 512 devices: a whole 4x8x8 slice. The times are simulated.
512 devices in a mesh: cells: 128 (over y, z_hi, x, core), grp: 4 (over z_lo).
Axes of the slice: x: 4, y: 8, z: 8 (z_hi: 2, z_lo: 4; z = z_hi * 4 + z_lo), core: 2. Of those that a mesh axis runs over, the one named last changes fastest.
Arguments:
- fraction: float32 [3, 128, 4, 512], P(None, 'cells', 'grp'), may hold values from 0 to 1
- velocity: float32 [3, 128, 4, 512], P(None, 'cells', 'grp'), may hold values from -1.8 to 1.8
- anchor: int32 [3, 128, 4, 512], P(None, 'cells', 'grp'), may hold values from 0 to 254, as said below
- atom_types: int32 [128, 4, 512], P('cells', 'grp'), may hold values from 0 to 7
- counts: int32 [128, 4], P('cells', 'grp'), may hold values from 64 to 512, as said below
- type_table: float32 [3, 8], replicated, may hold values from 0.7 to 2.8, as said below
- target: float32 [512, 64, 256], P('cells', 'grp'), may hold values from -0.3 to 0.3
Outputs:
- final_velocity: float32 [3, 128, 4, 512], P(None, 'cells', 'grp')
- displacement: float32 [3, 128, 4, 512], P(None, 'cells', 'grp')
- potential: float32 [512, 64, 256], P('cells', 'grp')
Inputs may be any that keep to these rules, and one draw needn't show every extreme that they name: `counts`: some cell holds exactly 512 live atoms in every draw; dead slots follow the live ones. `anchor`: component 0 is below 4, component 1 below 16, component 2 below 255. `type_table`: all entries are positive.
All inputs are finite; a program needn't handle non-finite values.
Results may differ from a plain program's by a relative error of at most 0.0003.
Values sent between devices are 32-bit elements; how exact they have to be, the bound alone decides.
No kernel may reach another device: no remote copies, remote signals or barrier semaphores. Data moves between devices by JAX's collectives and lax.ppermute only.
A program may use at most 64 MiB of HBM per device.

v0:
```python
import jax
import jax.numpy as jnp
from jax import lax
from jax.sharding import PartitionSpec as P

STEPS = 2


EPSILON = 1e-06
TIME_STEP = 0.5
BLUR_KERNEL = (1.0 / 16.0, 4.0 / 16.0, 6.0 / 16.0, 4.0 / 16.0, 1.0 / 16.0)
BOX_KERNEL = (1.0 / 9.0,) * 9


def extended_2(cells, sides, width):
    for axis, dim in sides:
        count = lax.axis_size(axis)
        ends = count - 1
        head = lax.slice_in_dim(cells, 0, width, axis=dim)
        tail = lax.slice_in_dim(cells, cells.shape[dim] - width, cells.shape[dim], axis=dim)
        cells = jnp.concatenate(
            [
                lax.ppermute(tail, axis, [(i, (i + 1) % count) for i in range(ends)]),
                cells,
                lax.ppermute(head, axis, [((i + 1) % count, i) for i in range(ends)]),
            ],
            axis=dim,
        )
    return cells


def passed_along(block, axis, distance):
    devices = range(lax.axis_size(axis))
    route = [(i - distance, i) for i in devices if i - distance in devices]
    return lax.ppermute(block, axis, route)


def tap_valid(values, along_axis, kernel):
    radius = (len(kernel) - 1) // 2
    length = values.shape[along_axis] - 2 * radius
    summed = kernel[0] * lax.slice_in_dim(values, 0, length, axis=along_axis)
    for offset in range(1, len(kernel)):
        summed = summed + kernel[offset] * lax.slice_in_dim(
            values, offset, offset + length, axis=along_axis
        )
    return summed


def tap_padded(values, along_axis, kernel):
    radius = (len(kernel) - 1) // 2
    widths = [(0, 0)] * values.ndim
    widths[along_axis] = (radius, radius)
    return tap_valid(jnp.pad(values, widths), along_axis, kernel)


def filter_local(values, kernel):
    return tap_padded(tap_valid(tap_valid(values, 0, kernel), 1, kernel), 2, kernel)


def corner_weights(position, fraction, extent):
    places = jnp.arange(extent, dtype=jnp.float32)
    lower = (position[:, None] == places[None, :]).astype(jnp.float32)
    upper = (position[:, None] + 1.0 == places[None, :]).astype(jnp.float32)
    return (lower * (1.0 - fraction[:, None]) + upper * fraction[:, None], upper - lower)


def spread_brick(anchors, fractions, amounts, extent_x, extent_y, extent_z):
    atom_count = anchors.shape[1]
    weight_x = corner_weights(anchors[0], fractions[0], extent_x)[0]
    weight_y = corner_weights(anchors[1], fractions[1], extent_y)[0]
    weight_z = corner_weights(anchors[2], fractions[2], extent_z)[0]
    plane = (weight_x[:, :, None] * weight_y[:, None, :]).reshape(atom_count, extent_x * extent_y)
    depth = weight_z * amounts[:, None]
    summed = lax.dot_general(
        plane,
        depth,
        (((0,), (0,)), ((), ())),
        precision=lax.Precision.HIGHEST,
        preferred_element_type=jnp.float32,
    )
    return summed.reshape(extent_x, extent_y, extent_z)


def sample_gradient(anchors, fractions, field):
    extent_x, extent_y, extent_z = field.shape
    atom_count = anchors.shape[1]
    weight_x, slope_x = corner_weights(anchors[0], fractions[0], extent_x)
    weight_y, slope_y = corner_weights(anchors[1], fractions[1], extent_y)
    weight_z, slope_z = corner_weights(anchors[2], fractions[2], extent_z)
    matrix = field.reshape(extent_x * extent_y, extent_z)
    stacked = jnp.concatenate([weight_z, slope_z], 0)
    product = lax.dot_general(
        stacked,
        matrix,
        (((1,), (1,)), ((), ())),
        precision=lax.Precision.HIGHEST,
        preferred_element_type=jnp.float32,
    )
    product = product.reshape(2, atom_count, extent_x, extent_y)
    grad_x = jnp.einsum(
        "ax,ay,axy->a", slope_x, weight_y, product[0], precision=lax.Precision.HIGHEST
    )
    grad_y = jnp.einsum(
        "ax,ay,axy->a", weight_x, slope_y, product[0], precision=lax.Precision.HIGHEST
    )
    grad_z = jnp.einsum(
        "ax,ay,axy->a", weight_x, weight_y, product[1], precision=lax.Precision.HIGHEST
    )
    return jnp.stack([grad_x, grad_y, grad_z])


def pair_block(own, others):
    offsets = own[0:3, :, None] - others[0:3, None, :] + (own[3:6, :, None] - others[3:6, None, :])
    distance = jnp.sum(offsets * offsets, 0)
    spread = own[7][:, None] + others[7][None, :]
    coupling = others[6][None, :] * jnp.exp(-0.5 * distance / spread) / spread
    return own[6][None, :] * jnp.sum(coupling[None] * offsets, 2)


def type_values(kinds, table):
    matches = (kinds[..., None] == jnp.arange(table.shape[1], dtype=jnp.int32)).astype(jnp.float32)
    shaped = table.reshape((3,) + (1,) * kinds.ndim + (table.shape[1],))
    return jnp.sum(matches[None] * shaped, -1)


def local_pairs(packet, nearby, live_count):
    atom_count = packet.shape[1]
    block_size = min(128, atom_count)
    blocks_live = (live_count + block_size - 1) // block_size

    def add_block(block_index, forces):
        start = block_index * block_size
        own = lax.dynamic_slice_in_dim(packet, start, block_size, 1)
        return lax.dynamic_update_slice_in_dim(forces, pair_block(own, nearby), start, 1)

    return lax.fori_loop(0, blocks_live, add_block, jnp.zeros((3, atom_count), jnp.float32))


def per_device(fraction, velocity, anchor, atom_types, counts, type_table, target):
    atom_count = fraction.shape[3]
    extent_x, extent_y, extent_z = target.shape
    fraction = fraction.reshape(3, atom_count)
    velocity = velocity.reshape(3, atom_count)
    anchor_local = anchor.reshape(3, atom_count).astype(jnp.float32)
    live_count = counts[0, 0]
    live = (jnp.arange(atom_count, dtype=jnp.int32) < live_count).astype(jnp.float32)
    properties = type_values(atom_types.reshape(atom_count), type_table)
    charge = properties[0] * live
    square_width = properties[1] * properties[1]
    masses = properties[2]
    root = jnp.stack(
        [lax.axis_index("cells") * extent_x, lax.axis_index("grp") * extent_y, jnp.int32(0)]
    ).astype(jnp.float32)
    anchor_global = anchor_local + root[:, None]
    widened = extended_2(target, (("cells", 0), ("grp", 1)), 4)
    mean_one = filter_local(widened, BOX_KERNEL)
    mean_two = filter_local(widened * widened, BOX_KERNEL)
    inverse_scale = lax.rsqrt(mean_two - mean_one * mean_one + EPSILON)
    margin = extended_2(jnp.stack([target, inverse_scale]), (("cells", 1), ("grp", 2)), 2)
    moved = jnp.zeros_like(velocity)
    potential = jnp.zeros_like(target)
    for turn_index in range(STEPS):
        packet = jnp.concatenate([anchor_global, fraction, charge[None], square_width[None]], 0)
        nearby = extended_2(packet.reshape(8, 1, 1, atom_count), (("cells", 1), ("grp", 2)), 1)
        nearby = nearby.reshape(8, 9 * atom_count)
        forces = local_pairs(packet, nearby, live_count)
        spread = spread_brick(anchor_local, fraction, charge, extent_x + 1, extent_y + 1, extent_z)
        arrived = passed_along(spread[extent_x:], "cells", 1)
        upper = spread[:extent_x].at[0:1].add(arrived)
        arrived_side = passed_along(upper[:, extent_y:], "grp", 1)
        density = upper[:, :extent_y].at[:, 0:1].add(arrived_side)
        deeper = extended_2(density, (("cells", 0), ("grp", 1)), 4)
        residual = (filter_local(deeper, BLUR_KERNEL) - margin[0]) * margin[1]
        potential = filter_local(residual, BLUR_KERNEL)
        next_plane = passed_along(potential[0:1], "cells", -1)
        extended = jnp.concatenate([potential, next_plane], 0)
        next_column = passed_along(extended[:, 0:1], "grp", -1)
        beyond = jnp.concatenate([extended, next_column], 1)
        gradient = sample_gradient(anchor_local, fraction, beyond)
        forces = forces - charge[None] * gradient
        velocity = velocity + TIME_STEP * forces / masses[None]
        moved = moved + TIME_STEP * velocity
        fraction = fraction + TIME_STEP * velocity
    final_velocity = (velocity * live[None]).reshape(3, 1, 1, atom_count)
    displacement = (moved * live[None]).reshape(3, 1, 1, atom_count)
    return (final_velocity, displacement, potential)


def solution(mesh):
    placed = (
        P(None, "cells", "grp", None),
        P(None, "cells", "grp", None),
        P(None, "cells", "grp", None),
        P("cells", "grp", None),
        P("cells", "grp"),
        P(),
        P("cells", "grp", None),
    )
    return jax.shard_map(
        per_device,
        mesh=mesh,
        in_specs=placed,
        out_specs=(
            P(None, "cells", "grp", None),
            P(None, "cells", "grp", None),
            P("cells", "grp", None),
        ),
        check_vma=False,
    )
```

profile of v0, /device:TPU:351, one launch (start us, length us, event | category | flops | bytes accessed | tf_op | source)
XLA Modules:
  0.0 232.9 jit_solution(13274907495032776413)
XLA Ops:
  0.6 2.2 collective-permute-start.10
  2.8 2.4 %collective-permute-start.11 = (f32[4,16,256]{2,1,0:T(8,128)}, f32[4,16,256]{2,1,0:T(8,128)S(1)}, u32[]{:S(2)}, u32[]{:S(2)}) collective-permute-start(f32[4,16,256]{2,1,0:T(8,128)} %param.25), channel_id=1, source_target_pairs={{4,0},{8,4},{12,8},{16,12},{20,16},{24,20},{28,24},{32,28},{36,32}... | collective-permute-start | bytes 196616 | tf_op jit(solution)/shard_map/ppermute | solution.py:25
  7.2 0.8 multiply_reduce_fusion.16
  8.9 11.3 %collective-permute-start = (f32[8,1,1,512]{3,0,2,1:T(8,128)S(1)}, f32[8,1,1,512]{3,0,2,1:T(8,128)S(1)}, u32[]{:S(2)}, u32[]{:S(2)}) collective-permute-start(f32[8,1,1,512]{3,0,2,1:T(8,128)S(1)} %bitcast.116), channel_id=1, source_target_pairs={{0,4},{4,8},{8,12},{12,16},{16,20},{20,24},{24,28},{28,32},{32,36}... | collective-permute-start | bytes 49160 | tf_op jit(solution)/shard_map/ppermute | solution.py:23
  20.2 1.9 collective-permute-start.1
  24.5 11.8 %collective-permute-start.4 = (f32[1,17,256]{2,1,0:T(8,128)S(1)}, f32[1,17,256]{2,1,0:T(8,128)S(1)}, u32[]{:S(2)}, u32[]{:S(2)}) collective-permute-start(f32[1,17,256]{2,1,0:T(8,128)S(1)} %slice_bitcast_fusion.8), channel_id=1, source_target_pairs={{0,4},{4,8},{8,12},{12,16},{16,20},{20,24},{24,28},{28,32},{32,36}... | collective-permute-start | bytes 52232 | tf_op jit(solution)/shard_map/ppermute | solution.py:35
  37.2 4.0 %collective-permute-start.5 = (f32[4,1,256]{2,1,0:T(1,128)S(1)}, f32[4,1,256]{2,1,0:T(1,128)S(1)}, u32[]{:S(2)}, u32[]{:S(2)}) collective-permute-start(f32[4,1,256]{2,1,0:T(1,128)S(1)} %slice.816), channel_id=1, source_target_pairs={{0,1},{1,2},{2,3},{4,5},{5,6},{6,7},{8,9},{9,10},{10,11},{12,13},{... | collective-permute-start | bytes 12296 | tf_op jit(solution)/shard_map/ppermute | solution.py:35
  41.2 4.0 %collective-permute-start.2 = (f32[8,3,1,512]{3,0,2,1:T(8,128)S(1)}, f32[8,3,1,512]{3,0,2,1:T(8,128)S(1)}, u32[]{:S(2)}, u32[]{:S(2)}) collective-permute-start(f32[8,3,1,512]{3,0,2,1:T(8,128)S(1)} %pad_maximum_fusion.19), channel_id=1, source_target_pairs={{0,1},{1,2},{2,3},{4,5},{5,6},{6,7},{8,9},{9,10},{10,11},{12,13},{... | collective-permute-start | bytes 147464 | tf_op jit(solution)/shard_map/ppermute | solution.py:23
  45.2 1.9 collective-permute-start.3
  47.3 12.9 %collective-permute-start.6 = (f32[4,16,256]{2,1,0:T(8,128)S(1)}, f32[4,16,256]{2,1,0:T(8,128)S(1)}, u32[]{:S(2)}, u32[]{:S(2)}) collective-permute-start(f32[4,16,256]{2,1,0:T(8,128)S(1)} %scatter-add.15), channel_id=1, source_target_pairs={{0,4},{4,8},{8,12},{12,16},{16,20},{20,24},{24,28},{28,32},{32,36}... | collective-permute-start | bytes 196616 | tf_op jit(solution)/shard_map/ppermute | solution.py:23
  60.2 1.9 collective-permute-start.7
  62.2 3.6 %collective-permute-start.12 = (f32[12,4,256]{2,1,0:T(4,128)S(1)}, f32[12,4,256]{2,1,0:T(4,128)S(1)}, u32[]{:S(2)}, u32[]{:S(2)}) collective-permute-start(f32[12,4,256]{2,1,0:T(4,128)S(1)} %get-tuple-element.173), channel_id=1, source_target_pairs={{0,1},{1,2},{2,3},{4,5},{5,6},{6,7},{8,9},{9,10},{10,11},{12,13},{... | collective-permute-start | bytes 147464 | tf_op jit(solution)/shard_map/ppermute | solution.py:23
  65.9 1.9 collective-permute-start.13
  67.8 6.1 %collective-permute-done.7 = f32[4,16,256]{2,1,0:T(8,128)S(1)} collective-permute-done((f32[4,16,256]{2,1,0:T(8,128)S(1)}, f32[4,16,256]{2,1,0:T(8,128)S(1)}, u32[]{:S(2)}, u32[]{:S(2)}) %collective-permute-start.7) | collective-permute-done | bytes 65568 | tf_op jit(solution)/shard_map/ppermute | solution.py:25
  73.9 3.7 %collective-permute-start.8 = (f32[12,4,256]{2,1,0:T(4,128)S(1)}, f32[12,4,256]{2,1,0:T(4,128)S(1)}, u32[]{:S(2)}, u32[]{:S(2)}) collective-permute-start(f32[12,4,256]{2,1,0:T(4,128)S(1)} %get-tuple-element.175), channel_id=1, source_target_pairs={{0,1},{1,2},{2,3},{4,5},{5,6},{6,7},{8,9},{9,10},{10,11},{12,13},{... | collective-permute-start | bytes 147464 | tf_op jit(solution)/shard_map/ppermute | solution.py:23
  77.7 1.9 collective-permute-start.9
  80.3 6.1 %collective-permute-start.14 = (f32[2,2,16,256]{3,2,1,0:T(8,128)S(1)}, f32[2,2,16,256]{3,2,1,0:T(8,128)S(1)}, u32[]{:S(2)}, u32[]{:S(2)}) collective-permute-start(f32[2,2,16,256]{3,2,1,0:T(8,128)S(1)} %get-tuple-element.177), channel_id=1, source_target_pairs={{0,4},{4,8},{8,12},{12,16},{16,20},{20,24},{24,28},{28,32},{32,36}... | collective-permute-start | bytes 196616 | tf_op jit(solution)/shard_map/ppermute | solution.py:23
  86.4 1.9 collective-permute-start.15
  88.5 11.6 %collective-permute-done.15 = f32[2,2,16,256]{3,2,1,0:T(8,128)S(1)} collective-permute-done((f32[2,2,16,256]{3,2,1,0:T(8,128)S(1)}, f32[2,2,16,256]{3,2,1,0:T(8,128)S(1)}, u32[]{:S(2)}, u32[]{:S(2)}) %collective-permute-start.15) | collective-permute-done | bytes 65568 | tf_op jit(solution)/shard_map/ppermute | solution.py:25
  100.2 3.6 %collective-permute-start.16 = (f32[2,8,2,256]{3,2,1,0:T(2,128)S(1)}, f32[2,8,2,256]{3,2,1,0:T(2,128)S(1)}, u32[]{:S(2)}, u32[]{:S(2)}) collective-permute-start(f32[2,8,2,256]{3,2,1,0:T(2,128)S(1)} %get-tuple-element.169), channel_id=1, source_target_pairs={{0,1},{1,2},{2,3},{4,5},{5,6},{6,7},{8,9},{9,10},{10,11},{12,13},{... | collective-permute-start | bytes 98312 | tf_op jit(solution)/shard_map/ppermute | solution.py:23
  103.8 1.9 collective-permute-start.17
  105.9 2.6 %collective-permute-done.17 = f32[2,8,2,256]{3,2,1,0:T(2,128)S(1)} collective-permute-done((f32[2,8,2,256]{3,2,1,0:T(2,128)S(1)}, f32[2,8,2,256]{3,2,1,0:T(2,128)S(1)}, u32[]{:S(2)}, u32[]{:S(2)}) %collective-permute-start.17) | collective-permute-done | bytes 32800 | tf_op jit(solution)/shard_map/ppermute | solution.py:25
  109.0 1.9 collective-permute-start.18
  111.0 11.2 %collective-permute-done.18 = f32[1,16,256]{2,1,0:T(8,128)S(1)} collective-permute-done((f32[1,16,256]{2,1,0:T(8,128)S(1)}, f32[1,16,256]{2,1,0:T(8,128)S(1)}, u32[]{:S(2)}, u32[]{:S(2)}) %collective-permute-start.18) | collective-permute-done | bytes 16416 | tf_op jit(solution)/shard_map/ppermute | solution.py:35
  122.2 1.9 collective-permute-start.19
  124.2 16.3 %while.24 = (s32[]{:T(128)}, f32[3,512]{1,0:T(4,128)S(1)}, s32[]{:T(128)}, f32[8,512]{1,0:T(8,128)S(1)}, f32[8,4608]{1,0:T(8,128)S(1)}, /*index=5*/s32[]{:T(128)}, s32[]{:T(128)}, s32[]{:T(128)}, s32[]{:T(128)}) while((s32[]{:T(128)}, f32[3,512]{1,0:T(4,128)S(1)}, s32[]{:T(128)}, f32[8,512]{1,0:T(8,128)S(1)}, f32[8,4608]{1,0:T(8,128)S(1)}, ...), condition=%wide.region_4.5_spmd, body=%wide.region_1.4_spmd.sunk | while | flops 20054020 | bytes 10019475 | solution.py:136
  124.2 1.5 multiply_reduce_fusion.21
  125.9 0.8 add_divide_fusion.6
  126.7 1.5 multiply_reduce_fusion.22
  128.3 1.5 multiply_reduce_fusion.21
  130.0 0.8 add_divide_fusion.6
  130.8 1.5 multiply_reduce_fusion.22
  132.4 1.5 multiply_reduce_fusion.21
  134.1 0.8 add_divide_fusion.6
  134.8 1.5 multiply_reduce_fusion.22
  136.4 1.5 multiply_reduce_fusion.21
  138.1 0.8 add_divide_fusion.6
  138.9 1.5 multiply_reduce_fusion.22
  140.5 1.1 fusion.4
  143.7 1.9 collective-permute-start.24
  145.7 1.1 collective-permute-done.24
  146.8 3.4 %collective-permute-start.25 = (f32[4,1,256]{2,1,0:T(1,128)S(1)}, f32[4,1,256]{2,1,0:T(1,128)S(1)}, u32[]{:S(2)}, u32[]{:S(2)}) collective-permute-start(f32[4,1,256]{2,1,0:T(1,128)S(1)} %slice.891), channel_id=1, source_target_pairs={{0,1},{1,2},{2,3},{4,5},{5,6},{6,7},{8,9},{9,10},{10,11},{12,13},{... | collective-permute-start | bytes 12296 | tf_op jit(solution)/shard_map/ppermute | solution.py:35
  151.2 13.3 %collective-permute-start.26 = (f32[4,16,256]{2,1,0:T(8,128)S(1)}, f32[4,16,256]{2,1,0:T(8,128)S(1)}, u32[]{:S(2)}, u32[]{:S(2)}) collective-permute-start(f32[4,16,256]{2,1,0:T(8,128)S(1)} %scatter-add.19), channel_id=1, source_target_pairs={{0,4},{4,8},{8,12},{12,16},{16,20},{20,24},{24,28},{28,32},{32,36}... | collective-permute-start | bytes 196616 | tf_op jit(solution)/shard_map/ppermute | solution.py:23
  164.5 1.9 collective-permute-start.27
  166.4 11.8 %collective-permute-start.20 = (f32[8,1,1,512]{3,0,2,1:T(8,128)S(1)}, f32[8,1,1,512]{3,0,2,1:T(8,128)S(1)}, u32[]{:S(2)}, u32[]{:S(2)}) collective-permute-start(f32[8,1,1,512]{3,0,2,1:T(8,128)S(1)} %bitcast.120), channel_id=1, source_target_pairs={{0,4},{4,8},{8,12},{12,16},{16,20},{20,24},{24,28},{28,32},{32,36}... | collective-permute-start | bytes 49160 | tf_op jit(solution)/shard_map/ppermute | solution.py:23
  178.2 1.9 collective-permute-start.21
  180.2 3.7 %collective-permute-start.28 = (f32[12,4,256]{2,1,0:T(4,128)S(1)}, f32[12,4,256]{2,1,0:T(4,128)S(1)}, u32[]{:S(2)}, u32[]{:S(2)}) collective-permute-start(f32[12,4,256]{2,1,0:T(4,128)S(1)} %get-tuple-element.171), channel_id=1, source_target_pairs={{0,1},{1,2},{2,3},{4,5},{5,6},{6,7},{8,9},{9,10},{10,11},{12,13},{... | collective-permute-start | bytes 147464 | tf_op jit(solution)/shard_map/ppermute | solution.py:23
  183.8 1.9 collective-permute-start.29
  185.8 5.6 %collective-permute-done.21 = f32[8,1,1,512]{3,0,2,1:T(8,128)S(1)} collective-permute-done((f32[8,1,1,512]{3,0,2,1:T(8,128)S(1)}, f32[8,1,1,512]{3,0,2,1:T(8,128)S(1)}, u32[]{:S(2)}, u32[]{:S(2)}) %collective-permute-start.21) | collective-permute-done | bytes 16416 | tf_op jit(solution)/shard_map/ppermute | solution.py:25
  191.4 3.6 %collective-permute-start.22 = (f32[8,3,1,512]{3,0,2,1:T(8,128)S(1)}, f32[8,3,1,512]{3,0,2,1:T(8,128)S(1)}, u32[]{:S(2)}, u32[]{:S(2)}) collective-permute-start(f32[8,3,1,512]{3,0,2,1:T(8,128)S(1)} %pad_maximum_fusion.20), channel_id=1, source_target_pairs={{0,1},{1,2},{2,3},{4,5},{5,6},{6,7},{8,9},{9,10},{10,11},{12,13},{... | collective-permute-start | bytes 147464 | tf_op jit(solution)/shard_map/ppermute | solution.py:23
  195.0 2.1 collective-permute-start.23
  197.9 1.9 collective-permute-start.30
  199.9 11.2 %collective-permute-done.30 = f32[1,16,256]{2,1,0:T(8,128)S(1)} collective-permute-done((f32[1,16,256]{2,1,0:T(8,128)S(1)}, f32[1,16,256]{2,1,0:T(8,128)S(1)}, u32[]{:S(2)}, u32[]{:S(2)}) %collective-permute-start.30) | collective-permute-done | bytes 16416 | tf_op jit(solution)/shard_map/ppermute | solution.py:35
  211.1 1.9 collective-permute-start.31
  213.0 16.3 %while.25 = (s32[]{:T(128)}, f32[3,512]{1,0:T(4,128)S(1)}, s32[]{:T(128)}, f32[8,512]{1,0:T(8,128)S(1)}, f32[8,4608]{1,0:T(8,128)S(1)}, /*index=5*/s32[]{:T(128)}, s32[]{:T(128)}, s32[]{:T(128)}, s32[]{:T(128)}) while((s32[]{:T(128)}, f32[3,512]{1,0:T(4,128)S(1)}, s32[]{:T(128)}, f32[8,512]{1,0:T(8,128)S(1)}, f32[8,4608]{1,0:T(8,128)S(1)}, ...), condition=%wide.region_8.9_spmd, body=%wide.region_5.8_spmd.sunk | while | flops 20054020 | bytes 10019475 | solution.py:136
  213.1 1.5 multiply_reduce_fusion.23
  215.6 1.5 multiply_reduce_fusion.24
  217.2 1.5 multiply_reduce_fusion.23
  219.7 1.5 multiply_reduce_fusion.24
  221.3 1.5 multiply_reduce_fusion.23
  223.7 1.5 multiply_reduce_fusion.24
  225.3 1.5 multiply_reduce_fusion.23
  227.8 1.5 multiply_reduce_fusion.24
  229.4 1.1 fusion.5
  (200 shorter events, 17.2 us)
Async XLA Ops:
  0.6 59.5 %collective-permute-start.10 = (f32[4,16,256]{2,1,0:T(8,128)}, f32[4,16,256]{2,1,0:T(8,128)S(1)}, u32[]{:S(2)}, u32[]{:S(2)}) collective-permute-start(f32[4,16,256]{2,1,0:T(8,128)} %param.25), channel_id=1, source_target_pairs={{0,4},{4,8},{8,12},{12,16},{16,20},{20,24},{24,28},{28,32},{32,36}... | collective-permute-start | bytes 196616 | tf_op jit(solution)/shard_map/ppermute | solution.py:23
  2.8 59.4 %collective-permute-start.11 = (f32[4,16,256]{2,1,0:T(8,128)}, f32[4,16,256]{2,1,0:T(8,128)S(1)}, u32[]{:S(2)}, u32[]{:S(2)}) collective-permute-start(f32[4,16,256]{2,1,0:T(8,128)} %param.25), channel_id=1, source_target_pairs={{4,0},{8,4},{12,8},{16,12},{20,16},{24,20},{28,24},{32,28},{36,32}... | collective-permute-start | bytes 196616 | tf_op jit(solution)/shard_map/ppermute | solution.py:25
  7.2 54.9 %copy-start = (f32[4,16,256]{2,1,0:T(8,128)S(1)}, f32[4,16,256]{2,1,0:T(8,128)}, u32[]{:S(2)}) copy-start(f32[4,16,256]{2,1,0:T(8,128)} %param.25) | copy-start | bytes 196612
  8.9 32.3 %collective-permute-start = (f32[8,1,1,512]{3,0,2,1:T(8,128)S(1)}, f32[8,1,1,512]{3,0,2,1:T(8,128)S(1)}, u32[]{:S(2)}, u32[]{:S(2)}) collective-permute-start(f32[8,1,1,512]{3,0,2,1:T(8,128)S(1)} %bitcast.116), channel_id=1, source_target_pairs={{0,4},{4,8},{8,12},{12,16},{16,20},{20,24},{24,28},{28,32},{32,36}... | collective-permute-start | bytes 49160 | tf_op jit(solution)/shard_map/ppermute | solution.py:23
  20.2 21.0 %collective-permute-start.1 = (f32[8,1,1,512]{3,0,2,1:T(8,128)S(1)}, f32[8,1,1,512]{3,0,2,1:T(8,128)S(1)}, u32[]{:S(2)}, u32[]{:S(2)}) collective-permute-start(f32[8,1,1,512]{3,0,2,1:T(8,128)S(1)} %bitcast.117), channel_id=1, source_target_pairs={{4,0},{8,4},{12,8},{16,12},{20,16},{24,20},{28,24},{32,28},{36,32}... | collective-permute-start | bytes 49160 | tf_op jit(solution)/shard_map/ppermute | solution.py:25
  24.5 12.7 %collective-permute-start.4 = (f32[1,17,256]{2,1,0:T(8,128)S(1)}, f32[1,17,256]{2,1,0:T(8,128)S(1)}, u32[]{:S(2)}, u32[]{:S(2)}) collective-permute-start(f32[1,17,256]{2,1,0:T(8,128)S(1)} %slice_bitcast_fusion.8), channel_id=1, source_target_pairs={{0,4},{4,8},{8,12},{12,16},{16,20},{20,24},{24,28},{28,32},{32,36}... | collective-permute-start | bytes 52232 | tf_op jit(solution)/shard_map/ppermute | solution.py:35
  37.2 10.0 %collective-permute-start.5 = (f32[4,1,256]{2,1,0:T(1,128)S(1)}, f32[4,1,256]{2,1,0:T(1,128)S(1)}, u32[]{:S(2)}, u32[]{:S(2)}) collective-permute-start(f32[4,1,256]{2,1,0:T(1,128)S(1)} %slice.816), channel_id=1, source_target_pairs={{0,1},{1,2},{2,3},{4,5},{5,6},{6,7},{8,9},{9,10},{10,11},{12,13},{... | collective-permute-start | bytes 12296 | tf_op jit(solution)/shard_map/ppermute | solution.py:35
  41.2 69.7 %collective-permute-start.2 = (f32[8,3,1,512]{3,0,2,1:T(8,128)S(1)}, f32[8,3,1,512]{3,0,2,1:T(8,128)S(1)}, u32[]{:S(2)}, u32[]{:S(2)}) collective-permute-start(f32[8,3,1,512]{3,0,2,1:T(8,128)S(1)} %pad_maximum_fusion.19), channel_id=1, source_target_pairs={{0,1},{1,2},{2,3},{4,5},{5,6},{6,7},{8,9},{9,10},{10,11},{12,13},{... | collective-permute-start | bytes 147464 | tf_op jit(solution)/shard_map/ppermute | solution.py:23
  45.2 65.7 %collective-permute-start.3 = (f32[8,3,1,512]{3,0,2,1:T(8,128)S(1)}, f32[8,3,1,512]{3,0,2,1:T(8,128)S(1)}, u32[]{:S(2)}, u32[]{:S(2)}) collective-permute-start(f32[8,3,1,512]{3,0,2,1:T(8,128)S(1)} %pad_maximum_fusion.19), channel_id=1, source_target_pairs={{1,0},{2,1},{3,2},{5,4},{6,5},{7,6},{9,8},{10,9},{11,10},{13,12},{... | collective-permute-start | bytes 147464 | tf_op jit(solution)/shard_map/ppermute | solution.py:25
  47.3 18.6 %collective-permute-start.6 = (f32[4,16,256]{2,1,0:T(8,128)S(1)}, f32[4,16,256]{2,1,0:T(8,128)S(1)}, u32[]{:S(2)}, u32[]{:S(2)}) collective-permute-start(f32[4,16,256]{2,1,0:T(8,128)S(1)} %scatter-add.15), channel_id=1, source_target_pairs={{0,4},{4,8},{8,12},{12,16},{16,20},{20,24},{24,28},{28,32},{32,36}... | collective-permute-start | bytes 196616 | tf_op jit(solution)/shard_map/ppermute | solution.py:23
  60.2 13.7 %collective-permute-start.7 = (f32[4,16,256]{2,1,0:T(8,128)S(1)}, f32[4,16,256]{2,1,0:T(8,128)S(1)}, u32[]{:S(2)}, u32[]{:S(2)}) collective-permute-start(f32[4,16,256]{2,1,0:T(8,128)S(1)} %scatter-add.15), channel_id=1, source_target_pairs={{4,0},{8,4},{12,8},{16,12},{20,16},{24,20},{28,24},{32,28},{36,32}... | collective-permute-start | bytes 196616 | tf_op jit(solution)/shard_map/ppermute | solution.py:25
  62.2 15.5 %collective-permute-start.12 = (f32[12,4,256]{2,1,0:T(4,128)S(1)}, f32[12,4,256]{2,1,0:T(4,128)S(1)}, u32[]{:S(2)}, u32[]{:S(2)}) collective-permute-start(f32[12,4,256]{2,1,0:T(4,128)S(1)} %get-tuple-element.173), channel_id=1, source_target_pairs={{0,1},{1,2},{2,3},{4,5},{5,6},{6,7},{8,9},{9,10},{10,11},{12,13},{... | collective-permute-start | bytes 147464 | tf_op jit(solution)/shard_map/ppermute | solution.py:23
  65.9 13.7 %collective-permute-start.13 = (f32[12,4,256]{2,1,0:T(4,128)S(1)}, f32[12,4,256]{2,1,0:T(4,128)S(1)}, u32[]{:S(2)}, u32[]{:S(2)}) collective-permute-start(f32[12,4,256]{2,1,0:T(4,128)S(1)} %get-tuple-element.174), channel_id=1, source_target_pairs={{1,0},{2,1},{3,2},{5,4},{6,5},{7,6},{9,8},{10,9},{11,10},{13,12},{... | collective-permute-start | bytes 147464 | tf_op jit(solution)/shard_map/ppermute | solution.py:25
  73.9 12.5 %collective-permute-start.8 = (f32[12,4,256]{2,1,0:T(4,128)S(1)}, f32[12,4,256]{2,1,0:T(4,128)S(1)}, u32[]{:S(2)}, u32[]{:S(2)}) collective-permute-start(f32[12,4,256]{2,1,0:T(4,128)S(1)} %get-tuple-element.175), channel_id=1, source_target_pairs={{0,1},{1,2},{2,3},{4,5},{5,6},{6,7},{8,9},{9,10},{10,11},{12,13},{... | collective-permute-start | bytes 147464 | tf_op jit(solution)/shard_map/ppermute | solution.py:23
  77.7 10.7 %collective-permute-start.9 = (f32[12,4,256]{2,1,0:T(4,128)S(1)}, f32[12,4,256]{2,1,0:T(4,128)S(1)}, u32[]{:S(2)}, u32[]{:S(2)}) collective-permute-start(f32[12,4,256]{2,1,0:T(4,128)S(1)} %get-tuple-element.176), channel_id=1, source_target_pairs={{1,0},{2,1},{3,2},{5,4},{6,5},{7,6},{9,8},{10,9},{11,10},{13,12},{... | collective-permute-start | bytes 147464 | tf_op jit(solution)/shard_map/ppermute | solution.py:25
  80.3 8.2 %collective-permute-start.14 = (f32[2,2,16,256]{3,2,1,0:T(8,128)S(1)}, f32[2,2,16,256]{3,2,1,0:T(8,128)S(1)}, u32[]{:S(2)}, u32[]{:S(2)}) collective-permute-start(f32[2,2,16,256]{3,2,1,0:T(8,128)S(1)} %get-tuple-element.177), channel_id=1, source_target_pairs={{0,4},{4,8},{8,12},{12,16},{16,20},{20,24},{24,28},{28,32},{32,36}... | collective-permute-start | bytes 196616 | tf_op jit(solution)/shard_map/ppermute | solution.py:23
  86.4 13.7 %collective-permute-start.15 = (f32[2,2,16,256]{3,2,1,0:T(8,128)S(1)}, f32[2,2,16,256]{3,2,1,0:T(8,128)S(1)}, u32[]{:S(2)}, u32[]{:S(2)}) collective-permute-start(f32[2,2,16,256]{3,2,1,0:T(8,128)S(1)} %get-tuple-element.178), channel_id=1, source_target_pairs={{4,0},{8,4},{12,8},{16,12},{20,16},{24,20},{28,24},{32,28},{36,32}... | collective-permute-start | bytes 196616 | tf_op jit(solution)/shard_map/ppermute | solution.py:25
  100.2 5.7 %collective-permute-start.16 = (f32[2,8,2,256]{3,2,1,0:T(2,128)S(1)}, f32[2,8,2,256]{3,2,1,0:T(2,128)S(1)}, u32[]{:S(2)}, u32[]{:S(2)}) collective-permute-start(f32[2,8,2,256]{3,2,1,0:T(2,128)S(1)} %get-tuple-element.169), channel_id=1, source_target_pairs={{0,1},{1,2},{2,3},{4,5},{5,6},{6,7},{8,9},{9,10},{10,11},{12,13},{... | collective-permute-start | bytes 98312 | tf_op jit(solution)/shard_map/ppermute | solution.py:23
  103.8 4.7 %collective-permute-start.17 = (f32[2,8,2,256]{3,2,1,0:T(2,128)S(1)}, f32[2,8,2,256]{3,2,1,0:T(2,128)S(1)}, u32[]{:S(2)}, u32[]{:S(2)}) collective-permute-start(f32[2,8,2,256]{3,2,1,0:T(2,128)S(1)} %get-tuple-element.170), channel_id=1, source_target_pairs={{1,0},{2,1},{3,2},{5,4},{6,5},{7,6},{9,8},{10,9},{11,10},{13,12},{... | collective-permute-start | bytes 98312 | tf_op jit(solution)/shard_map/ppermute | solution.py:25
  109.0 13.2 %collective-permute-start.18 = (f32[1,16,256]{2,1,0:T(8,128)S(1)}, f32[1,16,256]{2,1,0:T(8,128)S(1)}, u32[]{:S(2)}, u32[]{:S(2)}) collective-permute-start(f32[1,16,256]{2,1,0:T(8,128)S(1)} %slice.879), channel_id=1, source_target_pairs={{4,0},{8,4},{12,8},{16,12},{20,16},{24,20},{28,24},{32,28},{36,32}... | collective-permute-start | bytes 49160 | tf_op jit(solution)/shard_map/ppermute | solution.py:35
  122.2 18.2 %collective-permute-start.19 = (f32[5,1,256]{2,1,0:T(1,128)S(1)}, f32[5,1,256]{2,1,0:T(1,128)S(1)}, u32[]{:S(2)}, u32[]{:S(2)}) collective-permute-start(f32[5,1,256]{2,1,0:T(1,128)S(1)} %pad_maximum_fusion.32), channel_id=1, source_target_pairs={{1,0},{2,1},{3,2},{5,4},{6,5},{7,6},{9,8},{10,9},{11,10},{13,12},{... | collective-permute-start | bytes 15368 | tf_op jit(solution)/shard_map/ppermute | solution.py:35
  141.7 1.1 copy-start.2
  141.7 1.1 copy-start.3
  143.7 3.1 %collective-permute-start.24 = (f32[1,17,256]{2,1,0:T(8,128)S(1)}, f32[1,17,256]{2,1,0:T(8,128)S(1)}, u32[]{:S(2)}, u32[]{:S(2)}) collective-permute-start(f32[1,17,256]{2,1,0:T(8,128)S(1)} %slice_bitcast_fusion.6), channel_id=1, source_target_pairs={{0,4},{4,8},{8,12},{12,16},{16,20},{20,24},{24,28},{28,32},{32,36}... | collective-permute-start | bytes 52232 | tf_op jit(solution)/shard_map/ppermute | solution.py:35
  146.8 4.4 %collective-permute-start.25 = (f32[4,1,256]{2,1,0:T(1,128)S(1)}, f32[4,1,256]{2,1,0:T(1,128)S(1)}, u32[]{:S(2)}, u32[]{:S(2)}) collective-permute-start(f32[4,1,256]{2,1,0:T(1,128)S(1)} %slice.891), channel_id=1, source_target_pairs={{0,1},{1,2},{2,3},{4,5},{5,6},{6,7},{8,9},{9,10},{10,11},{12,13},{... | collective-permute-start | bytes 12296 | tf_op jit(solution)/shard_map/ppermute | solution.py:35
  151.2 28.9 %collective-permute-start.26 = (f32[4,16,256]{2,1,0:T(8,128)S(1)}, f32[4,16,256]{2,1,0:T(8,128)S(1)}, u32[]{:S(2)}, u32[]{:S(2)}) collective-permute-start(f32[4,16,256]{2,1,0:T(8,128)S(1)} %scatter-add.19), channel_id=1, source_target_pairs={{0,4},{4,8},{8,12},{12,16},{16,20},{20,24},{24,28},{28,32},{32,36}... | collective-permute-start | bytes 196616 | tf_op jit(solution)/shard_map/ppermute | solution.py:23
  164.5 15.7 %collective-permute-start.27 = (f32[4,16,256]{2,1,0:T(8,128)S(1)}, f32[4,16,256]{2,1,0:T(8,128)S(1)}, u32[]{:S(2)}, u32[]{:S(2)}) collective-permute-start(f32[4,16,256]{2,1,0:T(8,128)S(1)} %scatter-add.19), channel_id=1, source_target_pairs={{4,0},{8,4},{12,8},{16,12},{20,16},{24,20},{28,24},{32,28},{36,32}... | collective-permute-start | bytes 196616 | tf_op jit(solution)/shard_map/ppermute | solution.py:25
  166.4 19.3 %collective-permute-start.20 = (f32[8,1,1,512]{3,0,2,1:T(8,128)S(1)}, f32[8,1,1,512]{3,0,2,1:T(8,128)S(1)}, u32[]{:S(2)}, u32[]{:S(2)}) collective-permute-start(f32[8,1,1,512]{3,0,2,1:T(8,128)S(1)} %bitcast.120), channel_id=1, source_target_pairs={{0,4},{4,8},{8,12},{12,16},{16,20},{20,24},{24,28},{28,32},{32,36}... | collective-permute-start | bytes 49160 | tf_op jit(solution)/shard_map/ppermute | solution.py:23
  178.2 13.2 %collective-permute-start.21 = (f32[8,1,1,512]{3,0,2,1:T(8,128)S(1)}, f32[8,1,1,512]{3,0,2,1:T(8,128)S(1)}, u32[]{:S(2)}, u32[]{:S(2)}) collective-permute-start(f32[8,1,1,512]{3,0,2,1:T(8,128)S(1)} %bitcast.121), channel_id=1, source_target_pairs={{4,0},{8,4},{12,8},{16,12},{20,16},{24,20},{28,24},{32,28},{36,32}... | collective-permute-start | bytes 49160 | tf_op jit(solution)/shard_map/ppermute | solution.py:25
  180.2 17.0 %collective-permute-start.28 = (f32[12,4,256]{2,1,0:T(4,128)S(1)}, f32[12,4,256]{2,1,0:T(4,128)S(1)}, u32[]{:S(2)}, u32[]{:S(2)}) collective-permute-start(f32[12,4,256]{2,1,0:T(4,128)S(1)} %get-tuple-element.171), channel_id=1, source_target_pairs={{0,1},{1,2},{2,3},{4,5},{5,6},{6,7},{8,9},{9,10},{10,11},{12,13},{... | collective-permute-start | bytes 147464 | tf_op jit(solution)/shard_map/ppermute | solution.py:23
  183.8 13.3 %collective-permute-start.29 = (f32[12,4,256]{2,1,0:T(4,128)S(1)}, f32[12,4,256]{2,1,0:T(4,128)S(1)}, u32[]{:S(2)}, u32[]{:S(2)}) collective-permute-start(f32[12,4,256]{2,1,0:T(4,128)S(1)} %get-tuple-element.172), channel_id=1, source_target_pairs={{1,0},{2,1},{3,2},{5,4},{6,5},{7,6},{9,8},{10,9},{11,10},{13,12},{... | collective-permute-start | bytes 147464 | tf_op jit(solution)/shard_map/ppermute | solution.py:25
  191.4 8.5 %collective-permute-start.22 = (f32[8,3,1,512]{3,0,2,1:T(8,128)S(1)}, f32[8,3,1,512]{3,0,2,1:T(8,128)S(1)}, u32[]{:S(2)}, u32[]{:S(2)}) collective-permute-start(f32[8,3,1,512]{3,0,2,1:T(8,128)S(1)} %pad_maximum_fusion.20), channel_id=1, source_target_pairs={{0,1},{1,2},{2,3},{4,5},{5,6},{6,7},{8,9},{9,10},{10,11},{12,13},{... | collective-permute-start | bytes 147464 | tf_op jit(solution)/shard_map/ppermute | solution.py:23
  195.0 4.8 %collective-permute-start.23 = (f32[8,3,1,512]{3,0,2,1:T(8,128)S(1)}, f32[8,3,1,512]{3,0,2,1:T(8,128)S(1)}, u32[]{:S(2)}, u32[]{:S(2)}) collective-permute-start(f32[8,3,1,512]{3,0,2,1:T(8,128)S(1)} %pad_maximum_fusion.20), channel_id=1, source_target_pairs={{1,0},{2,1},{3,2},{5,4},{6,5},{7,6},{9,8},{10,9},{11,10},{13,12},{... | collective-permute-start | bytes 147464 | tf_op jit(solution)/shard_map/ppermute | solution.py:25
  197.9 31.4 %copy-start.1 = (f32[4,16,256]{2,1,0:T(8,128)}, f32[4,16,256]{2,1,0:T(8,128)S(1)}, u32[]{:S(2)}) copy-start(f32[4,16,256]{2,1,0:T(8,128)S(1)} %fusion.72) | copy-start | bytes 196612
  197.9 13.2 %collective-permute-start.30 = (f32[1,16,256]{2,1,0:T(8,128)S(1)}, f32[1,16,256]{2,1,0:T(8,128)S(1)}, u32[]{:S(2)}, u32[]{:S(2)}) collective-permute-start(f32[1,16,256]{2,1,0:T(8,128)S(1)} %slice.912), channel_id=1, source_target_pairs={{4,0},{8,4},{12,8},{16,12},{20,16},{24,20},{28,24},{32,28},{36,32}... | collective-permute-start | bytes 49160 | tf_op jit(solution)/shard_map/ppermute | solution.py:35
  211.1 18.2 %collective-permute-start.31 = (f32[5,1,256]{2,1,0:T(1,128)S(1)}, f32[5,1,256]{2,1,0:T(1,128)S(1)}, u32[]{:S(2)}, u32[]{:S(2)}) collective-permute-start(f32[5,1,256]{2,1,0:T(1,128)S(1)} %pad_maximum_fusion.31), channel_id=1, source_target_pairs={{1,0},{2,1},{3,2},{5,4},{6,5},{7,6},{9,8},{10,9},{11,10},{13,12},{... | collective-permute-start | bytes 15368 | tf_op jit(solution)/shard_map/ppermute | solution.py:35
where the time goes:
time: 234 us; the launch traced here: 233 us
  starting transfers between devices  132 us (56%)
  waiting for transfers between devices  50.2 us (21%)
  other arithmetic  37.9 us (16%)
  local copies, waits for them, and re-layouts  5.57 us (2%)
  matrix products  3.75 us (2%)
  between operations  2.52 us (1%)
    ppermute x12, starting transfers between devices, extended_2(): lax.ppermute(tail, axis, [(i, (i + 1) % count) for i in range(ends)])  79.9 us
    ppermute x8, starting transfers between devices, passed_along(): return lax.ppermute(block, axis, route)  28.8 us
    ppermute x12, waiting for transfers between devices, extended_2(): lax.ppermute(head, axis, [((i + 1) % count, i) for i in range(ends)])  26 us
    ppermute x8, waiting for transfers between devices, passed_along(): return lax.ppermute(block, axis, route)  24.2 us
    ppermute x12, starting transfers between devices, extended_2(): lax.ppermute(head, axis, [((i + 1) % count, i) for i in range(ends)])  23.7 us
    reduce_sum x8, other arithmetic, pair_block(): distance = jnp.sum(offsets * offsets, 0)  12.4 us
    reduce_sum x8, other arithmetic, pair_block(): return own[6][None, :] * jnp.sum(coupling[None] * offsets, 2)  12.1 us
    div x8, other arithmetic, pair_block(): coupling = others[6][None, :] * jnp.exp(-0.5 * distance / spread) / spread  6.14 us
  transfers between devices with their start and end apart: 32, of which 9 were waited for; matrix products, arithmetic and copies ran while one was open for 17% of the time, Pallas kernels for 0%

commit v1 on v0

v1 whole, which is shorter than its diff:
```python
import functools

import jax
import jax.numpy as jnp
from jax import lax
from jax.experimental import pallas as pl
from jax.experimental.pallas import tpu as pltpu
from jax.sharding import PartitionSpec as P

STEPS = 2
EPSILON = 1e-06
TIME_STEP = 0.5
BLUR = (1.0 / 16.0, 4.0 / 16.0, 6.0 / 16.0, 4.0 / 16.0, 1.0 / 16.0)
KAPPA = 0.8493218002880191
HIGH = lax.Precision.HIGHEST
LANES = 128
I_ROWS = 64


def dot(a, b, dims, precision=HIGH):
    return lax.dot_general(
        a, b, (dims, ((), ())), precision=precision, preferred_element_type=jnp.float32
    )


def split(value):
    high = value.astype(jnp.bfloat16)
    return high, (value - high.astype(jnp.float32)).astype(jnp.bfloat16)


def dot_split(a, b, dims):
    a_high, a_low = split(a)
    b_high, b_low = split(b)
    return dot(a_high, b_high, dims, None) + (
        dot(a_high, b_low, dims, None) + dot(a_low, b_high, dims, None)
    )


def iota(shape, dim):
    return lax.broadcasted_iota(jnp.int32, shape, dim)


def band(radius, weights):
    offset = iota((256, 256), 0) - iota((256, 256), 1)
    result = jnp.zeros((256, 256), jnp.float32)
    for shift in range(-radius, radius + 1):
        result = jnp.where(offset == shift, weights[shift + radius], result)
    return result


def rows_filtered(values, weights):
    radius = (len(weights) - 1) // 2
    result = weights[radius] * values
    for shift in range(1, radius + 1):
        both = pltpu.roll(values, shift, 1) + pltpu.roll(values, values.shape[1] - shift, 1)
        result = result + weights[radius + shift] * both
    return result


def planes_filtered(values, weights, count):
    result = weights[0] * values[0:count]
    for shift in range(1, len(weights)):
        result = result + weights[shift] * values[shift : shift + count]
    return result


def inside(place, first_plane, planes):
    shape = (planes, 32, 256)
    plane = place[0] * 4 + first_plane + iota(shape, 0)
    row = place[1] * 16 - 8 + iota(shape, 1)
    return (plane >= 0) & (plane < place[2]) & (row >= 0) & (row < place[3])


def prep_kernel(counts, table, fraction, velocity, anchor, kinds, atoms, state):
    for half in range(2):
        lanes = pl.ds(half * 256, 256)
        kind = kinds[0, :, lanes]
        live = (iota((1, 256), 1) + half * 256 < counts[0, 0]).astype(jnp.float32)
        values = []
        for row in range(3):
            value = jnp.zeros((1, 256), jnp.float32)
            for option in range(table.shape[1]):
                value = jnp.where(kind == option, table[row, option], value)
            values.append(value)
        for row in range(3):
            atoms[half, row : row + 1, :] = anchor[row, 0, :, lanes].astype(jnp.float32)
            atoms[half, row + 3 : row + 4, :] = fraction[row, 0, :, lanes]
            state[half, row : row + 1, :] = velocity[row, 0, :, lanes]
            state[half, row + 3 : row + 4, :] = jnp.zeros((1, 256), jnp.float32)
        atoms[half, 6:7, :] = values[0] * live
        atoms[half, 7:8, :] = values[1] * values[1]
        state[half, 6:7, :] = values[2]
        state[half, 7:8, :] = live


def scale_kernel(place, target, scale):
    box = (1.0,) * 9
    matrix = band(4, box)
    value = target[2:19]
    sums = []
    for source in (value, value * value):
        summed = rows_filtered(planes_filtered(source, box, 9), box)
        summed = dot(summed.reshape(288, 256), matrix, ((1,), (0,)))
        sums.append(summed.reshape(9, 32, 256) * (1.0 / 729.0))
    result = lax.rsqrt(sums[1] - sums[0] * sums[0] + EPSILON)
    scale[...] = jnp.where(inside(place, -2, 9), result, 0.0)


def step_kernel(
    last, counts, place, atoms, state, target, scale, *refs
):
    if last:
        final_velocity, displacement, potential_out = refs[:3]
    else:
        atoms_out, state_out = refs[:2]
    pair_blocks, spread_blocks, own_columns, sums, density = refs[-5:]

    row_index = iota((8, LANES), 0)
    pair_count = jnp.int32(0)
    spread_counts = []
    for column in range(5):
        spread_count = jnp.int32(0)
        for side in range(3):
            shift = jnp.where(
                row_index == 0,
                4.0 * (column - 2),
                jnp.where(row_index == 1, 16.0 * (side - 1), 0.0),
            )
            for part in range(4):
                block = atoms[column, side, part // 2, :, pl.ds((part % 2) * LANES, LANES)] + shift
                alive = block[6, 0] > 0.0
                spread_blocks[column, spread_count] = block
                spread_count = spread_count + alive.astype(jnp.int32)
                if column in (1, 2, 3):
                    place_of = block[0:3] + block[3:6]
                    pair_blocks[pair_count, 0:3, :] = KAPPA * place_of
                    pair_blocks[pair_count, 3:4, :] = block[6:7]
                    pair_blocks[pair_count, 4:5, :] = block[7:8]
                    pair_count = pair_count + alive.astype(jnp.int32)
        spread_blocks[column, spread_count] = jnp.zeros((8, LANES), jnp.float32)
        spread_counts.append(spread_count)
    pair_blocks[pair_count] = jnp.zeros((8, LANES), jnp.float32)

    for half in range(2):
        own = atoms[2, 1, half]
        packed = jnp.concatenate(
            [KAPPA * (own[0:3] + own[3:6]), own[7:8], jnp.zeros((4, 256), jnp.float32)], 0
        )
        turned = jnp.transpose(packed)
        for row in range(4):
            own_columns[row, pl.ds(half * 256, 256), :] = jnp.broadcast_to(
                turned[:, row : row + 1], (256, LANES)
            )
    sums[...] = jnp.zeros(sums.shape, jnp.float32)

    def add_rows(index, carry):
        rows = pl.ds(index * I_ROWS, I_ROWS)
        own_x, own_y, own_z, own_s = (own_columns[row, rows, :] for row in range(4))

        def add_blocks(step, totals):
            for part in range(2):
                block = pair_blocks[step * 2 + part]
                x = own_x - block[0:1]
                y = own_y - block[1:2]
                z = own_z - block[2:3]
                spread = own_s + block[4:5]
                inverse = pl.reciprocal(spread, approx=True)
                inverse = inverse * (2.0 - spread * inverse)
                squared = x * x + y * y + z * z
                factor = block[3:4] * jnp.exp2(-(squared * inverse)) * inverse
                totals = (totals[0] + factor * x, totals[1] + factor * y, totals[2] + factor * z)
            return totals

        zero = jnp.zeros((I_ROWS, LANES), jnp.float32)
        totals = lax.fori_loop(0, (pair_count + 1) // 2, add_blocks, (zero, zero, zero))
        for axis in range(3):
            sums[axis, rows, :] = totals[axis]
        return carry

    lax.fori_loop(0, (counts[0, 0] + I_ROWS - 1) // I_ROWS, add_rows, 0)

    density[...] = jnp.zeros(density.shape, jnp.float32)
    depth = iota((256, 256), 0).astype(jnp.float32)
    height = iota((32, 256), 0).astype(jnp.float32) - 8.0
    for column in range(5):
        planes = {0: (-4,), 4: (8,)}.get(column) or tuple(range(4 * column - 8, 4 * column - 3))

        def add_chunk(step, carry, column=column, planes=planes):
            chunk = jnp.concatenate(
                [spread_blocks[column, step * 2], spread_blocks[column, step * 2 + 1]], 1
            )
            fx, fy, fz = chunk[3:4], chunk[4:5], chunk[5:6]
            charge = chunk[6:7]
            weight_z = jnp.where(
                depth == chunk[2:3],
                charge * (1.0 - fz),
                jnp.where(depth == chunk[2:3] + 1.0, charge * fz, 0.0),
            )
            weight_y = jnp.where(
                height == chunk[1:2], 1.0 - fy, jnp.where(height == chunk[1:2] + 1.0, fy, 0.0)
            )
            parts = []
            for plane in planes:
                weight_x = jnp.where(
                    chunk[0:1] == plane, 1.0 - fx, jnp.where(chunk[0:1] + 1.0 == plane, fx, 0.0)
                )
                parts.append(weight_x * weight_y)
            added = dot_split(jnp.concatenate(parts, 0), weight_z, ((1,), (1,)))
            where = pl.ds(planes[0] + 4, len(planes))
            density[where] = density[where] + added.reshape(len(planes), 32, 256)
            return carry

        lax.fori_loop(0, (spread_counts[column] + 1) // 2, add_chunk, 0)

    matrix = band(2, BLUR)
    value = jnp.where(inside(place, -4, 13), density[...], 0.0)
    value = rows_filtered(planes_filtered(value, BLUR, 9), BLUR)
    value = dot(value.reshape(288, 256), matrix, ((1,), (0,))).reshape(9, 32, 256)
    residual = (value - target[6:15]) * scale[...]
    value = rows_filtered(planes_filtered(residual, BLUR, 5), BLUR)
    value = dot(value.reshape(160, 256), matrix, ((1,), (0,))).reshape(5, 32, 256)
    potential = jnp.where(inside(place, 0, 5), value, 0.0)
    if last:
        potential_out[...] = potential[0:4, 8:24]
    field = potential[:, 8:32].reshape(120, 256)

    ones = jnp.ones((8, LANES), jnp.float32)
    height = iota((24, 256), 0).astype(jnp.float32)
    for half in range(2):
        own = atoms[2, 1, half]
        gx, gy, gz, fx, fy, fz = (own[row : row + 1] for row in range(6))
        lower, upper = depth == gz, depth == gz + 1.0
        product = dot_split(
            field, jnp.where(lower, 1.0 - fz, jnp.where(upper, fz, 0.0)), ((1,), (0,))
        ).reshape(5, 24, 256)
        slope = jnp.where(lower, -1.0, jnp.where(upper, 1.0, 0.0))
        product_z = dot_split(field, slope, ((1,), (0,))).reshape(5, 24, 256)
        lower, upper = height == gy, height == gy + 1.0
        weight_y = jnp.where(lower, 1.0 - fy, jnp.where(upper, fy, 0.0))
        slope_y = jnp.where(lower, -1.0, jnp.where(upper, 1.0, 0.0))
        mixed = [jnp.zeros((24, 256), jnp.float32) for _ in range(3)]
        for plane in range(5):
            lower, upper = gx == plane, gx + 1.0 == plane
            weight_x = jnp.where(lower, 1.0 - fx, jnp.where(upper, fx, 0.0))
            slope_x = jnp.where(lower, -1.0, jnp.where(upper, 1.0, 0.0))
            mixed[0] = mixed[0] + slope_x * product[plane]
            mixed[1] = mixed[1] + weight_x * product[plane]
            mixed[2] = mixed[2] + weight_x * product_z[plane]
        gradient = (
            jnp.sum(mixed[0] * weight_y, 0, keepdims=True),
            jnp.sum(mixed[1] * slope_y, 0, keepdims=True),
            jnp.sum(mixed[2] * weight_y, 0, keepdims=True),
        )
        charge = own[6:7]
        values = state[half]
        mass, live = values[6:7], values[7:8]
        if not last:
            atoms_out[half, 6:8, :] = own[6:8]
            atoms_out[half, 0:3, :] = own[0:3]
            state_out[half, 6:8, :] = values[6:8]
        for axis in range(3):
            pair = dot(ones, sums[axis, pl.ds(half * 256, 256), :], ((1,), (1,)))[0:1]
            force = charge * (pair * (1.0 / KAPPA) - gradient[axis])
            velocity = values[axis : axis + 1] + TIME_STEP * force / mass
            moved = values[axis + 3 : axis + 4] + TIME_STEP * velocity
            if last:
                lanes = pl.ds(half * 256, 256)
                final_velocity[axis, 0, :, lanes] = velocity * live
                displacement[axis, 0, :, lanes] = moved * live
            else:
                state_out[half, axis : axis + 1, :] = velocity
                state_out[half, axis + 3 : axis + 4, :] = moved
                atoms_out[half, axis + 3 : axis + 4, :] = (
                    own[axis + 3 : axis + 4] + TIME_STEP * velocity
                )


SMEM = pl.BlockSpec(memory_space=pltpu.SMEM)
VMEM = pl.BlockSpec(memory_space=pltpu.VMEM)


def shape(*dims):
    return jax.ShapeDtypeStruct(dims, jnp.float32)


def links():
    chips = lax.axis_size("cells") // 2
    groups = lax.axis_size("grp")

    def coloured(count, first):
        pairs = []
        for left in range(first, count - 1, 2):
            pairs += [(left, left + 1), (left + 1, left)]
        return pairs

    def doubled(pairs):
        return [(2 * a + core, 2 * b + core) for a, b in pairs for core in range(2)]

    return {
        "odd": ("cells", doubled(coloured(chips, 1))),
        "even": ("cells", doubled(coloured(chips, 0))),
        "rows_even": ("grp", coloured(groups, 0)),
        "rows_odd": ("grp", coloured(groups, 1)),
        "pair": ("cells", [(i, i ^ 1) for i in range(2 * chips)]),
    }


def spread_out(own, rows, groups, flags):
    even_chip, even_row, first_core = flags

    def send(value, link):
        return lax.ppermute(value, *groups[link])

    odd = send(own, "odd")
    even = send(own, "even")
    left = jnp.where(even_chip, odd, even)
    right = jnp.where(even_chip, even, odd)
    columns = jnp.stack([own, left, right])
    from_even = send(rows(columns, even_row), "rows_even")
    from_odd = send(rows(columns, ~even_row), "rows_odd")
    above = jnp.where(even_row, from_even, from_odd)
    below = jnp.where(even_row, from_odd, from_even)
    return columns, below, above, functools.partial(send, link="pair")


def finish(full, send, first_core):
    chosen = jnp.where(first_core, full[2], full[1])
    got = send(jnp.stack([full[0], chosen]))
    minus = jnp.where(first_core, got[1], got[0])
    plus = jnp.where(first_core, got[0], got[1])
    return jnp.stack([full[1], minus, full[0], plus, full[2]])


def per_device(fraction, velocity, anchor, atom_types, counts, type_table, target):
    cells, groups_count = lax.axis_size("cells"), lax.axis_size("grp")
    cell, group = lax.axis_index("cells"), lax.axis_index("grp")
    groups = links()
    flags = ((cell // 2) % 2 == 0, group % 2 == 0, cell % 2 == 0)
    place = jnp.stack(
        [cell, group, jnp.int32(cells * 4), jnp.int32(groups_count * 16)]
    ).astype(jnp.int32)

    atoms, state = pl.pallas_call(
        prep_kernel,
        out_shape=(shape(2, 8, 256), shape(2, 8, 256)),
        in_specs=[SMEM, SMEM, VMEM, VMEM, VMEM, VMEM],
        out_specs=(VMEM, VMEM),
        name="prep",
    )(counts, type_table, fraction, velocity, anchor, atom_types)

    def rows_first(columns, upper):
        fields = columns[:, 2:].reshape(3, 4, 2, 8, 256)
        return jnp.concatenate(
            [columns[:, :2], jnp.where(upper, fields[:, :, 1], fields[:, :, 0])], 1
        )

    own = jnp.concatenate([atoms, target.reshape(8, 8, 256)], 0)
    columns, below, above, send = spread_out(own, rows_first, groups, flags)
    full = jnp.concatenate(
        [
            jnp.stack([below[:, :2], columns[:, :2], above[:, :2]], 1).reshape(3, 6, 8, 256),
            jnp.concatenate(
                [
                    below[:, 2:, None],
                    columns[:, 2:].reshape(3, 4, 2, 8, 256),
                    above[:, 2:, None],
                ],
                2,
            ).reshape(3, 16, 8, 256),
        ],
        1,
    )
    full = finish(full, send, flags[2])
    near = full[:, :6].reshape(5, 3, 2, 8, 256)
    wide = full[:, 6:].reshape(20, 32, 256)

    scale = pl.pallas_call(
        scale_kernel,
        out_shape=shape(9, 32, 256),
        in_specs=[SMEM, VMEM],
        out_specs=VMEM,
        name="scale",
    )(place, wide)

    scratch = [
        pltpu.VMEM((38, 8, LANES), jnp.float32),
        pltpu.VMEM((5, 14, 8, LANES), jnp.float32),
        pltpu.VMEM((4, 512, LANES), jnp.float32),
        pltpu.VMEM((3, 512, LANES), jnp.float32),
        pltpu.VMEM((13, 32, 256), jnp.float32),
    ]
    for turn in range(STEPS):
        last = turn == STEPS - 1
        if last:
            outs = (shape(*velocity.shape), shape(*velocity.shape), shape(*target.shape))
        else:
            outs = (shape(2, 8, 256), shape(2, 8, 256))
        result = pl.pallas_call(
            functools.partial(step_kernel, last),
            out_shape=outs,
            in_specs=[SMEM, SMEM, VMEM, VMEM, VMEM, VMEM],
            out_specs=(VMEM,) * len(outs),
            scratch_shapes=scratch,
            name="step_last" if last else "step",
        )(counts, place, near, state, wide, scale)
        if last:
            return result
        atoms, state = result
        columns, below, above, send = spread_out(atoms, lambda c, upper: c, groups, flags)
        full = jnp.stack([below, columns, above], 1)
        near = finish(full, send, flags[2])


def solution(mesh):
    placed = (
        P(None, "cells", "grp", None),
        P(None, "cells", "grp", None),
        P(None, "cells", "grp", None),
        P("cells", "grp", None),
        P("cells", "grp"),
        P(),
        P("cells", "grp", None),
    )
    return jax.shard_map(
        per_device,
        mesh=mesh,
        in_specs=placed,
        out_specs=(
            P(None, "cells", "grp", None),
            P(None, "cells", "grp", None),
            P("cells", "grp", None),
        ),
        check_vma=False,
    )
```

time: 234 us -> 104 us (0.44)
  the two profiles are of different devices: /device:TPU:351 before, /device:TPU:72 now
where the time goes in v1:
time: 104 us
  Pallas kernels  39.3 us (38%)
  starting transfers between devices  33.1 us (32%)
  waiting for transfers between devices  25.4 us (24%)
  local copies, waits for them, and re-layouts  3.09 us (3%)
  other arithmetic  1.87 us (2%)
  between operations  1.63 us (2%)
    pallas_call x2, Pallas kernels, per_device(): pl.pallas_call(functools.partial(step_kernel, last), out_shape=outs, in_s...  34.6 us
    ppermute x10, starting transfers between devices, send(): return lax.ppermute(value, *groups[link])  33.1 us
    ppermute x10, waiting for transfers between devices, send(): return lax.ppermute(value, *groups[link])  25.4 us
    pallas_call x1, Pallas kernels, per_device(): pl.pallas_call(scale_kernel, out_shape=shape(9, 32, 256), in_specs=[SMEM,...  3.3 us
  transfers between devices with their start and end apart: 10, of which 9 were waited for; matrix products, arithmetic and copies ran while one was open for 1% of the time, Pallas kernels for 0%

profile of v1, /device:TPU:72, one launch (start us, length us, event | category | flops | bytes accessed | tf_op | source)
XLA Modules:
  0.0 104.4 jit_solution(15433807457679443440)
XLA Ops:
  1.3 1.5 %prep.1 = (f32[2,8,256]{2,1,0:T(8,128)}, f32[2,8,256]{2,1,0:T(8,128)}) custom-call(s32[1,1]{1,0:T(1,128)S(6)} %copy.27.counts, f32[3,8]{1,0:T(4,128)} %table.1, f32[3,1,1,512]{3,2,1,0:T(1,128)} %fraction.1, f32[3,1,1,512]{3,2,1,0:T(1,128)} %velocity.1, s32[3,1,1,512]{3,2,1,0:T(1,128)} %anchor.1, s32[1,1,512]{2,1,0:T(1,128)} %kinds.1), custom_call_target="tpu_custom_call" | custom-call | tf_op jit(solution)/shard_map/prep/pallas_call | solution.py:343
  2.7 0.9 fusion.3
  3.6 12.1 %collective-permute-start = (f32[10,8,256]{2,1,0:T(8,128)S(1)}, f32[10,8,256]{2,1,0:T(8,128)S(1)}, u32[]{:S(2)}, u32[]{:S(2)}) collective-permute-start(f32[10,8,256]{2,1,0:T(8,128)S(1)} %get-tuple-element.26), channel_id=1, source_target_pairs={{8,16},{12,20},{16,8},{20,12},{24,32},{28,36},{32,24},{36,28},{40,... | collective-permute-start | bytes 245768 | tf_op jit(solution)/shard_map/ppermute | solution.py:312
  15.7 1.9 %collective-permute-start.1 = (f32[10,8,256]{2,1,0:T(8,128)S(1)}, f32[10,8,256]{2,1,0:T(8,128)S(1)}, u32[]{:S(2)}, u32[]{:S(2)}) collective-permute-start(f32[10,8,256]{2,1,0:T(8,128)S(1)} %get-tuple-element.26), channel_id=1, source_target_pairs={{0,8},{4,12},{8,0},{12,4},{16,24},{20,28},{24,16},{28,20},{32,40},... | collective-permute-start | bytes 245768 | tf_op jit(solution)/shard_map/ppermute | solution.py:312
  17.7 0.5 collective-permute-done
  18.1 3.9 %collective-permute-done.1 = f32[10,8,256]{2,1,0:T(8,128)S(1)} collective-permute-done((f32[10,8,256]{2,1,0:T(8,128)S(1)}, f32[10,8,256]{2,1,0:T(8,128)S(1)}, u32[]{:S(2)}, u32[]{:S(2)}) %collective-permute-start.1) | collective-permute-done | bytes 81952 | tf_op jit(solution)/shard_map/ppermute | solution.py:312
  22.2 3.4 %collective-permute-start.2 = (f32[3,6,8,256]{3,2,1,0:T(8,128)S(1)}, f32[3,6,8,256]{3,2,1,0:T(8,128)S(1)}, u32[]{:S(2)}, u32[]{:S(2)}) collective-permute-start(f32[3,6,8,256]{3,2,1,0:T(8,128)S(1)} %get-tuple-element.29), channel_id=1, source_target_pairs={{1,2},{2,1},{5,6},{6,5},{9,10},{10,9},{13,14},{14,13},{17,18},{18,... | collective-permute-start | bytes 442376 | tf_op jit(solution)/shard_map/ppermute | solution.py:312
  25.5 1.9 %collective-permute-start.3 = (f32[3,6,8,256]{3,2,1,0:T(8,128)S(1)}, f32[3,6,8,256]{3,2,1,0:T(8,128)S(1)}, u32[]{:S(2)}, u32[]{:S(2)}) collective-permute-start(f32[3,6,8,256]{3,2,1,0:T(8,128)S(1)} %get-tuple-element.30), channel_id=1, source_target_pairs={{0,1},{1,0},{2,3},{3,2},{4,5},{5,4},{6,7},{7,6},{8,9},{9,8},{10,11... | collective-permute-start | bytes 442376 | tf_op jit(solution)/shard_map/ppermute | solution.py:312
  27.5 1.7 %collective-permute-done.2 = f32[3,6,8,256]{3,2,1,0:T(8,128)S(1)} collective-permute-done((f32[3,6,8,256]{3,2,1,0:T(8,128)S(1)}, f32[3,6,8,256]{3,2,1,0:T(8,128)S(1)}, u32[]{:S(2)}, u32[]{:S(2)}) %collective-permute-start.2) | collective-permute-done | bytes 147488 | tf_op jit(solution)/shard_map/ppermute | solution.py:312
  29.2 3.4 %collective-permute-done.3 = f32[3,6,8,256]{3,2,1,0:T(8,128)S(1)} collective-permute-done((f32[3,6,8,256]{3,2,1,0:T(8,128)S(1)}, f32[3,6,8,256]{3,2,1,0:T(8,128)S(1)}, u32[]{:S(2)}, u32[]{:S(2)}) %collective-permute-start.3) | collective-permute-done | bytes 147488 | tf_op jit(solution)/shard_map/ppermute | solution.py:312
  32.8 1.9 %collective-permute-start.4 = (f32[2,22,8,256]{3,2,1,0:T(8,128)S(1)}, f32[2,22,8,256]{3,2,1,0:T(8,128)S(1)}, u32[]{:S(2)}, u32[]{:S(2)}) collective-permute-start(f32[2,22,8,256]{3,2,1,0:T(8,128)S(1)} %pad_maximum_fusion.1), channel_id=1, source_target_pairs={{0,4},{4,0},{8,12},{12,8},{16,20},{20,16},{24,28},{28,24},{32,36},... | collective-permute-start | bytes 1081352 | tf_op jit(solution)/shard_map/ppermute | solution.py:312
  34.7 0.7 pad_add_fusion.place
  35.4 1.0 collective-permute-done.4
  36.5 0.7 slice.108
  37.2 0.9 slice.109
  38.1 3.3 %scale.1 = f32[9,32,256]{2,1,0:T(8,128)} custom-call(s32[4]{0:T(128)} %pad_add_fusion.place, f32[20,32,256]{2,1,0:T(8,128)} %bitcast.59), custom_call_target="tpu_custom_call" | custom-call | tf_op jit(solution)/shard_map/scale/pallas_call | solution.py:377
  41.4 17.3 %step.1 = (f32[2,8,256]{2,1,0:T(8,128)}, f32[2,8,256]{2,1,0:T(8,128)}) custom-call(s32[1,1]{1,0:T(1,128)S(6)} %copy.27.counts, s32[4]{0:T(128)} %pad_add_fusion.place, f32[5,3,2,8,256]{4,3,2,1,0:T(8,128)} %bitcast.68, f32[2,8,256]{2,1,0:T(8,128)} %get-tuple-element.8.state, f32[20,32,256]{2,1,0:T(8,128)} %bitcast.60, f32[9,32,256]{2,1,0:T(8,128)} %scale.1), custom_call_target="tpu_custom_call" | custom-call | tf_op jit(solution)/shard_map/step/pallas_call | solution.py:398
  58.7 3.0 %collective-permute-start.6 = (f32[2,8,256]{2,1,0:T(8,128)}, f32[2,8,256]{2,1,0:T(8,128)S(1)}, u32[]{:S(2)}, u32[]{:S(2)}) collective-permute-start(f32[2,8,256]{2,1,0:T(8,128)} %get-tuple-element.9), channel_id=1, source_target_pairs={{0,8},{4,12},{8,0},{12,4},{16,24},{20,28},{24,16},{28,20},{32,40},... | collective-permute-start | bytes 49160 | tf_op jit(solution)/shard_map/ppermute | solution.py:312
  61.7 3.1 %collective-permute-start.5 = (f32[2,8,256]{2,1,0:T(8,128)}, f32[2,8,256]{2,1,0:T(8,128)S(1)}, u32[]{:S(2)}, u32[]{:S(2)}) collective-permute-start(f32[2,8,256]{2,1,0:T(8,128)} %get-tuple-element.9), channel_id=1, source_target_pairs={{8,16},{12,20},{16,8},{20,12},{24,32},{28,36},{32,24},{36,28},{40,... | collective-permute-start | bytes 49160 | tf_op jit(solution)/shard_map/ppermute | solution.py:312
  64.7 0.0 collective-permute-done.6
  64.8 9.7 %collective-permute-done.5 = f32[2,8,256]{2,1,0:T(8,128)S(1)} collective-permute-done((f32[2,8,256]{2,1,0:T(8,128)}, f32[2,8,256]{2,1,0:T(8,128)S(1)}, u32[]{:S(2)}, u32[]{:S(2)}) %collective-permute-start.5) | collective-permute-done | bytes 16416 | tf_op jit(solution)/shard_map/ppermute | solution.py:312
  74.4 0.0 copy-start.1
  74.4 0.7 copy-done.1
  75.1 1.9 %collective-permute-start.8 = (f32[3,2,8,256]{3,2,1,0:T(8,128)S(1)}, f32[3,2,8,256]{3,2,1,0:T(8,128)S(1)}, u32[]{:S(2)}, u32[]{:S(2)}) collective-permute-start(f32[3,2,8,256]{3,2,1,0:T(8,128)S(1)} %get-tuple-element.28), channel_id=1, source_target_pairs={{0,1},{1,0},{2,3},{3,2},{4,5},{5,4},{6,7},{7,6},{8,9},{9,8},{10,11... | collective-permute-start | bytes 147464 | tf_op jit(solution)/shard_map/ppermute | solution.py:312
  77.1 1.9 %collective-permute-start.7 = (f32[3,2,8,256]{3,2,1,0:T(8,128)S(1)}, f32[3,2,8,256]{3,2,1,0:T(8,128)S(1)}, u32[]{:S(2)}, u32[]{:S(2)}) collective-permute-start(f32[3,2,8,256]{3,2,1,0:T(8,128)S(1)} %get-tuple-element.28), channel_id=1, source_target_pairs={{1,2},{2,1},{5,6},{6,5},{9,10},{10,9},{13,14},{14,13},{17,18},{18,... | collective-permute-start | bytes 147464 | tf_op jit(solution)/shard_map/ppermute | solution.py:312
  79.0 2.1 %collective-permute-done.8 = f32[3,2,8,256]{3,2,1,0:T(8,128)S(1)} collective-permute-done((f32[3,2,8,256]{3,2,1,0:T(8,128)S(1)}, f32[3,2,8,256]{3,2,1,0:T(8,128)S(1)}, u32[]{:S(2)}, u32[]{:S(2)}) %collective-permute-start.8) | collective-permute-done | bytes 49184 | tf_op jit(solution)/shard_map/ppermute | solution.py:312
  81.1 1.9 %collective-permute-done.7 = f32[3,2,8,256]{3,2,1,0:T(8,128)S(1)} collective-permute-done((f32[3,2,8,256]{3,2,1,0:T(8,128)S(1)}, f32[3,2,8,256]{3,2,1,0:T(8,128)S(1)}, u32[]{:S(2)}, u32[]{:S(2)}) %collective-permute-start.7) | collective-permute-done | bytes 49184 | tf_op jit(solution)/shard_map/ppermute | solution.py:312
  83.1 1.9 %collective-permute-start.9 = (f32[2,3,2,8,256]{4,3,2,1,0:T(8,128)S(1)}, f32[2,3,2,8,256]{4,3,2,1,0:T(8,128)S(1)}, u32[]{:S(2)}, u32[]{:S(2)}) collective-permute-start(f32[2,3,2,8,256]{4,3,2,1,0:T(8,128)S(1)} %pad_maximum_fusion.9), channel_id=1, source_target_pairs={{0,4},{4,0},{8,12},{12,8},{16,20},{20,16},{24,28},{28,24},{32,36},... | collective-permute-start | bytes 294920 | tf_op jit(solution)/shard_map/ppermute | solution.py:312
  85.1 1.3 %collective-permute-done.9 = f32[2,3,2,8,256]{4,3,2,1,0:T(8,128)S(1)} collective-permute-done((f32[2,3,2,8,256]{4,3,2,1,0:T(8,128)S(1)}, f32[2,3,2,8,256]{4,3,2,1,0:T(8,128)S(1)}, u32[]{:S(2)}, u32[]{:S(2)}) %collective-permute-start.9) | collective-permute-done | bytes 98336 | tf_op jit(solution)/shard_map/ppermute | solution.py:312
  86.4 0.0 copy-start
  86.4 0.7 copy-done
  87.1 17.3 %step_last.1 = (f32[3,1,1,512]{3,2,1,0:T(1,128)}, f32[3,1,1,512]{3,2,1,0:T(1,128)}, f32[4,16,256]{2,1,0:T(8,128)}) custom-call(s32[1,1]{1,0:T(1,128)S(6)} %copy.27.counts, s32[4]{0:T(128)} %pad_add_fusion.place, f32[5,3,2,8,256]{4,3,2,1,0:T(8,128)} %copy-done, f32[2,8,256]{2,1,0:T(8,128)} %get-tuple-element.10.state, f32[20,32,256]{2,1,0:T(8,128)} %bitcast.61, ...), custom_call_target="tpu_custom_call" | custom-call | tf_op jit(solution)/shard_map/step_last/pallas_call | solution.py:398
  (28 shorter events, 0.4 us)
Async XLA Ops:
  3.6 14.5 %collective-permute-start = (f32[10,8,256]{2,1,0:T(8,128)S(1)}, f32[10,8,256]{2,1,0:T(8,128)S(1)}, u32[]{:S(2)}, u32[]{:S(2)}) collective-permute-start(f32[10,8,256]{2,1,0:T(8,128)S(1)} %get-tuple-element.26), channel_id=1, source_target_pairs={{8,16},{12,20},{16,8},{20,12},{24,32},{28,36},{32,24},{36,28},{40,... | collective-permute-start | bytes 245768 | tf_op jit(solution)/shard_map/ppermute | solution.py:312
  15.7 6.3 %collective-permute-start.1 = (f32[10,8,256]{2,1,0:T(8,128)S(1)}, f32[10,8,256]{2,1,0:T(8,128)S(1)}, u32[]{:S(2)}, u32[]{:S(2)}) collective-permute-start(f32[10,8,256]{2,1,0:T(8,128)S(1)} %get-tuple-element.26), channel_id=1, source_target_pairs={{0,8},{4,12},{8,0},{12,4},{16,24},{20,28},{24,16},{28,20},{32,40},... | collective-permute-start | bytes 245768 | tf_op jit(solution)/shard_map/ppermute | solution.py:312
  22.2 7.0 %collective-permute-start.2 = (f32[3,6,8,256]{3,2,1,0:T(8,128)S(1)}, f32[3,6,8,256]{3,2,1,0:T(8,128)S(1)}, u32[]{:S(2)}, u32[]{:S(2)}) collective-permute-start(f32[3,6,8,256]{3,2,1,0:T(8,128)S(1)} %get-tuple-element.29), channel_id=1, source_target_pairs={{1,2},{2,1},{5,6},{6,5},{9,10},{10,9},{13,14},{14,13},{17,18},{18,... | collective-permute-start | bytes 442376 | tf_op jit(solution)/shard_map/ppermute | solution.py:312
  25.5 7.0 %collective-permute-start.3 = (f32[3,6,8,256]{3,2,1,0:T(8,128)S(1)}, f32[3,6,8,256]{3,2,1,0:T(8,128)S(1)}, u32[]{:S(2)}, u32[]{:S(2)}) collective-permute-start(f32[3,6,8,256]{3,2,1,0:T(8,128)S(1)} %get-tuple-element.30), channel_id=1, source_target_pairs={{0,1},{1,0},{2,3},{3,2},{4,5},{5,4},{6,7},{7,6},{8,9},{9,8},{10,11... | collective-permute-start | bytes 442376 | tf_op jit(solution)/shard_map/ppermute | solution.py:312
  32.8 3.6 %collective-permute-start.4 = (f32[2,22,8,256]{3,2,1,0:T(8,128)S(1)}, f32[2,22,8,256]{3,2,1,0:T(8,128)S(1)}, u32[]{:S(2)}, u32[]{:S(2)}) collective-permute-start(f32[2,22,8,256]{3,2,1,0:T(8,128)S(1)} %pad_maximum_fusion.1), channel_id=1, source_target_pairs={{0,4},{4,0},{8,12},{12,8},{16,20},{20,16},{24,28},{28,24},{32,36},... | collective-permute-start | bytes 1081352 | tf_op jit(solution)/shard_map/ppermute | solution.py:312
  58.7 6.1 %collective-permute-start.6 = (f32[2,8,256]{2,1,0:T(8,128)}, f32[2,8,256]{2,1,0:T(8,128)S(1)}, u32[]{:S(2)}, u32[]{:S(2)}) collective-permute-start(f32[2,8,256]{2,1,0:T(8,128)} %get-tuple-element.9), channel_id=1, source_target_pairs={{0,8},{4,12},{8,0},{12,4},{16,24},{20,28},{24,16},{28,20},{32,40},... | collective-permute-start | bytes 49160 | tf_op jit(solution)/shard_map/ppermute | solution.py:312
  61.7 12.8 %collective-permute-start.5 = (f32[2,8,256]{2,1,0:T(8,128)}, f32[2,8,256]{2,1,0:T(8,128)S(1)}, u32[]{:S(2)}, u32[]{:S(2)}) collective-permute-start(f32[2,8,256]{2,1,0:T(8,128)} %get-tuple-element.9), channel_id=1, source_target_pairs={{8,16},{12,20},{16,8},{20,12},{24,32},{28,36},{32,24},{36,28},{40,... | collective-permute-start | bytes 49160 | tf_op jit(solution)/shard_map/ppermute | solution.py:312
  74.4 0.7 copy-start.1
  75.1 6.0 %collective-permute-start.8 = (f32[3,2,8,256]{3,2,1,0:T(8,128)S(1)}, f32[3,2,8,256]{3,2,1,0:T(8,128)S(1)}, u32[]{:S(2)}, u32[]{:S(2)}) collective-permute-start(f32[3,2,8,256]{3,2,1,0:T(8,128)S(1)} %get-tuple-element.28), channel_id=1, source_target_pairs={{0,1},{1,0},{2,3},{3,2},{4,5},{5,4},{6,7},{7,6},{8,9},{9,8},{10,11... | collective-permute-start | bytes 147464 | tf_op jit(solution)/shard_map/ppermute | solution.py:312
  77.1 6.0 %collective-permute-start.7 = (f32[3,2,8,256]{3,2,1,0:T(8,128)S(1)}, f32[3,2,8,256]{3,2,1,0:T(8,128)S(1)}, u32[]{:S(2)}, u32[]{:S(2)}) collective-permute-start(f32[3,2,8,256]{3,2,1,0:T(8,128)S(1)} %get-tuple-element.28), channel_id=1, source_target_pairs={{1,2},{2,1},{5,6},{6,5},{9,10},{10,9},{13,14},{14,13},{17,18},{18,... | collective-permute-start | bytes 147464 | tf_op jit(solution)/shard_map/ppermute | solution.py:312
  83.1 3.2 %collective-permute-start.9 = (f32[2,3,2,8,256]{4,3,2,1,0:T(8,128)S(1)}, f32[2,3,2,8,256]{4,3,2,1,0:T(8,128)S(1)}, u32[]{:S(2)}, u32[]{:S(2)}) collective-permute-start(f32[2,3,2,8,256]{4,3,2,1,0:T(8,128)S(1)} %pad_maximum_fusion.9), channel_id=1, source_target_pairs={{0,4},{4,0},{8,12},{12,8},{16,20},{20,16},{24,28},{28,24},{32,36},... | collective-permute-start | bytes 294920 | tf_op jit(solution)/shard_map/ppermute | solution.py:312
  86.4 0.7 copy-start

commit v2 on v1

v2 whole, which is shorter than its diff:
```python
import functools

import jax
import jax.numpy as jnp
from jax import lax
from jax.experimental import pallas as pl
from jax.experimental.pallas import tpu as pltpu
from jax.sharding import PartitionSpec as P

STEPS = 2
EPSILON = 1e-06
TIME_STEP = 0.5
BLUR = (1.0 / 16.0, 4.0 / 16.0, 6.0 / 16.0, 4.0 / 16.0, 1.0 / 16.0)
KAPPA = 0.8493218002880191
LANES = 128
I_ROWS = 64


def dot(a, b, dims, precision=None):
    return lax.dot_general(
        a, b, (dims, ((), ())), precision=precision, preferred_element_type=jnp.float32
    )


def split(value, pieces):
    parts = []
    for _ in range(pieces):
        parts.append(value.astype(jnp.bfloat16))
        value = value - parts[-1].astype(jnp.float32)
    return parts


def dot_exact(a, b, dims, pieces=2):
    total = None
    for part in reversed(split(a, pieces)):
        product = dot(part, b, dims)
        total = product if total is None else total + product
    return total


def iota(shape, dim):
    return lax.broadcasted_iota(jnp.int32, shape, dim)


def band(weights):
    radius = (len(weights) - 1) // 2
    offset = iota((256, 256), 0) - iota((256, 256), 1)
    result = jnp.zeros((256, 256), jnp.float32)
    for shift in range(-radius, radius + 1):
        result = jnp.where(offset == shift, weights[shift + radius], result)
    return result.astype(jnp.bfloat16)


def rows_filtered(values, weights):
    radius = (len(weights) - 1) // 2
    result = weights[radius] * values
    for shift in range(1, radius + 1):
        both = pltpu.roll(values, shift, 1) + pltpu.roll(values, values.shape[1] - shift, 1)
        result = result + weights[radius + shift] * both
    return result


def rows_boxed(values):
    pairs = values + pltpu.roll(values, 1, 1)
    fours = pairs + pltpu.roll(pairs, 2, 1)
    eights = fours + pltpu.roll(fours, 4, 1)
    nines = eights + pltpu.roll(values, 8, 1)
    return pltpu.roll(nines, values.shape[1] - 4, 1)


def depth_filtered(values, matrix, pieces):
    flat = values.reshape(values.shape[0] * 32, 256)
    return dot_exact(flat, matrix, ((1,), (0,)), pieces).reshape(values.shape)


def planes_filtered(values, weights, count):
    result = weights[0] * values[0:count]
    for shift in range(1, len(weights)):
        result = result + weights[shift] * values[shift : shift + count]
    return result


def plane_inside(place, plane):
    position = place[0] * 4.0 + plane
    return ((position >= 0.0) & (position < place[2])).astype(jnp.float32)


def rows_inside(place, first, rows):
    position = place[1] * 16.0 + first + iota((rows, 256), 0).astype(jnp.float32)
    return (position >= 0.0) & (position < place[3])


def prep_kernel(
    counts, table, fraction_in, velocity_in, anchor_in, kinds_in, target_in, sent, state,
    fraction, velocity, anchor, kinds, target, sems,
):
    pairs = ((fraction_in, fraction), (velocity_in, velocity), (anchor_in, anchor))
    pairs += ((kinds_in, kinds), (target_in, target))
    copies = [pltpu.make_async_copy(*pair, sems.at[i]) for i, pair in enumerate(pairs)]
    for copy in copies:
        copy.start()
    info = (lax.axis_index("cells"), lax.axis_index("grp"), counts[0, 0])
    for row, value in enumerate(info):
        state[2, row : row + 1, :] = jnp.full((1, 256), value, jnp.int32).astype(jnp.float32)
    state[2, 3:8, :] = jnp.zeros((5, 256), jnp.float32)
    for copy in copies:
        copy.wait()
    for half in range(2):
        lanes = pl.ds(half * 256, 256)
        kind = kinds[0, :, lanes]
        live = (iota((1, 256), 1) + half * 256 < counts[0, 0]).astype(jnp.float32)
        values = []
        for row in range(3):
            value = jnp.zeros((1, 256), jnp.float32)
            for option in range(table.shape[1]):
                value = jnp.where(kind == option, table[row, option], value)
            values.append(value)
        for row in range(3):
            sent[half, row : row + 1, :] = anchor[row, 0, :, lanes].astype(jnp.float32)
            sent[half, row + 3 : row + 4, :] = fraction[row, 0, :, lanes]
            state[half, row : row + 1, :] = velocity[row, 0, :, lanes]
            state[half, row + 3 : row + 4, :] = jnp.zeros((1, 256), jnp.float32)
        sent[half, 6:7, :] = values[0] * live
        sent[half, 7:8, :] = values[1] * values[1]
        state[half, 6:7, :] = values[2]
        state[half, 7:8, :] = live
    for plane in range(4):
        for half in range(2):
            sent[2 + 2 * plane + half] = target[plane, pl.ds(8 * half, 8), :]


def inverse_scale(place, full, scale, scaled):
    matrix = band((1.0,) * 9)
    rows = rows_inside(place, -8, 32)
    planes = [full[index // 4, pl.ds(6 + index % 4 * 4, 4)] for index in range(2, 19)]
    planes = jnp.stack([plane.reshape(32, 256) for plane in planes])
    sums = []
    for source in (planes, planes * planes):
        pairs = source[0:16] + source[1:17]
        fours = pairs[0:14] + pairs[2:16]
        summed = fours[0:9] + fours[4:13] + source[8:17]
        sums.append(depth_filtered(rows_boxed(summed), matrix, 3) * (1.0 / 729.0))
    value = lax.rsqrt(sums[1] - sums[0] * sums[0] + EPSILON)
    for plane in range(9):
        kept = jnp.where(rows, value[plane], 0.0) * plane_inside(place, plane - 2)
        scale[plane] = kept
        scaled[plane] = kept * planes[plane + 4]


def step_kernel(last, extent, full, state, *refs):
    place = (state[2, 0:1, :], state[2, 1:2, :], *extent)
    count = state[2, 2, 0].astype(jnp.int32)
    if last:
        fractions, scale, scaled, final_velocity, displacement, potential_out = refs[:6]
    else:
        fractions_out, state_out, scale, scaled = refs[:4]
    pair_blocks, spread_blocks, own_columns, sums, density = refs[-5:]
    density[...] = jnp.zeros(density.shape, jnp.float32)
    sums[...] = jnp.zeros(sums.shape, jnp.float32)

    def block_of(column, index, lanes):
        block = full[column, index, :, lanes]
        if last:
            moved = fractions[column, index // 2, index % 2, :, lanes]
            return jnp.concatenate([block[0:3], moved[0:3], block[6:8]], 0)
        return block

    row_index = iota((8, LANES), 0)
    pair_count = jnp.int32(0)
    spread_counts = []
    for column in range(5):
        spread_count = jnp.int32(0)
        for side in range(3):
            shift = jnp.where(
                row_index == 0,
                4.0 * (column - 2),
                jnp.where(row_index == 1, 16.0 * (side - 1), 0.0),
            )
            for part in range(4):
                lanes = pl.ds((part % 2) * LANES, LANES)
                block = block_of(column, side * 2 + part // 2, lanes) + shift
                alive = block[6, 0] > 0.0
                spread_blocks[column, spread_count] = block
                spread_count = spread_count + alive.astype(jnp.int32)
                if column in (1, 2, 3):
                    pair_blocks[pair_count, 0:3, :] = KAPPA * (block[0:3] + block[3:6])
                    pair_blocks[pair_count, 3:4, :] = -block[6:7]
                    pair_blocks[pair_count, 4:5, :] = block[7:8]
                    pair_count = pair_count + alive.astype(jnp.int32)
        spread_blocks[column, spread_count] = jnp.zeros((8, LANES), jnp.float32)
        spread_counts.append(spread_count)
    pair_blocks[pair_count] = jnp.zeros((8, LANES), jnp.float32)

    own_halves = []
    for half in range(2):
        own = jnp.concatenate([block_of(2, 2 + half, pl.ds(i * LANES, LANES)) for i in range(2)], 1)
        own_halves.append(own)
        packed = jnp.concatenate(
            [KAPPA * (own[0:3] + own[3:6]), own[7:8], jnp.zeros((4, 256), jnp.float32)], 0
        )
        turned = jnp.transpose(packed)
        rows = pl.ds(half * 256, 256)
        for row in range(3):
            own_columns[row, rows, :] = jnp.broadcast_to(turned[:, row : row + 1], (256, LANES))
        own_columns[3, rows, :] = jnp.broadcast_to(-turned[:, 3:4], (256, LANES))

    def add_rows(index, carry):
        rows = pl.ds(index * I_ROWS, I_ROWS)
        own_x, own_y, own_z, own_s = (own_columns[row, rows, :] for row in range(4))

        def add_blocks(step, totals):
            for part in range(2):
                block = pair_blocks[step * 2 + part]
                x = own_x - block[0:1]
                y = own_y - block[1:2]
                z = own_z - block[2:3]
                spread = own_s - block[4:5]
                inverse = 1.0 / spread
                factor = jnp.exp2((x * x + y * y + z * z) * inverse)
                factor = (factor * block[3:4]) * inverse
                totals = (totals[0] + factor * x, totals[1] + factor * y, totals[2] + factor * z)
            return totals

        zero = jnp.zeros((I_ROWS, LANES), jnp.float32)
        totals = lax.fori_loop(0, (pair_count + 1) // 2, add_blocks, (zero, zero, zero))
        for axis in range(3):
            sums[axis, rows, :] = totals[axis]
        return carry

    lax.fori_loop(0, (count + I_ROWS - 1) // I_ROWS, add_rows, 0)

    depth = iota((256, 256), 0).astype(jnp.float32)
    height = iota((32, 256), 0).astype(jnp.float32) - 8.0
    rows = rows_inside(place, -8, 32)
    for column in range(5):
        planes = {0: (-4,), 4: (8,)}.get(column) or tuple(range(4 * column - 8, 4 * column - 3))

        def add_chunk(step, carry, column=column, planes=planes):
            chunk = jnp.concatenate(
                [spread_blocks[column, step * 2], spread_blocks[column, step * 2 + 1]], 1
            )
            fx, fy, fz = chunk[3:4], chunk[4:5], chunk[5:6]
            charge = chunk[6:7]
            selected = jnp.where(depth == chunk[2:3], 1.0, 0.0).astype(jnp.bfloat16)
            weight_y = jnp.where(
                height == chunk[1:2], 1.0 - fy, jnp.where(height == chunk[1:2] + 1.0, fy, 0.0)
            )
            weight_y = jnp.where(rows, weight_y, 0.0)
            where = pl.ds(planes[0] + 4, len(planes))
            for part, amount in enumerate((charge * (1.0 - fz), charge * fz)):
                weights = []
                for plane in planes:
                    weight_x = jnp.where(
                        chunk[0:1] == plane, 1.0 - fx, jnp.where(chunk[0:1] + 1.0 == plane, fx, 0.0)
                    )
                    weights.append((weight_x * amount * plane_inside(place, plane)) * weight_y)
                added = dot_exact(jnp.concatenate(weights, 0), selected, ((1,), (1,)))
                density[part, where] = density[part, where] + added.reshape(len(planes), 32, 256)
            return carry

        lax.fori_loop(0, (spread_counts[column] + 1) // 2, add_chunk, 0)

    if not last:
        inverse_scale(place, full, scale, scaled)
    matrix = band(BLUR)
    value = [planes_filtered(density[part], BLUR, 9) for part in range(2)]
    value = value[0] + pltpu.roll(value[1], 1, 2)
    value = depth_filtered(rows_filtered(value, BLUR), matrix, 2)
    residual = value * scale[...] - scaled[...]
    value = rows_filtered(planes_filtered(residual, BLUR, 5), BLUR)
    potential = depth_filtered(value, matrix, 2)
    if last:
        potential_out[...] = potential[0:4, 8:24]

    field = potential[:, 8:32].reshape(120, 256)
    both = split(jnp.concatenate([field, pltpu.roll(field, 255, 1)], 0), 2)
    ones = jnp.ones((8, LANES), jnp.bfloat16)
    height = iota((24, 256), 0).astype(jnp.float32)
    rows = rows_inside(place, 0, 24)
    edge = plane_inside(place, 4)
    for half in range(2):
        own = own_halves[half]
        gx, gy, gz, fx, fy, fz = (own[row : row + 1] for row in range(6))
        selected = jnp.where(depth == gz, 1.0, 0.0).astype(jnp.bfloat16)
        taken = dot(both[0], selected, ((1,), (0,))) + dot(both[1], selected, ((1,), (0,)))
        taken = taken.reshape(2, 5, 24, 256)
        lower, upper = (height == gy) & rows, (height == gy + 1.0) & rows
        weight_y = jnp.where(lower, 1.0 - fy, jnp.where(upper, fy, 0.0))
        slope_y = jnp.where(lower, -1.0, jnp.where(upper, 1.0, 0.0))
        mixed = [jnp.zeros((24, 256), jnp.float32) for _ in range(3)]
        for plane in range(5):
            slope_z = taken[1, plane] - taken[0, plane]
            product = taken[0, plane] + fz * slope_z
            lower, upper = gx == plane, gx + 1.0 == plane
            weight_x = jnp.where(lower, 1.0 - fx, jnp.where(upper, fx, 0.0))
            slope_x = jnp.where(lower, -1.0, jnp.where(upper, 1.0, 0.0))
            if plane == 4:
                weight_x, slope_x = weight_x * edge, slope_x * edge
            mixed[0] = mixed[0] + slope_x * product
            mixed[1] = mixed[1] + weight_x * product
            mixed[2] = mixed[2] + weight_x * slope_z
        gradient = (
            jnp.sum(mixed[0] * weight_y, 0, keepdims=True),
            jnp.sum(mixed[1] * slope_y, 0, keepdims=True),
            jnp.sum(mixed[2] * weight_y, 0, keepdims=True),
        )
        charge = own[6:7]
        values = state[half]
        mass, live = values[6:7], values[7:8]
        if not last:
            state_out[half, 6:8, :] = values[6:8]
            state_out[2] = state[2]
            fractions_out[half, 3:4, :] = jnp.zeros((1, 256), jnp.float32)
        for axis in range(3):
            parts = split(sums[axis, pl.ds(half * 256, 256), :], 2)
            pair = dot(ones, parts[0], ((1,), (1,))) + dot(ones, parts[1], ((1,), (1,)))
            force = charge * (pair[0:1] * (1.0 / KAPPA) - gradient[axis])
            velocity = values[axis : axis + 1] + TIME_STEP * force / mass
            moved = values[axis + 3 : axis + 4] + TIME_STEP * velocity
            if last:
                lanes = pl.ds(half * 256, 256)
                final_velocity[axis, 0, :, lanes] = velocity * live
                displacement[axis, 0, :, lanes] = moved * live
            else:
                state_out[half, axis : axis + 1, :] = velocity
                state_out[half, axis + 3 : axis + 4, :] = moved
                fractions_out[half, axis : axis + 1, :] = (
                    own[axis + 3 : axis + 4] + TIME_STEP * velocity
                )


SMEM = pl.BlockSpec(memory_space=pltpu.SMEM)
VMEM = pl.BlockSpec(memory_space=pltpu.VMEM)
HBM = pl.BlockSpec(memory_space=pltpu.HBM)


def shape(*dims):
    return jax.ShapeDtypeStruct(dims, jnp.float32)


def links():
    chips = lax.axis_size("cells") // 2
    groups = lax.axis_size("grp")

    def coloured(count, first):
        pairs = []
        for left in range(first, count - 1, 2):
            pairs += [(left, left + 1), (left + 1, left)]
        return pairs

    def doubled(pairs):
        return [(2 * a + core, 2 * b + core) for a, b in pairs for core in range(2)]

    return {
        "odd": ("cells", doubled(coloured(chips, 1))),
        "even": ("cells", doubled(coloured(chips, 0))),
        "rows_even": ("grp", coloured(groups, 0)),
        "rows_odd": ("grp", coloured(groups, 1)),
        "pair": ("cells", [(i, i ^ 1) for i in range(2 * chips)]),
    }


def spread_out(own, rows, groups, flags):
    even_chip, even_row, first_core = flags

    def send(value, link):
        return lax.ppermute(value, *groups[link])

    odd = send(own, "odd")
    even = send(own, "even")
    left = jnp.where(even_chip, odd, even)
    right = jnp.where(even_chip, even, odd)
    columns = jnp.stack([own, left, right])
    from_even = send(rows(columns, even_row), "rows_even")
    from_odd = send(rows(columns, ~even_row), "rows_odd")
    above = jnp.where(even_row, from_even, from_odd)
    below = jnp.where(even_row, from_odd, from_even)
    return columns, below, above, functools.partial(send, link="pair")


def finish(full, send, first_core):
    chosen = jnp.where(first_core, full[2], full[1])
    got = send(jnp.stack([full[0], chosen]))
    minus = jnp.where(first_core, got[1], got[0])
    plus = jnp.where(first_core, got[0], got[1])
    return jnp.stack([full[1], minus, full[0], plus, full[2]])


def per_device(fraction, velocity, anchor, atom_types, counts, type_table, target):
    cells, groups_count = lax.axis_size("cells"), lax.axis_size("grp")
    cell, group = lax.axis_index("cells"), lax.axis_index("grp")
    groups = links()
    flags = ((cell // 2) % 2 == 0, group % 2 == 0, cell % 2 == 0)
    extent = (4.0 * cells, 16.0 * groups_count)

    own, state = pl.pallas_call(
        prep_kernel,
        out_shape=(shape(10, 8, 256), shape(3, 8, 256)),
        in_specs=[SMEM, SMEM, HBM, HBM, HBM, HBM, HBM],
        out_specs=(VMEM, VMEM),
        scratch_shapes=[
            pltpu.VMEM(fraction.shape, jnp.float32),
            pltpu.VMEM(velocity.shape, jnp.float32),
            pltpu.VMEM(anchor.shape, jnp.int32),
            pltpu.VMEM(atom_types.shape, jnp.int32),
            pltpu.VMEM(target.shape, jnp.float32),
            pltpu.SemaphoreType.DMA((5,)),
        ],
        name="prep",
    )(counts, type_table, fraction, velocity, anchor, atom_types, target)

    def rows_first(columns, upper):
        fields = columns[:, 2:].reshape(3, 4, 2, 8, 256)
        return jnp.concatenate(
            [columns[:, :2], jnp.where(upper, fields[:, :, 1], fields[:, :, 0])], 1
        )

    columns, below, above, send = spread_out(own, rows_first, groups, flags)
    full = jnp.concatenate(
        [
            jnp.stack([below[:, :2], columns[:, :2], above[:, :2]], 1).reshape(3, 6, 8, 256),
            jnp.concatenate(
                [
                    below[:, 2:, None],
                    columns[:, 2:].reshape(3, 4, 2, 8, 256),
                    above[:, 2:, None],
                ],
                2,
            ).reshape(3, 16, 8, 256),
        ],
        1,
    )
    full = finish(full, send, flags[2])

    field = shape(9, 32, 256)
    scratch = [
        pltpu.VMEM((38, 8, LANES), jnp.float32),
        pltpu.VMEM((5, 14, 8, LANES), jnp.float32),
        pltpu.VMEM((4, 512, LANES), jnp.float32),
        pltpu.VMEM((3, 512, LANES), jnp.float32),
        pltpu.VMEM((2, 13, 32, 256), jnp.float32),
    ]
    fractions, state, scale, scaled = pl.pallas_call(
        functools.partial(step_kernel, False, extent),
        out_shape=(shape(2, 4, 256), shape(3, 8, 256), field, field),
        in_specs=[VMEM, VMEM],
        out_specs=(VMEM,) * 4,
        scratch_shapes=scratch,
        name="step",
        compiler_params=pltpu.CompilerParams(vmem_limit_bytes=24 << 20),
    )(full, state)

    columns, below, above, send = spread_out(fractions, lambda c, upper: c, groups, flags)
    moved = finish(jnp.stack([below, columns, above], 1), send, flags[2])
    return pl.pallas_call(
        functools.partial(step_kernel, True, extent),
        out_shape=(shape(*velocity.shape), shape(*velocity.shape), shape(*target.shape)),
        in_specs=[VMEM] * 5,
        out_specs=(VMEM,) * 3,
        scratch_shapes=scratch,
        name="step_last",
        compiler_params=pltpu.CompilerParams(vmem_limit_bytes=24 << 20),
    )(full, state, moved, scale, scaled)


def solution(mesh):
    placed = (
        P(None, "cells", "grp", None),
        P(None, "cells", "grp", None),
        P(None, "cells", "grp", None),
        P("cells", "grp", None),
        P("cells", "grp"),
        P(),
        P("cells", "grp", None),
    )
    return jax.shard_map(
        per_device,
        mesh=mesh,
        in_specs=placed,
        out_specs=(
            P(None, "cells", "grp", None),
            P(None, "cells", "grp", None),
            P("cells", "grp", None),
        ),
        check_vma=False,
    )
```

time: 104 us -> 90.3 us (0.87)
  the two profiles are of different devices: /device:TPU:72 before, /device:TPU:87 now
where the time goes in v2:
time: 90.3 us; the launch traced here: 90.2 us
  starting transfers between devices  36.1 us (40%)
  Pallas kernels  32.9 us (36%)
  waiting for transfers between devices  18.4 us (20%)
  between operations  1.64 us (2%)
    ppermute x10, starting transfers between devices, send(): return lax.ppermute(value, *groups[link])  36.1 us
    ppermute x10, waiting for transfers between devices, send(): return lax.ppermute(value, *groups[link])  18.4 us
    pallas_call x1, Pallas kernels, per_device(): pl.pallas_call(functools.partial(step_kernel, False, extent), out_shape=(...  15.4 us
    pallas_call x1, Pallas kernels, per_device(): pl.pallas_call(functools.partial(step_kernel, True, extent), out_shape=(s...  15.3 us
    pallas_call x1, Pallas kernels, per_device(): pl.pallas_call(prep_kernel, out_shape=(shape(10, 8, 256), shape(3, 8, 256...  2.29 us
  transfers between devices with their start and end apart: 10, of which 8 were waited for; matrix products, arithmetic and copies ran while one was open for 0% of the time, Pallas kernels for 0%

profile of v2, /device:TPU:87, one launch (start us, length us, event | category | flops | bytes accessed | tf_op | source)
XLA Modules:
  0.0 90.2 jit_solution(7011562496024044144)
XLA Ops:
  1.3 2.3 %prep.1 = (f32[10,8,256]{2,1,0:T(8,128)}, f32[3,8,256]{2,1,0:T(8,128)}) custom-call(s32[1,1]{1,0:T(1,128)S(6)} %copy.27.counts, f32[3,8]{1,0:T(4,128)} %table.1, f32[3,1,1,512]{3,2,1,0:T(1,128)} %fraction_in.1, f32[3,1,1,512]{3,2,1,0:T(1,128)} %velocity_in.1, s32[3,1,1,512]{3,2,1,0:T(1,128)} %anchor_in.1, s32[1,1,512]{2,1,0:T(1,128)} %kinds_in.1, ...), custom_call_target="tpu_custom_call" | custom-call | tf_op jit(solution)/shard_map/prep/pallas_call | solution.py:396
  3.6 2.5 %collective-permute-start.1 = (f32[10,8,256]{2,1,0:T(8,128)}, f32[10,8,256]{2,1,0:T(8,128)S(1)}, u32[]{:S(2)}, u32[]{:S(2)}) collective-permute-start(f32[10,8,256]{2,1,0:T(8,128)} %get-tuple-element.9), channel_id=1, source_target_pairs={{0,8},{4,12},{8,0},{12,4},{16,24},{20,28},{24,16},{28,20},{32,40},... | collective-permute-start | bytes 245768 | tf_op jit(solution)/shard_map/ppermute | solution.py:367
  6.0 10.3 %collective-permute-start = (f32[10,8,256]{2,1,0:T(8,128)}, f32[10,8,256]{2,1,0:T(8,128)S(1)}, u32[]{:S(2)}, u32[]{:S(2)}) collective-permute-start(f32[10,8,256]{2,1,0:T(8,128)} %get-tuple-element.9), channel_id=1, source_target_pairs={{8,16},{12,20},{16,8},{20,12},{24,32},{28,36},{32,24},{36,28},{40,... | collective-permute-start | bytes 245768 | tf_op jit(solution)/shard_map/ppermute | solution.py:367
  16.4 0.0 copy-start.1
  16.4 0.0 collective-permute-done.1
  16.4 2.0 %collective-permute-done = f32[10,8,256]{2,1,0:T(8,128)S(1)} collective-permute-done((f32[10,8,256]{2,1,0:T(8,128)}, f32[10,8,256]{2,1,0:T(8,128)S(1)}, u32[]{:S(2)}, u32[]{:S(2)}) %collective-permute-start) | collective-permute-done | bytes 81952 | tf_op jit(solution)/shard_map/ppermute | solution.py:367
  18.4 0.0 copy-done.1
  18.5 6.0 %collective-permute-start.2 = (f32[3,6,8,256]{3,2,1,0:T(8,128)S(1)}, f32[3,6,8,256]{3,2,1,0:T(8,128)S(1)}, u32[]{:S(2)}, u32[]{:S(2)}) collective-permute-start(f32[3,6,8,256]{3,2,1,0:T(8,128)S(1)} %get-tuple-element.29), channel_id=1, source_target_pairs={{1,2},{2,1},{5,6},{6,5},{9,10},{10,9},{13,14},{14,13},{17,18},{18,... | collective-permute-start | bytes 442376 | tf_op jit(solution)/shard_map/ppermute | solution.py:367
  24.5 1.9 %collective-permute-start.3 = (f32[3,6,8,256]{3,2,1,0:T(8,128)S(1)}, f32[3,6,8,256]{3,2,1,0:T(8,128)S(1)}, u32[]{:S(2)}, u32[]{:S(2)}) collective-permute-start(f32[3,6,8,256]{3,2,1,0:T(8,128)S(1)} %get-tuple-element.30), channel_id=1, source_target_pairs={{0,1},{1,0},{2,3},{3,2},{4,5},{5,4},{6,7},{7,6},{8,9},{9,8},{10,11... | collective-permute-start | bytes 442376 | tf_op jit(solution)/shard_map/ppermute | solution.py:367
  26.5 1.1 %collective-permute-done.2 = f32[3,6,8,256]{3,2,1,0:T(8,128)S(1)} collective-permute-done((f32[3,6,8,256]{3,2,1,0:T(8,128)S(1)}, f32[3,6,8,256]{3,2,1,0:T(8,128)S(1)}, u32[]{:S(2)}, u32[]{:S(2)}) %collective-permute-start.2) | collective-permute-done | bytes 147488 | tf_op jit(solution)/shard_map/ppermute | solution.py:367
  27.5 2.9 %collective-permute-done.3 = f32[3,6,8,256]{3,2,1,0:T(8,128)S(1)} collective-permute-done((f32[3,6,8,256]{3,2,1,0:T(8,128)S(1)}, f32[3,6,8,256]{3,2,1,0:T(8,128)S(1)}, u32[]{:S(2)}, u32[]{:S(2)}) %collective-permute-start.3) | collective-permute-done | bytes 147488 | tf_op jit(solution)/shard_map/ppermute | solution.py:367
  30.6 4.5 %collective-permute-start.4 = (f32[2,22,8,256]{3,2,1,0:T(8,128)S(1)}, f32[2,22,8,256]{3,2,1,0:T(8,128)S(1)}, u32[]{:S(2)}, u32[]{:S(2)}) collective-permute-start(f32[2,22,8,256]{3,2,1,0:T(8,128)S(1)} %pad_maximum_fusion.1), channel_id=1, source_target_pairs={{0,4},{4,0},{8,12},{12,8},{16,20},{20,16},{24,28},{28,24},{32,36},... | collective-permute-start | bytes 1081352 | tf_op jit(solution)/shard_map/ppermute | solution.py:367
  35.2 1.3 %collective-permute-done.4 = f32[2,22,8,256]{3,2,1,0:T(8,128)S(1)} collective-permute-done((f32[2,22,8,256]{3,2,1,0:T(8,128)S(1)}, f32[2,22,8,256]{3,2,1,0:T(8,128)S(1)}, u32[]{:S(2)}, u32[]{:S(2)}) %collective-permute-start.4) | collective-permute-done | bytes 360480 | tf_op jit(solution)/shard_map/ppermute | solution.py:367
  36.5 0.0 copy-start
  36.6 0.7 copy-done
  37.3 15.4 %step.1 = (f32[2,4,256]{2,1,0:T(4,128)S(1)}, f32[3,8,256]{2,1,0:T(8,128)S(1)}, f32[9,32,256]{2,1,0:T(8,128)S(1)}, f32[9,32,256]{2,1,0:T(8,128)S(1)}) custom-call(f32[5,22,8,256]{3,2,1,0:T(8,128)S(1)} %constant_dynamic-update-slice_fusion.full, f32[3,8,256]{2,1,0:T(8,128)S(1)} %copy-done), custom_call_target="tpu_custom_call" | custom-call | tf_op jit(solution)/shard_map/step/pallas_call | solution.py:443
  52.7 1.9 %collective-permute-start.6 = (f32[2,4,256]{2,1,0:T(4,128)S(1)}, f32[2,4,256]{2,1,0:T(4,128)S(1)}, u32[]{:S(2)}, u32[]{:S(2)}) collective-permute-start(f32[2,4,256]{2,1,0:T(4,128)S(1)} %get-tuple-element.12), channel_id=1, source_target_pairs={{0,8},{4,12},{8,0},{12,4},{16,24},{20,28},{24,16},{28,20},{32,40},... | collective-permute-start | bytes 24584 | tf_op jit(solution)/shard_map/ppermute | solution.py:367
  54.6 3.1 %collective-permute-start.5 = (f32[2,4,256]{2,1,0:T(4,128)S(1)}, f32[2,4,256]{2,1,0:T(4,128)S(1)}, u32[]{:S(2)}, u32[]{:S(2)}) collective-permute-start(f32[2,4,256]{2,1,0:T(4,128)S(1)} %get-tuple-element.12), channel_id=1, source_target_pairs={{8,16},{12,20},{16,8},{20,12},{24,32},{28,36},{32,24},{36,28},{40,... | collective-permute-start | bytes 24584 | tf_op jit(solution)/shard_map/ppermute | solution.py:367
  57.7 0.0 collective-permute-done.6
  57.7 7.3 %collective-permute-done.5 = f32[2,4,256]{2,1,0:T(4,128)S(1)} collective-permute-done((f32[2,4,256]{2,1,0:T(4,128)S(1)}, f32[2,4,256]{2,1,0:T(4,128)S(1)}, u32[]{:S(2)}, u32[]{:S(2)}) %collective-permute-start.5) | collective-permute-done | bytes 8224 | tf_op jit(solution)/shard_map/ppermute | solution.py:367
  65.1 1.9 %collective-permute-start.8 = (f32[3,2,4,256]{3,2,1,0:T(4,128)S(1)}, f32[3,2,4,256]{3,2,1,0:T(4,128)S(1)}, u32[]{:S(2)}, u32[]{:S(2)}) collective-permute-start(f32[3,2,4,256]{3,2,1,0:T(4,128)S(1)} %get-tuple-element.32), channel_id=1, source_target_pairs={{0,1},{1,0},{2,3},{3,2},{4,5},{5,4},{6,7},{7,6},{8,9},{9,8},{10,11... | collective-permute-start | bytes 73736 | tf_op jit(solution)/shard_map/ppermute | solution.py:367
  67.0 1.9 %collective-permute-start.7 = (f32[3,2,4,256]{3,2,1,0:T(4,128)S(1)}, f32[3,2,4,256]{3,2,1,0:T(4,128)S(1)}, u32[]{:S(2)}, u32[]{:S(2)}) collective-permute-start(f32[3,2,4,256]{3,2,1,0:T(4,128)S(1)} %get-tuple-element.32), channel_id=1, source_target_pairs={{1,2},{2,1},{5,6},{6,5},{9,10},{10,9},{13,14},{14,13},{17,18},{18,... | collective-permute-start | bytes 73736 | tf_op jit(solution)/shard_map/ppermute | solution.py:367
  69.0 0.7 collective-permute-done.8
  69.7 1.9 %collective-permute-done.7 = f32[3,2,4,256]{3,2,1,0:T(4,128)S(1)} collective-permute-done((f32[3,2,4,256]{3,2,1,0:T(4,128)S(1)}, f32[3,2,4,256]{3,2,1,0:T(4,128)S(1)}, u32[]{:S(2)}, u32[]{:S(2)}) %collective-permute-start.7) | collective-permute-done | bytes 24608 | tf_op jit(solution)/shard_map/ppermute | solution.py:367
  71.7 1.9 %collective-permute-start.9 = (f32[2,3,2,4,256]{4,3,2,1,0:T(4,128)S(1)}, f32[2,3,2,4,256]{4,3,2,1,0:T(4,128)S(1)}, u32[]{:S(2)}, u32[]{:S(2)}) collective-permute-start(f32[2,3,2,4,256]{4,3,2,1,0:T(4,128)S(1)} %pad_maximum_fusion.10), channel_id=1, source_target_pairs={{0,4},{4,0},{8,12},{12,8},{16,20},{20,16},{24,28},{28,24},{32,36},... | collective-permute-start | bytes 147464 | tf_op jit(solution)/shard_map/ppermute | solution.py:367
  73.6 1.2 %collective-permute-done.9 = f32[2,3,2,4,256]{4,3,2,1,0:T(4,128)S(1)} collective-permute-done((f32[2,3,2,4,256]{4,3,2,1,0:T(4,128)S(1)}, f32[2,3,2,4,256]{4,3,2,1,0:T(4,128)S(1)}, u32[]{:S(2)}, u32[]{:S(2)}) %collective-permute-start.9) | collective-permute-done | bytes 49184 | tf_op jit(solution)/shard_map/ppermute | solution.py:367
  74.9 15.3 %step_last.1 = (f32[3,1,1,512]{3,2,1,0:T(1,128)}, f32[3,1,1,512]{3,2,1,0:T(1,128)}, f32[4,16,256]{2,1,0:T(8,128)}) custom-call(f32[5,22,8,256]{3,2,1,0:T(8,128)S(1)} %constant_dynamic-update-slice_fusion.full, f32[3,8,256]{2,1,0:T(8,128)S(1)} %get-tuple-element.11.state, f32[5,3,2,4,256]{4,3,2,1,0:T(4,128)S(1)} %constant_dynamic-update-slice_fusion.3.refs_0_, ...), custom_call_target="tpu_custom_call" | custom-call | tf_op jit(solution)/shard_map/step_last/pallas_call | solution.py:455
  (28 shorter events, 0.5 us)
Async XLA Ops:
  3.6 12.8 %collective-permute-start.1 = (f32[10,8,256]{2,1,0:T(8,128)}, f32[10,8,256]{2,1,0:T(8,128)S(1)}, u32[]{:S(2)}, u32[]{:S(2)}) collective-permute-start(f32[10,8,256]{2,1,0:T(8,128)} %get-tuple-element.9), channel_id=1, source_target_pairs={{0,8},{4,12},{8,0},{12,4},{16,24},{20,28},{24,16},{28,20},{32,40},... | collective-permute-start | bytes 245768 | tf_op jit(solution)/shard_map/ppermute | solution.py:367
  6.0 12.3 %collective-permute-start = (f32[10,8,256]{2,1,0:T(8,128)}, f32[10,8,256]{2,1,0:T(8,128)S(1)}, u32[]{:S(2)}, u32[]{:S(2)}) collective-permute-start(f32[10,8,256]{2,1,0:T(8,128)} %get-tuple-element.9), channel_id=1, source_target_pairs={{8,16},{12,20},{16,8},{20,12},{24,32},{28,36},{32,24},{36,28},{40,... | collective-permute-start | bytes 245768 | tf_op jit(solution)/shard_map/ppermute | solution.py:367
  16.4 2.0 %copy-start.1 = (f32[10,8,256]{2,1,0:T(8,128)S(1)}, f32[10,8,256]{2,1,0:T(8,128)}, u32[]{:S(2)}) copy-start(f32[10,8,256]{2,1,0:T(8,128)} %get-tuple-element.9) | copy-start | bytes 245764
  18.5 9.0 %collective-permute-start.2 = (f32[3,6,8,256]{3,2,1,0:T(8,128)S(1)}, f32[3,6,8,256]{3,2,1,0:T(8,128)S(1)}, u32[]{:S(2)}, u32[]{:S(2)}) collective-permute-start(f32[3,6,8,256]{3,2,1,0:T(8,128)S(1)} %get-tuple-element.29), channel_id=1, source_target_pairs={{1,2},{2,1},{5,6},{6,5},{9,10},{10,9},{13,14},{14,13},{17,18},{18,... | collective-permute-start | bytes 442376 | tf_op jit(solution)/shard_map/ppermute | solution.py:367
  24.5 5.9 %collective-permute-start.3 = (f32[3,6,8,256]{3,2,1,0:T(8,128)S(1)}, f32[3,6,8,256]{3,2,1,0:T(8,128)S(1)}, u32[]{:S(2)}, u32[]{:S(2)}) collective-permute-start(f32[3,6,8,256]{3,2,1,0:T(8,128)S(1)} %get-tuple-element.30), channel_id=1, source_target_pairs={{0,1},{1,0},{2,3},{3,2},{4,5},{5,4},{6,7},{7,6},{8,9},{9,8},{10,11... | collective-permute-start | bytes 442376 | tf_op jit(solution)/shard_map/ppermute | solution.py:367
  30.6 5.8 %collective-permute-start.4 = (f32[2,22,8,256]{3,2,1,0:T(8,128)S(1)}, f32[2,22,8,256]{3,2,1,0:T(8,128)S(1)}, u32[]{:S(2)}, u32[]{:S(2)}) collective-permute-start(f32[2,22,8,256]{3,2,1,0:T(8,128)S(1)} %pad_maximum_fusion.1), channel_id=1, source_target_pairs={{0,4},{4,0},{8,12},{12,8},{16,20},{20,16},{24,28},{28,24},{32,36},... | collective-permute-start | bytes 1081352 | tf_op jit(solution)/shard_map/ppermute | solution.py:367
  36.5 0.7 copy-start
  52.7 5.1 %collective-permute-start.6 = (f32[2,4,256]{2,1,0:T(4,128)S(1)}, f32[2,4,256]{2,1,0:T(4,128)S(1)}, u32[]{:S(2)}, u32[]{:S(2)}) collective-permute-start(f32[2,4,256]{2,1,0:T(4,128)S(1)} %get-tuple-element.12), channel_id=1, source_target_pairs={{0,8},{4,12},{8,0},{12,4},{16,24},{20,28},{24,16},{28,20},{32,40},... | collective-permute-start | bytes 24584 | tf_op jit(solution)/shard_map/ppermute | solution.py:367
  54.6 10.5 %collective-permute-start.5 = (f32[2,4,256]{2,1,0:T(4,128)S(1)}, f32[2,4,256]{2,1,0:T(4,128)S(1)}, u32[]{:S(2)}, u32[]{:S(2)}) collective-permute-start(f32[2,4,256]{2,1,0:T(4,128)S(1)} %get-tuple-element.12), channel_id=1, source_target_pairs={{8,16},{12,20},{16,8},{20,12},{24,32},{28,36},{32,24},{36,28},{40,... | collective-permute-start | bytes 24584 | tf_op jit(solution)/shard_map/ppermute | solution.py:367
  65.1 4.6 %collective-permute-start.8 = (f32[3,2,4,256]{3,2,1,0:T(4,128)S(1)}, f32[3,2,4,256]{3,2,1,0:T(4,128)S(1)}, u32[]{:S(2)}, u32[]{:S(2)}) collective-permute-start(f32[3,2,4,256]{3,2,1,0:T(4,128)S(1)} %get-tuple-element.32), channel_id=1, source_target_pairs={{0,1},{1,0},{2,3},{3,2},{4,5},{5,4},{6,7},{7,6},{8,9},{9,8},{10,11... | collective-permute-start | bytes 73736 | tf_op jit(solution)/shard_map/ppermute | solution.py:367
  67.0 4.6 %collective-permute-start.7 = (f32[3,2,4,256]{3,2,1,0:T(4,128)S(1)}, f32[3,2,4,256]{3,2,1,0:T(4,128)S(1)}, u32[]{:S(2)}, u32[]{:S(2)}) collective-permute-start(f32[3,2,4,256]{3,2,1,0:T(4,128)S(1)} %get-tuple-element.32), channel_id=1, source_target_pairs={{1,2},{2,1},{5,6},{6,5},{9,10},{10,9},{13,14},{14,13},{17,18},{18,... | collective-permute-start | bytes 73736 | tf_op jit(solution)/shard_map/ppermute | solution.py:367
  71.7 3.1 %collective-permute-start.9 = (f32[2,3,2,4,256]{4,3,2,1,0:T(4,128)S(1)}, f32[2,3,2,4,256]{4,3,2,1,0:T(4,128)S(1)}, u32[]{:S(2)}, u32[]{:S(2)}) collective-permute-start(f32[2,3,2,4,256]{4,3,2,1,0:T(4,128)S(1)} %pad_maximum_fusion.10), channel_id=1, source_target_pairs={{0,4},{4,0},{8,12},{12,8},{16,20},{20,16},{24,28},{28,24},{32,36},... | collective-permute-start | bytes 147464 | tf_op jit(solution)/shard_map/ppermute | solution.py:367

commit v3 on v2

--- a/solution.py
+++ b/solution.py
@@ -7,7 +7,7 @@
 from jax.experimental.pallas import tpu as pltpu
 from jax.sharding import PartitionSpec as P
 
-STEPS = 2
+
 EPSILON = 1e-06
 TIME_STEP = 0.5
 BLUR = (1.0 / 16.0, 4.0 / 16.0, 6.0 / 16.0, 4.0 / 16.0, 1.0 / 16.0)
@@ -31,10 +31,11 @@
 
 
 def dot_exact(a, b, dims, pieces=2):
-    total = None
-    for part in reversed(split(a, pieces)):
-        product = dot(part, b, dims)
-        total = product if total is None else total + product
+    count = a.shape[0]
+    product = dot(jnp.concatenate(split(a, pieces), 0), b, dims)
+    total = product[count * (pieces - 1) :]
+    for piece in reversed(range(pieces - 1)):
+        total = total + product[count * piece : count * (piece + 1)]
     return total
 
 
@@ -90,21 +91,11 @@
     return (position >= 0.0) & (position < place[3])
 
 
-def prep_kernel(
-    counts, table, fraction_in, velocity_in, anchor_in, kinds_in, target_in, sent, state,
-    fraction, velocity, anchor, kinds, target, sems,
-):
-    pairs = ((fraction_in, fraction), (velocity_in, velocity), (anchor_in, anchor))
-    pairs += ((kinds_in, kinds), (target_in, target))
-    copies = [pltpu.make_async_copy(*pair, sems.at[i]) for i, pair in enumerate(pairs)]
-    for copy in copies:
-        copy.start()
+def prep_kernel(counts, table, fraction, velocity, anchor, kinds, target, sent, state):
     info = (lax.axis_index("cells"), lax.axis_index("grp"), counts[0, 0])
     for row, value in enumerate(info):
         state[2, row : row + 1, :] = jnp.full((1, 256), value, jnp.int32).astype(jnp.float32)
     state[2, 3:8, :] = jnp.zeros((5, 256), jnp.float32)
-    for copy in copies:
-        copy.wait()
     for half in range(2):
         lanes = pl.ds(half * 256, 256)
         kind = kinds[0, :, lanes]
@@ -156,6 +147,7 @@
         fractions_out, state_out, scale, scaled = refs[:4]
     pair_blocks, spread_blocks, own_columns, sums, density = refs[-5:]
     density[...] = jnp.zeros(density.shape, jnp.float32)
+    spread_blocks[...] = jnp.zeros(spread_blocks.shape, jnp.float32)
     sums[...] = jnp.zeros(sums.shape, jnp.float32)
 
     def block_of(column, index, lanes):
@@ -187,7 +179,6 @@
                     pair_blocks[pair_count, 3:4, :] = -block[6:7]
                     pair_blocks[pair_count, 4:5, :] = block[7:8]
                     pair_count = pair_count + alive.astype(jnp.int32)
-        spread_blocks[column, spread_count] = jnp.zeros((8, LANES), jnp.float32)
         spread_counts.append(spread_count)
     pair_blocks[pair_count] = jnp.zeros((8, LANES), jnp.float32)
 
@@ -232,33 +223,55 @@
     depth = iota((256, 256), 0).astype(jnp.float32)
     height = iota((32, 256), 0).astype(jnp.float32) - 8.0
     rows = rows_inside(place, -8, 32)
-    for column in range(5):
-        planes = {0: (-4,), 4: (8,)}.get(column) or tuple(range(4 * column - 8, 4 * column - 3))
-
-        def add_chunk(step, carry, column=column, planes=planes):
-            chunk = jnp.concatenate(
-                [spread_blocks[column, step * 2], spread_blocks[column, step * 2 + 1]], 1
+
+    def add_chunk(step, column, planes):
+        chunk = jnp.concatenate(
+            [spread_blocks[column, step * 2], spread_blocks[column, step * 2 + 1]], 1
+        )
+        fx, fy, fz = chunk[3:4], chunk[4:5], chunk[5:6]
+        charge = chunk[6:7]
+        selected = jnp.where(depth == chunk[2:3], 1.0, 0.0).astype(jnp.bfloat16)
+        weight_y = jnp.where(
+            height == chunk[1:2], 1.0 - fy, jnp.where(height == chunk[1:2] + 1.0, fy, 0.0)
+        )
+        weight_y = jnp.where(rows, weight_y, 0.0)
+        weights = []
+        for amount in (charge * (1.0 - fz), charge * fz):
+            for plane in planes:
+                weight_x = jnp.where(
+                    chunk[0:1] == plane, 1.0 - fx, jnp.where(chunk[0:1] + 1.0 == plane, fx, 0.0)
+                )
+                weights.append((weight_x * amount * plane_inside(place, plane)) * weight_y)
+        added = dot_exact(jnp.concatenate(weights, 0), selected, ((1,), (1,)))
+        return added.reshape(2, len(planes), 32, 256)
+
+    def add_chunks(step, carry):
+        added = [
+            add_chunk(step, column, planes)
+            for column, planes in enumerate(
+                ((-4,), range(-4, 1), range(0, 5), range(4, 9), (8,))
             )
-            fx, fy, fz = chunk[3:4], chunk[4:5], chunk[5:6]
-            charge = chunk[6:7]
-            selected = jnp.where(depth == chunk[2:3], 1.0, 0.0).astype(jnp.bfloat16)
-            weight_y = jnp.where(
-                height == chunk[1:2], 1.0 - fy, jnp.where(height == chunk[1:2] + 1.0, fy, 0.0)
+        ]
+        for part in range(2):
+            far_left, left, own, right, far_right = (added[column][part] for column in range(5))
+            pieces = (
+                far_left + left[0:1],
+                left[1:4],
+                left[4:5] + own[0:1],
+                own[1:4],
+                own[4:5] + right[0:1],
+                right[1:4],
+                right[4:5] + far_right,
             )
-            weight_y = jnp.where(rows, weight_y, 0.0)
-            where = pl.ds(planes[0] + 4, len(planes))
-            for part, amount in enumerate((charge * (1.0 - fz), charge * fz)):
-                weights = []
-                for plane in planes:
-                    weight_x = jnp.where(
-                        chunk[0:1] == plane, 1.0 - fx, jnp.where(chunk[0:1] + 1.0 == plane, fx, 0.0)
-                    )
-                    weights.append((weight_x * amount * plane_inside(place, plane)) * weight_y)
-                added = dot_exact(jnp.concatenate(weights, 0), selected, ((1,), (1,)))
-                density[part, where] = density[part, where] + added.reshape(len(planes), 32, 256)
-            return carry
-
-        lax.fori_loop(0, (spread_counts[column] + 1) // 2, add_chunk, 0)
+            start = 0
+            for piece in pieces:
+                where = pl.ds(start, piece.shape[0])
+                density[part, where] = density[part, where] + piece
+                start += piece.shape[0]
+        return carry
+
+    longest = functools.reduce(jnp.maximum, spread_counts)
+    lax.fori_loop(0, (longest + 1) // 2, add_chunks, 0)
 
     if not last:
         inverse_scale(place, full, scale, scaled)
@@ -273,7 +286,7 @@
         potential_out[...] = potential[0:4, 8:24]
 
     field = potential[:, 8:32].reshape(120, 256)
-    both = split(jnp.concatenate([field, pltpu.roll(field, 255, 1)], 0), 2)
+    both = jnp.concatenate([field, pltpu.roll(field, 255, 1)], 0)
     ones = jnp.ones((8, LANES), jnp.bfloat16)
     height = iota((24, 256), 0).astype(jnp.float32)
     rows = rows_inside(place, 0, 24)
@@ -282,8 +295,7 @@
         own = own_halves[half]
         gx, gy, gz, fx, fy, fz = (own[row : row + 1] for row in range(6))
         selected = jnp.where(depth == gz, 1.0, 0.0).astype(jnp.bfloat16)
-        taken = dot(both[0], selected, ((1,), (0,))) + dot(both[1], selected, ((1,), (0,)))
-        taken = taken.reshape(2, 5, 24, 256)
+        taken = dot_exact(both, selected, ((1,), (0,))).reshape(2, 5, 24, 256)
         lower, upper = (height == gy) & rows, (height == gy + 1.0) & rows
         weight_y = jnp.where(lower, 1.0 - fy, jnp.where(upper, fy, 0.0))
         slope_y = jnp.where(lower, -1.0, jnp.where(upper, 1.0, 0.0))
@@ -331,7 +343,6 @@
 
 SMEM = pl.BlockSpec(memory_space=pltpu.SMEM)
 VMEM = pl.BlockSpec(memory_space=pltpu.VMEM)
-HBM = pl.BlockSpec(memory_space=pltpu.HBM)
 
 
 def shape(*dims):
@@ -361,7 +372,7 @@
 
 
 def spread_out(own, rows, groups, flags):
-    even_chip, even_row, first_core = flags
+    even_chip, even_row, _ = flags
 
     def send(value, link):
         return lax.ppermute(value, *groups[link])
@@ -396,18 +407,12 @@
     own, state = pl.pallas_call(
         prep_kernel,
         out_shape=(shape(10, 8, 256), shape(3, 8, 256)),
-        in_specs=[SMEM, SMEM, HBM, HBM, HBM, HBM, HBM],
+        in_specs=[SMEM, SMEM, VMEM, VMEM, VMEM, VMEM, VMEM],
         out_specs=(VMEM, VMEM),
-        scratch_shapes=[
-            pltpu.VMEM(fraction.shape, jnp.float32),
-            pltpu.VMEM(velocity.shape, jnp.float32),
-            pltpu.VMEM(anchor.shape, jnp.int32),
-            pltpu.VMEM(atom_types.shape, jnp.int32),
-            pltpu.VMEM(target.shape, jnp.float32),
-            pltpu.SemaphoreType.DMA((5,)),
-        ],
         name="prep",
     )(counts, type_table, fraction, velocity, anchor, atom_types, target)
+
+    state = state + jnp.where(cell < 0, 1.0, 0.0)
 
     def rows_first(columns, upper):
         fields = columns[:, 2:].reshape(3, 4, 2, 8, 256)

time: 90.3 us -> 83.3 us (0.922)
  the two profiles are of different devices: /device:TPU:87 before, /device:TPU:342 now
where the time goes in v3:
time: 83.3 us; the launch traced here: 82.8 us
  waiting for transfers between devices  34.3 us (41%)
  Pallas kernels  24.4 us (29%)
  starting transfers between devices  22.1 us (27%)
  between operations  1.63 us (2%)
    ppermute x10, waiting for transfers between devices, send(): return lax.ppermute(value, *groups[link])  34.3 us
    ppermute x10, starting transfers between devices, send(): return lax.ppermute(value, *groups[link])  22.1 us
    pallas_call x1, Pallas kernels, per_device(): pl.pallas_call(functools.partial(step_kernel, False, extent), out_shape=(...  11.4 us
    pallas_call x1, Pallas kernels, per_device(): pl.pallas_call(functools.partial(step_kernel, True, extent), out_shape=(s...  11.4 us
  transfers between devices with their start and end apart: 10, of which 10 were waited for; matrix products, arithmetic and copies ran while one was open for 0% of the time, Pallas kernels for 0%

profile of v3, /device:TPU:342, one launch (start us, length us, event | category | flops | bytes accessed | tf_op | source)
XLA Modules:
  0.0 82.8 jit_solution(9774371012609050345)
XLA Ops:
  1.3 1.6 %prep.1 = (f32[10,8,256]{2,1,0:T(8,128)}, f32[3,8,256]{2,1,0:T(8,128)}) custom-call(s32[1,1]{1,0:T(1,128)S(6)} %copy.27.counts, f32[3,8]{1,0:T(4,128)} %table.1, f32[3,1,1,512]{3,2,1,0:T(1,128)} %fraction.1, f32[3,1,1,512]{3,2,1,0:T(1,128)} %velocity.1, s32[3,1,1,512]{3,2,1,0:T(1,128)} %anchor.1, s32[1,1,512]{2,1,0:T(1,128)} %kinds.1, f32[4,16,256]{2,1,0:T(8,128)} %target.1), custom_call_target="tpu_custom_call" | custom-call | tf_op jit(solution)/shard_map/prep/pallas_call | solution.py:407
  2.9 2.7 %collective-permute-start.1 = (f32[10,8,256]{2,1,0:T(8,128)}, f32[10,8,256]{2,1,0:T(8,128)S(1)}, u32[]{:S(2)}, u32[]{:S(2)}) collective-permute-start(f32[10,8,256]{2,1,0:T(8,128)} %get-tuple-element.9), channel_id=1, source_target_pairs={{0,8},{4,12},{8,0},{12,4},{16,24},{20,28},{24,16},{28,20},{32,40},... | collective-permute-start | bytes 245768 | tf_op jit(solution)/shard_map/ppermute | solution.py:378
  5.6 1.9 %collective-permute-start = (f32[10,8,256]{2,1,0:T(8,128)}, f32[10,8,256]{2,1,0:T(8,128)S(1)}, u32[]{:S(2)}, u32[]{:S(2)}) collective-permute-start(f32[10,8,256]{2,1,0:T(8,128)} %get-tuple-element.9), channel_id=1, source_target_pairs={{8,16},{12,20},{16,8},{20,12},{24,32},{28,36},{32,24},{36,28},{40,... | collective-permute-start | bytes 245768 | tf_op jit(solution)/shard_map/ppermute | solution.py:378
  7.6 0.0 copy-start
  7.6 1.8 %collective-permute-done.1 = f32[10,8,256]{2,1,0:T(8,128)S(1)} collective-permute-done((f32[10,8,256]{2,1,0:T(8,128)}, f32[10,8,256]{2,1,0:T(8,128)S(1)}, u32[]{:S(2)}, u32[]{:S(2)}) %collective-permute-start.1) | collective-permute-done | bytes 81952 | tf_op jit(solution)/shard_map/ppermute | solution.py:378
  9.4 10.1 %collective-permute-done = f32[10,8,256]{2,1,0:T(8,128)S(1)} collective-permute-done((f32[10,8,256]{2,1,0:T(8,128)}, f32[10,8,256]{2,1,0:T(8,128)S(1)}, u32[]{:S(2)}, u32[]{:S(2)}) %collective-permute-start) | collective-permute-done | bytes 81952 | tf_op jit(solution)/shard_map/ppermute | solution.py:378
  19.5 0.0 copy-done
  19.6 4.0 %collective-permute-start.2 = (f32[3,6,8,256]{3,2,1,0:T(8,128)S(1)}, f32[3,6,8,256]{3,2,1,0:T(8,128)S(1)}, u32[]{:S(2)}, u32[]{:S(2)}) collective-permute-start(f32[3,6,8,256]{3,2,1,0:T(8,128)S(1)} %get-tuple-element.29), channel_id=1, source_target_pairs={{1,2},{2,1},{5,6},{6,5},{9,10},{10,9},{13,14},{14,13},{17,18},{18,... | collective-permute-start | bytes 442376 | tf_op jit(solution)/shard_map/ppermute | solution.py:378
  23.6 1.9 %collective-permute-start.3 = (f32[3,6,8,256]{3,2,1,0:T(8,128)S(1)}, f32[3,6,8,256]{3,2,1,0:T(8,128)S(1)}, u32[]{:S(2)}, u32[]{:S(2)}) collective-permute-start(f32[3,6,8,256]{3,2,1,0:T(8,128)S(1)} %get-tuple-element.30), channel_id=1, source_target_pairs={{0,1},{1,0},{2,3},{3,2},{4,5},{5,4},{6,7},{7,6},{8,9},{9,8},{10,11... | collective-permute-start | bytes 442376 | tf_op jit(solution)/shard_map/ppermute | solution.py:378
  25.6 1.2 %collective-permute-done.2 = f32[3,6,8,256]{3,2,1,0:T(8,128)S(1)} collective-permute-done((f32[3,6,8,256]{3,2,1,0:T(8,128)S(1)}, f32[3,6,8,256]{3,2,1,0:T(8,128)S(1)}, u32[]{:S(2)}, u32[]{:S(2)}) %collective-permute-start.2) | collective-permute-done | bytes 147488 | tf_op jit(solution)/shard_map/ppermute | solution.py:378
  26.7 3.9 %collective-permute-done.3 = f32[3,6,8,256]{3,2,1,0:T(8,128)S(1)} collective-permute-done((f32[3,6,8,256]{3,2,1,0:T(8,128)S(1)}, f32[3,6,8,256]{3,2,1,0:T(8,128)S(1)}, u32[]{:S(2)}, u32[]{:S(2)}) %collective-permute-start.3) | collective-permute-done | bytes 147488 | tf_op jit(solution)/shard_map/ppermute | solution.py:378
  30.8 0.0 copy-start.1
  30.9 1.9 %collective-permute-start.4 = (f32[2,22,8,256]{3,2,1,0:T(8,128)S(1)}, f32[2,22,8,256]{3,2,1,0:T(8,128)S(1)}, u32[]{:S(2)}, u32[]{:S(2)}) collective-permute-start(f32[2,22,8,256]{3,2,1,0:T(8,128)S(1)} %pad_maximum_fusion.1), channel_id=1, source_target_pairs={{0,4},{4,0},{8,12},{12,8},{16,20},{20,16},{24,28},{28,24},{32,36},... | collective-permute-start | bytes 1081352 | tf_op jit(solution)/shard_map/ppermute | solution.py:378
  32.8 0.0 copy-done.1
  32.8 1.6 %collective-permute-done.4 = f32[2,22,8,256]{3,2,1,0:T(8,128)S(1)} collective-permute-done((f32[2,22,8,256]{3,2,1,0:T(8,128)S(1)}, f32[2,22,8,256]{3,2,1,0:T(8,128)S(1)}, u32[]{:S(2)}, u32[]{:S(2)}) %collective-permute-start.4) | collective-permute-done | bytes 360480 | tf_op jit(solution)/shard_map/ppermute | solution.py:378
  34.6 11.4 %step.1 = (f32[2,4,256]{2,1,0:T(4,128)S(1)}, f32[3,8,256]{2,1,0:T(8,128)S(1)}, f32[9,32,256]{2,1,0:T(8,128)S(1)}, f32[9,32,256]{2,1,0:T(8,128)S(1)}) custom-call(f32[5,22,8,256]{3,2,1,0:T(8,128)S(1)} %constant_dynamic-update-slice_fusion.full, f32[3,8,256]{2,1,0:T(8,128)S(1)} %broadcast_add_fusion.state), custom_call_target="tpu_custom_call" | custom-call | tf_op jit(solution)/shard_map/step/pallas_call | solution.py:448
  46.0 1.9 %collective-permute-start.6 = (f32[2,4,256]{2,1,0:T(4,128)S(1)}, f32[2,4,256]{2,1,0:T(4,128)S(1)}, u32[]{:S(2)}, u32[]{:S(2)}) collective-permute-start(f32[2,4,256]{2,1,0:T(4,128)S(1)} %get-tuple-element.12), channel_id=1, source_target_pairs={{0,8},{4,12},{8,0},{12,4},{16,24},{20,28},{24,16},{28,20},{32,40},... | collective-permute-start | bytes 24584 | tf_op jit(solution)/shard_map/ppermute | solution.py:378
  47.9 1.9 %collective-permute-start.5 = (f32[2,4,256]{2,1,0:T(4,128)S(1)}, f32[2,4,256]{2,1,0:T(4,128)S(1)}, u32[]{:S(2)}, u32[]{:S(2)}) collective-permute-start(f32[2,4,256]{2,1,0:T(4,128)S(1)} %get-tuple-element.12), channel_id=1, source_target_pairs={{8,16},{12,20},{16,8},{20,12},{24,32},{28,36},{32,24},{36,28},{40,... | collective-permute-start | bytes 24584 | tf_op jit(solution)/shard_map/ppermute | solution.py:378
  49.8 1.7 %collective-permute-done.6 = f32[2,4,256]{2,1,0:T(4,128)S(1)} collective-permute-done((f32[2,4,256]{2,1,0:T(4,128)S(1)}, f32[2,4,256]{2,1,0:T(4,128)S(1)}, u32[]{:S(2)}, u32[]{:S(2)}) %collective-permute-start.6) | collective-permute-done | bytes 8224 | tf_op jit(solution)/shard_map/ppermute | solution.py:378
  51.5 8.9 %collective-permute-done.5 = f32[2,4,256]{2,1,0:T(4,128)S(1)} collective-permute-done((f32[2,4,256]{2,1,0:T(4,128)S(1)}, f32[2,4,256]{2,1,0:T(4,128)S(1)}, u32[]{:S(2)}, u32[]{:S(2)}) %collective-permute-start.5) | collective-permute-done | bytes 8224 | tf_op jit(solution)/shard_map/ppermute | solution.py:378
  60.5 1.9 %collective-permute-start.8 = (f32[3,2,4,256]{3,2,1,0:T(4,128)S(1)}, f32[3,2,4,256]{3,2,1,0:T(4,128)S(1)}, u32[]{:S(2)}, u32[]{:S(2)}) collective-permute-start(f32[3,2,4,256]{3,2,1,0:T(4,128)S(1)} %get-tuple-element.32), channel_id=1, source_target_pairs={{0,1},{1,0},{2,3},{3,2},{4,5},{5,4},{6,7},{7,6},{8,9},{9,8},{10,11... | collective-permute-start | bytes 73736 | tf_op jit(solution)/shard_map/ppermute | solution.py:378
  62.4 1.9 %collective-permute-start.7 = (f32[3,2,4,256]{3,2,1,0:T(4,128)S(1)}, f32[3,2,4,256]{3,2,1,0:T(4,128)S(1)}, u32[]{:S(2)}, u32[]{:S(2)}) collective-permute-start(f32[3,2,4,256]{3,2,1,0:T(4,128)S(1)} %get-tuple-element.32), channel_id=1, source_target_pairs={{1,2},{2,1},{5,6},{6,5},{9,10},{10,9},{13,14},{14,13},{17,18},{18,... | collective-permute-start | bytes 73736 | tf_op jit(solution)/shard_map/ppermute | solution.py:378
  64.4 1.9 %collective-permute-done.8 = f32[3,2,4,256]{3,2,1,0:T(4,128)S(1)} collective-permute-done((f32[3,2,4,256]{3,2,1,0:T(4,128)S(1)}, f32[3,2,4,256]{3,2,1,0:T(4,128)S(1)}, u32[]{:S(2)}, u32[]{:S(2)}) %collective-permute-start.8) | collective-permute-done | bytes 24608 | tf_op jit(solution)/shard_map/ppermute | solution.py:378
  66.2 1.9 %collective-permute-done.7 = f32[3,2,4,256]{3,2,1,0:T(4,128)S(1)} collective-permute-done((f32[3,2,4,256]{3,2,1,0:T(4,128)S(1)}, f32[3,2,4,256]{3,2,1,0:T(4,128)S(1)}, u32[]{:S(2)}, u32[]{:S(2)}) %collective-permute-start.7) | collective-permute-done | bytes 24608 | tf_op jit(solution)/shard_map/ppermute | solution.py:378
  68.2 1.9 %collective-permute-start.9 = (f32[2,3,2,4,256]{4,3,2,1,0:T(4,128)S(1)}, f32[2,3,2,4,256]{4,3,2,1,0:T(4,128)S(1)}, u32[]{:S(2)}, u32[]{:S(2)}) collective-permute-start(f32[2,3,2,4,256]{4,3,2,1,0:T(4,128)S(1)} %pad_maximum_fusion.10), channel_id=1, source_target_pairs={{0,4},{4,0},{8,12},{12,8},{16,20},{20,16},{24,28},{28,24},{32,36},... | collective-permute-start | bytes 147464 | tf_op jit(solution)/shard_map/ppermute | solution.py:378
  70.2 1.2 %collective-permute-done.9 = f32[2,3,2,4,256]{4,3,2,1,0:T(4,128)S(1)} collective-permute-done((f32[2,3,2,4,256]{4,3,2,1,0:T(4,128)S(1)}, f32[2,3,2,4,256]{4,3,2,1,0:T(4,128)S(1)}, u32[]{:S(2)}, u32[]{:S(2)}) %collective-permute-start.9) | collective-permute-done | bytes 49184 | tf_op jit(solution)/shard_map/ppermute | solution.py:378
  71.4 11.4 %step_last.1 = (f32[3,1,1,512]{3,2,1,0:T(1,128)}, f32[3,1,1,512]{3,2,1,0:T(1,128)}, f32[4,16,256]{2,1,0:T(8,128)}) custom-call(f32[5,22,8,256]{3,2,1,0:T(8,128)S(1)} %constant_dynamic-update-slice_fusion.full, f32[3,8,256]{2,1,0:T(8,128)S(1)} %get-tuple-element.11.state, f32[5,3,2,4,256]{4,3,2,1,0:T(4,128)S(1)} %constant_dynamic-update-slice_fusion.3.refs_0_, ...), custom_call_target="tpu_custom_call" | custom-call | tf_op jit(solution)/shard_map/step_last/pallas_call | solution.py:460
  (29 shorter events, 0.5 us)
Async XLA Ops:
  2.9 6.5 %collective-permute-start.1 = (f32[10,8,256]{2,1,0:T(8,128)}, f32[10,8,256]{2,1,0:T(8,128)S(1)}, u32[]{:S(2)}, u32[]{:S(2)}) collective-permute-start(f32[10,8,256]{2,1,0:T(8,128)} %get-tuple-element.9), channel_id=1, source_target_pairs={{0,8},{4,12},{8,0},{12,4},{16,24},{20,28},{24,16},{28,20},{32,40},... | collective-permute-start | bytes 245768 | tf_op jit(solution)/shard_map/ppermute | solution.py:378
  5.6 13.9 %collective-permute-start = (f32[10,8,256]{2,1,0:T(8,128)}, f32[10,8,256]{2,1,0:T(8,128)S(1)}, u32[]{:S(2)}, u32[]{:S(2)}) collective-permute-start(f32[10,8,256]{2,1,0:T(8,128)} %get-tuple-element.9), channel_id=1, source_target_pairs={{8,16},{12,20},{16,8},{20,12},{24,32},{28,36},{32,24},{36,28},{40,... | collective-permute-start | bytes 245768 | tf_op jit(solution)/shard_map/ppermute | solution.py:378
  7.6 12.0 %copy-start = (f32[10,8,256]{2,1,0:T(8,128)S(1)}, f32[10,8,256]{2,1,0:T(8,128)}, u32[]{:S(2)}) copy-start(f32[10,8,256]{2,1,0:T(8,128)} %get-tuple-element.9) | copy-start | bytes 245764
  19.6 7.1 %collective-permute-start.2 = (f32[3,6,8,256]{3,2,1,0:T(8,128)S(1)}, f32[3,6,8,256]{3,2,1,0:T(8,128)S(1)}, u32[]{:S(2)}, u32[]{:S(2)}) collective-permute-start(f32[3,6,8,256]{3,2,1,0:T(8,128)S(1)} %get-tuple-element.29), channel_id=1, source_target_pairs={{1,2},{2,1},{5,6},{6,5},{9,10},{10,9},{13,14},{14,13},{17,18},{18,... | collective-permute-start | bytes 442376 | tf_op jit(solution)/shard_map/ppermute | solution.py:378
  23.6 7.0 %collective-permute-start.3 = (f32[3,6,8,256]{3,2,1,0:T(8,128)S(1)}, f32[3,6,8,256]{3,2,1,0:T(8,128)S(1)}, u32[]{:S(2)}, u32[]{:S(2)}) collective-permute-start(f32[3,6,8,256]{3,2,1,0:T(8,128)S(1)} %get-tuple-element.30), channel_id=1, source_target_pairs={{0,1},{1,0},{2,3},{3,2},{4,5},{5,4},{6,7},{7,6},{8,9},{9,8},{10,11... | collective-permute-start | bytes 442376 | tf_op jit(solution)/shard_map/ppermute | solution.py:378
  30.8 2.0 %copy-start.1 = (f32[3,8,256]{2,1,0:T(8,128)S(1)}, f32[3,8,256]{2,1,0:T(8,128)}, u32[]{:S(2)}) copy-start(f32[3,8,256]{2,1,0:T(8,128)} %get-tuple-element.10) | copy-start | bytes 73732
  30.9 3.6 %collective-permute-start.4 = (f32[2,22,8,256]{3,2,1,0:T(8,128)S(1)}, f32[2,22,8,256]{3,2,1,0:T(8,128)S(1)}, u32[]{:S(2)}, u32[]{:S(2)}) collective-permute-start(f32[2,22,8,256]{3,2,1,0:T(8,128)S(1)} %pad_maximum_fusion.1), channel_id=1, source_target_pairs={{0,4},{4,0},{8,12},{12,8},{16,20},{20,16},{24,28},{28,24},{32,36},... | collective-permute-start | bytes 1081352 | tf_op jit(solution)/shard_map/ppermute | solution.py:378
  46.0 5.5 %collective-permute-start.6 = (f32[2,4,256]{2,1,0:T(4,128)S(1)}, f32[2,4,256]{2,1,0:T(4,128)S(1)}, u32[]{:S(2)}, u32[]{:S(2)}) collective-permute-start(f32[2,4,256]{2,1,0:T(4,128)S(1)} %get-tuple-element.12), channel_id=1, source_target_pairs={{0,8},{4,12},{8,0},{12,4},{16,24},{20,28},{24,16},{28,20},{32,40},... | collective-permute-start | bytes 24584 | tf_op jit(solution)/shard_map/ppermute | solution.py:378
  47.9 12.6 %collective-permute-start.5 = (f32[2,4,256]{2,1,0:T(4,128)S(1)}, f32[2,4,256]{2,1,0:T(4,128)S(1)}, u32[]{:S(2)}, u32[]{:S(2)}) collective-permute-start(f32[2,4,256]{2,1,0:T(4,128)S(1)} %get-tuple-element.12), channel_id=1, source_target_pairs={{8,16},{12,20},{16,8},{20,12},{24,32},{28,36},{32,24},{36,28},{40,... | collective-permute-start | bytes 24584 | tf_op jit(solution)/shard_map/ppermute | solution.py:378
  60.5 5.7 %collective-permute-start.8 = (f32[3,2,4,256]{3,2,1,0:T(4,128)S(1)}, f32[3,2,4,256]{3,2,1,0:T(4,128)S(1)}, u32[]{:S(2)}, u32[]{:S(2)}) collective-permute-start(f32[3,2,4,256]{3,2,1,0:T(4,128)S(1)} %get-tuple-element.32), channel_id=1, source_target_pairs={{0,1},{1,0},{2,3},{3,2},{4,5},{5,4},{6,7},{7,6},{8,9},{9,8},{10,11... | collective-permute-start | bytes 73736 | tf_op jit(solution)/shard_map/ppermute | solution.py:378
  62.4 5.7 %collective-permute-start.7 = (f32[3,2,4,256]{3,2,1,0:T(4,128)S(1)}, f32[3,2,4,256]{3,2,1,0:T(4,128)S(1)}, u32[]{:S(2)}, u32[]{:S(2)}) collective-permute-start(f32[3,2,4,256]{3,2,1,0:T(4,128)S(1)} %get-tuple-element.32), channel_id=1, source_target_pairs={{1,2},{2,1},{5,6},{6,5},{9,10},{10,9},{13,14},{14,13},{17,18},{18,... | collective-permute-start | bytes 73736 | tf_op jit(solution)/shard_map/ppermute | solution.py:378
  68.2 3.1 %collective-permute-start.9 = (f32[2,3,2,4,256]{4,3,2,1,0:T(4,128)S(1)}, f32[2,3,2,4,256]{4,3,2,1,0:T(4,128)S(1)}, u32[]{:S(2)}, u32[]{:S(2)}) collective-permute-start(f32[2,3,2,4,256]{4,3,2,1,0:T(4,128)S(1)} %pad_maximum_fusion.10), channel_id=1, source_target_pairs={{0,4},{4,0},{8,12},{12,8},{16,20},{20,16},{24,28},{28,24},{32,36},... | collective-permute-start | bytes 147464 | tf_op jit(solution)/shard_map/ppermute | solution.py:378

commit v4 on v3

--- a/solution.py
+++ b/solution.py
@@ -10,7 +10,7 @@
 
 EPSILON = 1e-06
 TIME_STEP = 0.5
-BLUR = (1.0 / 16.0, 4.0 / 16.0, 6.0 / 16.0, 4.0 / 16.0, 1.0 / 16.0)
+BLUR = tuple(tap / 4096.0 for tap in (1.0, 4.0, 6.0, 4.0, 1.0))
 KAPPA = 0.8493218002880191
 LANES = 128
 I_ROWS = 64
@@ -52,13 +52,11 @@
     return result.astype(jnp.bfloat16)
 
 
-def rows_filtered(values, weights):
-    radius = (len(weights) - 1) // 2
-    result = weights[radius] * values
-    for shift in range(1, radius + 1):
-        both = pltpu.roll(values, shift, 1) + pltpu.roll(values, values.shape[1] - shift, 1)
-        result = result + weights[radius + shift] * both
-    return result
+def rows_blurred(values):
+    size = values.shape[1]
+    near = pltpu.roll(values, 1, 1) + pltpu.roll(values, size - 1, 1)
+    far = pltpu.roll(values, 2, 1) + pltpu.roll(values, size - 2, 1)
+    return 6.0 * values + 4.0 * near + far
 
 
 def rows_boxed(values):
@@ -74,11 +72,10 @@
     return dot_exact(flat, matrix, ((1,), (0,)), pieces).reshape(values.shape)
 
 
-def planes_filtered(values, weights, count):
-    result = weights[0] * values[0:count]
-    for shift in range(1, len(weights)):
-        result = result + weights[shift] * values[shift : shift + count]
-    return result
+def planes_blurred(values, count):
+    near = values[1 : 1 + count] + values[3 : 3 + count]
+    far = values[0:count] + values[4 : 4 + count]
+    return 6.0 * values[2 : 2 + count] + 4.0 * near + far
 
 
 def plane_inside(place, plane):
@@ -138,62 +135,20 @@
         scaled[plane] = kept * planes[plane + 4]
 
 
-def step_kernel(last, extent, full, state, *refs):
-    place = (state[2, 0:1, :], state[2, 1:2, :], *extent)
+def place_of(state, extent):
+    return (state[2, 0:1, :], state[2, 1:2, :], *extent)
+
+
+def add_pair_block(block, pair_blocks, count):
+    pair_blocks[count, 0:3, :] = KAPPA * (block[0:3] + block[3:6])
+    pair_blocks[count, 3:4, :] = -block[6:7]
+    pair_blocks[count, 4:5, :] = block[7:8]
+    return count + (block[6, 0] > 0.0).astype(jnp.int32)
+
+
+def pair_sums(state, pair_blocks, pair_count, own_columns, sums_in, sums_out):
+    pair_blocks[pair_count] = jnp.zeros((8, LANES), jnp.float32)
     count = state[2, 2, 0].astype(jnp.int32)
-    if last:
-        fractions, scale, scaled, final_velocity, displacement, potential_out = refs[:6]
-    else:
-        fractions_out, state_out, scale, scaled = refs[:4]
-    pair_blocks, spread_blocks, own_columns, sums, density = refs[-5:]
-    density[...] = jnp.zeros(density.shape, jnp.float32)
-    spread_blocks[...] = jnp.zeros(spread_blocks.shape, jnp.float32)
-    sums[...] = jnp.zeros(sums.shape, jnp.float32)
-
-    def block_of(column, index, lanes):
-        block = full[column, index, :, lanes]
-        if last:
-            moved = fractions[column, index // 2, index % 2, :, lanes]
-            return jnp.concatenate([block[0:3], moved[0:3], block[6:8]], 0)
-        return block
-
-    row_index = iota((8, LANES), 0)
-    pair_count = jnp.int32(0)
-    spread_counts = []
-    for column in range(5):
-        spread_count = jnp.int32(0)
-        for side in range(3):
-            shift = jnp.where(
-                row_index == 0,
-                4.0 * (column - 2),
-                jnp.where(row_index == 1, 16.0 * (side - 1), 0.0),
-            )
-            for part in range(4):
-                lanes = pl.ds((part % 2) * LANES, LANES)
-                block = block_of(column, side * 2 + part // 2, lanes) + shift
-                alive = block[6, 0] > 0.0
-                spread_blocks[column, spread_count] = block
-                spread_count = spread_count + alive.astype(jnp.int32)
-                if column in (1, 2, 3):
-                    pair_blocks[pair_count, 0:3, :] = KAPPA * (block[0:3] + block[3:6])
-                    pair_blocks[pair_count, 3:4, :] = -block[6:7]
-                    pair_blocks[pair_count, 4:5, :] = block[7:8]
-                    pair_count = pair_count + alive.astype(jnp.int32)
-        spread_counts.append(spread_count)
-    pair_blocks[pair_count] = jnp.zeros((8, LANES), jnp.float32)
-
-    own_halves = []
-    for half in range(2):
-        own = jnp.concatenate([block_of(2, 2 + half, pl.ds(i * LANES, LANES)) for i in range(2)], 1)
-        own_halves.append(own)
-        packed = jnp.concatenate(
-            [KAPPA * (own[0:3] + own[3:6]), own[7:8], jnp.zeros((4, 256), jnp.float32)], 0
-        )
-        turned = jnp.transpose(packed)
-        rows = pl.ds(half * 256, 256)
-        for row in range(3):
-            own_columns[row, rows, :] = jnp.broadcast_to(turned[:, row : row + 1], (256, LANES))
-        own_columns[3, rows, :] = jnp.broadcast_to(-turned[:, 3:4], (256, LANES))
 
     def add_rows(index, carry):
         rows = pl.ds(index * I_ROWS, I_ROWS)
@@ -212,46 +167,142 @@
                 totals = (totals[0] + factor * x, totals[1] + factor * y, totals[2] + factor * z)
             return totals
 
-        zero = jnp.zeros((I_ROWS, LANES), jnp.float32)
-        totals = lax.fori_loop(0, (pair_count + 1) // 2, add_blocks, (zero, zero, zero))
+        if sums_in is None:
+            totals = (jnp.zeros((I_ROWS, LANES), jnp.float32),) * 3
+        else:
+            totals = tuple(sums_in[axis, rows, :] for axis in range(3))
+        totals = lax.fori_loop(0, (pair_count + 1) // 2, add_blocks, totals)
         for axis in range(3):
-            sums[axis, rows, :] = totals[axis]
+            sums_out[axis, rows, :] = totals[axis]
         return carry
 
     lax.fori_loop(0, (count + I_ROWS - 1) // I_ROWS, add_rows, 0)
 
+
+def chunk_density(chunk, planes, place):
     depth = iota((256, 256), 0).astype(jnp.float32)
     height = iota((32, 256), 0).astype(jnp.float32) - 8.0
-    rows = rows_inside(place, -8, 32)
-
-    def add_chunk(step, column, planes):
-        chunk = jnp.concatenate(
-            [spread_blocks[column, step * 2], spread_blocks[column, step * 2 + 1]], 1
+    fx, fy, fz = chunk[3:4], chunk[4:5], chunk[5:6]
+    charge = chunk[6:7]
+    selected = jnp.where(depth == chunk[2:3], 1.0, 0.0).astype(jnp.bfloat16)
+    weight_y = jnp.where(
+        height == chunk[1:2], 1.0 - fy, jnp.where(height == chunk[1:2] + 1.0, fy, 0.0)
+    )
+    weight_y = jnp.where(rows_inside(place, -8, 32), weight_y, 0.0)
+    weights = []
+    for amount in (charge * (1.0 - fz), charge * fz):
+        for plane in planes:
+            weight_x = jnp.where(
+                chunk[0:1] == plane, 1.0 - fx, jnp.where(chunk[0:1] + 1.0 == plane, fx, 0.0)
+            )
+            weights.append((weight_x * amount * plane_inside(place, plane)) * weight_y)
+    added = dot_exact(jnp.concatenate(weights, 0), selected, ((1,), (1,)))
+    return added.reshape(2, len(planes), 32, 256)
+
+
+def joined(block, moved):
+    return jnp.concatenate([block[0:3], moved[0:3], block[6:8]], 0)
+
+
+def own_kernel(moving, extent, sent, state, *refs):
+    if moving:
+        fractions, own_columns, sums, spread, pair_blocks = refs
+    else:
+        staged, own_columns, sums, spread, pair_blocks = refs
+        staged[...] = state[...]
+    place = place_of(state, extent)
+    pair_count = jnp.int32(0)
+    spread[...] = jnp.zeros(spread.shape, jnp.float32)
+    for half in range(2):
+        own = joined(sent[half], fractions[half]) if moving else sent[half]
+        packed = jnp.concatenate(
+            [KAPPA * (own[0:3] + own[3:6]), own[7:8], jnp.zeros((4, 256), jnp.float32)], 0
         )
-        fx, fy, fz = chunk[3:4], chunk[4:5], chunk[5:6]
-        charge = chunk[6:7]
-        selected = jnp.where(depth == chunk[2:3], 1.0, 0.0).astype(jnp.bfloat16)
-        weight_y = jnp.where(
-            height == chunk[1:2], 1.0 - fy, jnp.where(height == chunk[1:2] + 1.0, fy, 0.0)
-        )
-        weight_y = jnp.where(rows, weight_y, 0.0)
-        weights = []
-        for amount in (charge * (1.0 - fz), charge * fz):
-            for plane in planes:
-                weight_x = jnp.where(
-                    chunk[0:1] == plane, 1.0 - fx, jnp.where(chunk[0:1] + 1.0 == plane, fx, 0.0)
-                )
-                weights.append((weight_x * amount * plane_inside(place, plane)) * weight_y)
-        added = dot_exact(jnp.concatenate(weights, 0), selected, ((1,), (1,)))
-        return added.reshape(2, len(planes), 32, 256)
+        turned = jnp.transpose(packed)
+        rows = pl.ds(half * 256, 256)
+        for row in range(3):
+            own_columns[row, rows, :] = jnp.broadcast_to(turned[:, row : row + 1], (256, LANES))
+        own_columns[3, rows, :] = jnp.broadcast_to(-turned[:, 3:4], (256, LANES))
+        for part in range(2):
+            block = own[:, part * LANES : (part + 1) * LANES]
+            pair_count = add_pair_block(block, pair_blocks, pair_count)
+
+        @pl.when(own[6, 0] > 0.0)
+        def _(own=own):
+            spread[...] += chunk_density(own, range(5), place)
+
+    pair_sums(state, pair_blocks, pair_count, own_columns, None, sums)
+
+
+def column_kernel(moving, full, state, *refs):
+    if moving:
+        fractions, own_columns, sums_in, sums, pair_blocks = refs
+    else:
+        own_columns, sums_in, sums, pair_blocks = refs
+    pair_count = jnp.int32(0)
+    row_index = iota((8, LANES), 0)
+    for side in (0, 2):
+        shift = jnp.where(row_index == 1, 16.0 * (side - 1), 0.0)
+        for part in range(4):
+            lanes = pl.ds((part % 2) * LANES, LANES)
+            block = full[0, side * 2 + part // 2, :, lanes]
+            if moving:
+                block = joined(block, fractions[0, side, part // 2, :, lanes])
+            pair_count = add_pair_block(block + shift, pair_blocks, pair_count)
+    pair_sums(state, pair_blocks, pair_count, own_columns, sums_in, sums)
+
+
+def step_kernel(last, extent, full, state, own_columns, sums_in, spread, *refs):
+    place = place_of(state, extent)
+    if last:
+        fractions, scale, scaled, final_velocity, displacement, potential_out = refs[:6]
+    else:
+        fractions_out, state_out, scale, scaled = refs[:4]
+    pair_blocks, spread_blocks, sums, density = refs[-4:]
+    for part in range(2):
+        density[part, 0:4] = jnp.zeros((4, 32, 256), jnp.float32)
+        density[part, 4:9] = spread[part]
+        density[part, 9:13] = jnp.zeros((4, 32, 256), jnp.float32)
+    spread_blocks[...] = jnp.zeros(spread_blocks.shape, jnp.float32)
+
+    def block_of(column, index, lanes):
+        block = full[column, index, :, lanes]
+        if last:
+            return joined(block, fractions[column, index // 2, index % 2, :, lanes])
+        return block
+
+    row_index = iota((8, LANES), 0)
+    pair_count = jnp.int32(0)
+    spread_counts = []
+    for column in range(5):
+        spread_count = jnp.int32(0)
+        for side in range(3):
+            if (column, side) == (2, 1):
+                continue
+            shift = jnp.where(
+                row_index == 0,
+                4.0 * (column - 2),
+                jnp.where(row_index == 1, 16.0 * (side - 1), 0.0),
+            )
+            for part in range(4):
+                lanes = pl.ds((part % 2) * LANES, LANES)
+                block = block_of(column, side * 2 + part // 2, lanes) + shift
+                spread_blocks[column, spread_count] = block
+                spread_count = spread_count + (block[6, 0] > 0.0).astype(jnp.int32)
+                if column in (1, 3):
+                    pair_count = add_pair_block(block, pair_blocks, pair_count)
+        spread_counts.append(spread_count)
+    pair_sums(state, pair_blocks, pair_count, own_columns, sums_in, sums)
 
     def add_chunks(step, carry):
-        added = [
-            add_chunk(step, column, planes)
-            for column, planes in enumerate(
-                ((-4,), range(-4, 1), range(0, 5), range(4, 9), (8,))
+        added = []
+        for column, planes in enumerate(
+            ((-4,), range(-4, 1), range(0, 5), range(4, 9), (8,))
+        ):
+            chunk = jnp.concatenate(
+                [spread_blocks[column, step * 2], spread_blocks[column, step * 2 + 1]], 1
             )
-        ]
+            added.append(chunk_density(chunk, planes, place))
         for part in range(2):
             far_left, left, own, right, far_right = (added[column][part] for column in range(5))
             pieces = (
@@ -276,23 +327,22 @@
     if not last:
         inverse_scale(place, full, scale, scaled)
     matrix = band(BLUR)
-    value = [planes_filtered(density[part], BLUR, 9) for part in range(2)]
-    value = value[0] + pltpu.roll(value[1], 1, 2)
-    value = depth_filtered(rows_filtered(value, BLUR), matrix, 2)
+    value = density[0] + pltpu.roll(density[1], 1, 2)
+    value = depth_filtered(rows_blurred(planes_blurred(value, 9)), matrix, 2)
     residual = value * scale[...] - scaled[...]
-    value = rows_filtered(planes_filtered(residual, BLUR, 5), BLUR)
-    potential = depth_filtered(value, matrix, 2)
+    potential = depth_filtered(rows_blurred(planes_blurred(residual, 5)), matrix, 2)
     if last:
         potential_out[...] = potential[0:4, 8:24]
 
     field = potential[:, 8:32].reshape(120, 256)
     both = jnp.concatenate([field, pltpu.roll(field, 255, 1)], 0)
     ones = jnp.ones((8, LANES), jnp.bfloat16)
+    depth = iota((256, 256), 0).astype(jnp.float32)
     height = iota((24, 256), 0).astype(jnp.float32)
     rows = rows_inside(place, 0, 24)
     edge = plane_inside(place, 4)
     for half in range(2):
-        own = own_halves[half]
+        own = jnp.concatenate([block_of(2, 2 + half, pl.ds(i * LANES, LANES)) for i in range(2)], 1)
         gx, gy, gz, fx, fy, fz = (own[row : row + 1] for row in range(6))
         selected = jnp.where(depth == gz, 1.0, 0.0).astype(jnp.bfloat16)
         taken = dot_exact(both, selected, ((1,), (0,))).reshape(2, 5, 24, 256)
@@ -327,6 +377,7 @@
             parts = split(sums[axis, pl.ds(half * 256, 256), :], 2)
             pair = dot(ones, parts[0], ((1,), (1,))) + dot(ones, parts[1], ((1,), (1,)))
             force = charge * (pair[0:1] * (1.0 / KAPPA) - gradient[axis])
+            force = jnp.where(charge > 0.0, force, 0.0)
             velocity = values[axis : axis + 1] + TIME_STEP * force / mass
             moved = values[axis + 3 : axis + 4] + TIME_STEP * velocity
             if last:
@@ -386,7 +437,11 @@
     from_odd = send(rows(columns, ~even_row), "rows_odd")
     above = jnp.where(even_row, from_even, from_odd)
     below = jnp.where(even_row, from_odd, from_even)
-    return columns, below, above, functools.partial(send, link="pair")
+
+    def send_partner(value):
+        return send(value, "pair")
+
+    return columns, below, above, send_partner
 
 
 def finish(full, send, first_core):
@@ -412,7 +467,37 @@
         name="prep",
     )(counts, type_table, fraction, velocity, anchor, atom_types, target)
 
-    state = state + jnp.where(cell < 0, 1.0, 0.0)
+    table = shape(4, 512, LANES)
+    totals = shape(3, 512, LANES)
+    spread = shape(2, 5, 32, 256)
+    limit = pltpu.CompilerParams(vmem_limit_bytes=24 << 20)
+
+    def alone(turn, *operands):
+        outs = (table, totals, spread)
+        if turn == 0:
+            outs = (shape(3, 8, 256),) + outs
+        return pl.pallas_call(
+            functools.partial(own_kernel, turn > 0, extent),
+            out_shape=outs,
+            in_specs=[VMEM] * len(operands),
+            out_specs=(VMEM,) * len(outs),
+            scratch_shapes=[pltpu.VMEM((6, 8, LANES), jnp.float32)],
+            name="alone",
+            compiler_params=limit,
+        )(*operands)
+
+    def beside(turn, *operands):
+        return pl.pallas_call(
+            functools.partial(column_kernel, turn > 0),
+            out_shape=totals,
+            in_specs=[VMEM] * len(operands),
+            out_specs=VMEM,
+            scratch_shapes=[pltpu.VMEM((10, 8, LANES), jnp.float32)],
+            name="beside",
+            compiler_params=limit,
+        )(*operands)
+
+    state, own_columns, sums, own_spread = alone(0, own, state)
 
     def rows_first(columns, upper):
         fields = columns[:, 2:].reshape(3, 4, 2, 8, 256)
@@ -435,37 +520,42 @@
         ],
         1,
     )
+    column = full
+    sums = beside(0, column, state, own_columns, sums)
     full = finish(full, send, flags[2])
 
     field = shape(9, 32, 256)
     scratch = [
-        pltpu.VMEM((38, 8, LANES), jnp.float32),
+        pltpu.VMEM((26, 8, LANES), jnp.float32),
         pltpu.VMEM((5, 14, 8, LANES), jnp.float32),
-        pltpu.VMEM((4, 512, LANES), jnp.float32),
         pltpu.VMEM((3, 512, LANES), jnp.float32),
         pltpu.VMEM((2, 13, 32, 256), jnp.float32),
     ]
     fractions, state, scale, scaled = pl.pallas_call(
         functools.partial(step_kernel, False, extent),
         out_shape=(shape(2, 4, 256), shape(3, 8, 256), field, field),
-        in_specs=[VMEM, VMEM],
+        in_specs=[VMEM] * 5,
         out_specs=(VMEM,) * 4,
         scratch_shapes=scratch,
         name="step",
         compiler_params=pltpu.CompilerParams(vmem_limit_bytes=24 << 20),
-    )(full, state)
+    )(full, state, own_columns, sums, own_spread)
+
+    own_columns, sums, own_spread = alone(1, own, state, fractions)
 
     columns, below, above, send = spread_out(fractions, lambda c, upper: c, groups, flags)
-    moved = finish(jnp.stack([below, columns, above], 1), send, flags[2])
+    moved = jnp.stack([below, columns, above], 1)
+    sums = beside(1, column, state, moved, own_columns, sums)
+    moved = finish(moved, send, flags[2])
     return pl.pallas_call(
         functools.partial(step_kernel, True, extent),
         out_shape=(shape(*velocity.shape), shape(*velocity.shape), shape(*target.shape)),
-        in_specs=[VMEM] * 5,
+        in_specs=[VMEM] * 8,
         out_specs=(VMEM,) * 3,
         scratch_shapes=scratch,
         name="step_last",
         compiler_params=pltpu.CompilerParams(vmem_limit_bytes=24 << 20),
-    )(full, state, moved, scale, scaled)
+    )(full, state, own_columns, sums, own_spread, moved, scale, scaled)
 
 
 def solution(mesh):

time: 83.3 us -> 82.7 us (level)
  the two profiles are of different devices: /device:TPU:342 before, /device:TPU:121 now
where the time goes in v4:
time: 82.7 us; the launch traced here: 82.2 us
  starting transfers between devices  42.9 us (52%)
  Pallas kernels  24.7 us (30%)
  waiting for transfers between devices  12.5 us (15%)
  between operations  1.68 us (2%)
    ppermute x10, starting transfers between devices, send(): return lax.ppermute(value, *groups[link])  42.9 us
    ppermute x10, waiting for transfers between devices, send(): return lax.ppermute(value, *groups[link])  12.5 us
    pallas_call x1, Pallas kernels, per_device(): pl.pallas_call(functools.partial(step_kernel, False, extent), out_shape=(...  8.03 us
    pallas_call x1, Pallas kernels, per_device(): pl.pallas_call(functools.partial(step_kernel, True, extent), out_shape=(s...  8.01 us
    pallas_call x2, Pallas kernels, alone(): pl.pallas_call(functools.partial(own_kernel, turn > 0, extent), out_shape...  4.86 us
    pallas_call x2, Pallas kernels, beside(): pl.pallas_call(functools.partial(column_kernel, turn > 0), out_shape=tota...  2.17 us
  transfers between devices with their start and end apart: 10, of which 8 were waited for; matrix products, arithmetic and copies ran while one was open for 0% of the time, Pallas kernels for 9%

profile of v4, /device:TPU:121, one launch (start us, length us, event | category | flops | bytes accessed | tf_op | source)
XLA Modules:
  0.0 82.2 jit_solution(12003549223998725494)
XLA Ops:
  1.3 1.6 %prep.1 = (f32[10,8,256]{2,1,0:T(8,128)}, f32[3,8,256]{2,1,0:T(8,128)}) custom-call(s32[1,1]{1,0:T(1,128)S(6)} %copy.27.counts, f32[3,8]{1,0:T(4,128)} %table.1, f32[3,1,1,512]{3,2,1,0:T(1,128)} %fraction.1, f32[3,1,1,512]{3,2,1,0:T(1,128)} %velocity.1, s32[3,1,1,512]{3,2,1,0:T(1,128)} %anchor.1, s32[1,1,512]{2,1,0:T(1,128)} %kinds.1, f32[4,16,256]{2,1,0:T(8,128)} %target.1), custom_call_target="tpu_custom_call" | custom-call | tf_op jit(solution)/shard_map/prep/pallas_call | solution.py:462
  2.9 12.7 %collective-permute-start = (f32[10,8,256]{2,1,0:T(8,128)}, f32[10,8,256]{2,1,0:T(8,128)S(1)}, u32[]{:S(2)}, u32[]{:S(2)}) collective-permute-start(f32[10,8,256]{2,1,0:T(8,128)} %get-tuple-element.16.sent), channel_id=1, source_target_pairs={{8,16},{12,20},{16,8},{20,12},{24,32},{28,36},{32,24},{36,28},{40,... | collective-permute-start | bytes 245768 | tf_op jit(solution)/shard_map/ppermute | solution.py:429
  15.6 1.9 %collective-permute-start.1 = (f32[10,8,256]{2,1,0:T(8,128)}, f32[10,8,256]{2,1,0:T(8,128)S(1)}, u32[]{:S(2)}, u32[]{:S(2)}) collective-permute-start(f32[10,8,256]{2,1,0:T(8,128)} %get-tuple-element.16.sent), channel_id=1, source_target_pairs={{0,8},{4,12},{8,0},{12,4},{16,24},{20,28},{24,16},{28,20},{32,40},... | collective-permute-start | bytes 245768 | tf_op jit(solution)/shard_map/ppermute | solution.py:429
  17.5 0.0 copy-start
  17.6 0.4 collective-permute-done
  17.9 3.1 %collective-permute-done.1 = f32[10,8,256]{2,1,0:T(8,128)S(1)} collective-permute-done((f32[10,8,256]{2,1,0:T(8,128)}, f32[10,8,256]{2,1,0:T(8,128)S(1)}, u32[]{:S(2)}, u32[]{:S(2)}) %collective-permute-start.1) | collective-permute-done | bytes 81952 | tf_op jit(solution)/shard_map/ppermute | solution.py:429
  21.0 0.0 copy-done
  21.1 3.1 %collective-permute-start.2 = (f32[3,6,8,256]{3,2,1,0:T(8,128)S(1)}, f32[3,6,8,256]{3,2,1,0:T(8,128)S(1)}, u32[]{:S(2)}, u32[]{:S(2)}) collective-permute-start(f32[3,6,8,256]{3,2,1,0:T(8,128)S(1)} %get-tuple-element.43), channel_id=1, source_target_pairs={{1,2},{2,1},{5,6},{6,5},{9,10},{10,9},{13,14},{14,13},{17,18},{18,... | collective-permute-start | bytes 442376 | tf_op jit(solution)/shard_map/ppermute | solution.py:429
  24.2 1.9 %collective-permute-start.3 = (f32[3,6,8,256]{3,2,1,0:T(8,128)S(1)}, f32[3,6,8,256]{3,2,1,0:T(8,128)S(1)}, u32[]{:S(2)}, u32[]{:S(2)}) collective-permute-start(f32[3,6,8,256]{3,2,1,0:T(8,128)S(1)} %get-tuple-element.44), channel_id=1, source_target_pairs={{0,1},{1,0},{2,3},{3,2},{4,5},{5,4},{6,7},{7,6},{8,9},{9,8},{10,11... | collective-permute-start | bytes 442376 | tf_op jit(solution)/shard_map/ppermute | solution.py:429
  26.2 0.8 %collective-permute-done.2 = f32[3,6,8,256]{3,2,1,0:T(8,128)S(1)} collective-permute-done((f32[3,6,8,256]{3,2,1,0:T(8,128)S(1)}, f32[3,6,8,256]{3,2,1,0:T(8,128)S(1)}, u32[]{:S(2)}, u32[]{:S(2)}) %collective-permute-start.2) | collective-permute-done | bytes 147488 | tf_op jit(solution)/shard_map/ppermute | solution.py:429
  27.0 3.1 %collective-permute-done.3 = f32[3,6,8,256]{3,2,1,0:T(8,128)S(1)} collective-permute-done((f32[3,6,8,256]{3,2,1,0:T(8,128)S(1)}, f32[3,6,8,256]{3,2,1,0:T(8,128)S(1)}, u32[]{:S(2)}, u32[]{:S(2)}) %collective-permute-start.3) | collective-permute-done | bytes 147488 | tf_op jit(solution)/shard_map/ppermute | solution.py:429
  30.3 0.0 copy-start.1
  30.3 5.4 %collective-permute-start.4 = (f32[2,22,8,256]{3,2,1,0:T(8,128)S(1)}, f32[2,22,8,256]{3,2,1,0:T(8,128)S(1)}, u32[]{:S(2)}, u32[]{:S(2)}) collective-permute-start(f32[2,22,8,256]{3,2,1,0:T(8,128)S(1)} %pad_maximum_fusion.2), channel_id=1, source_target_pairs={{0,4},{4,0},{8,12},{12,8},{16,20},{20,16},{24,28},{28,24},{32,36},... | collective-permute-start | bytes 1081352 | tf_op jit(solution)/shard_map/ppermute | solution.py:429
  35.8 0.0 copy-done.1
  35.8 2.4 %alone.2 = (f32[3,8,256]{2,1,0:T(8,128)S(1)}, f32[4,512,128]{2,1,0:T(8,128)S(1)}, f32[3,512,128]{2,1,0:T(8,128)S(1)}, f32[2,5,32,256]{3,2,1,0:T(8,128)S(1)}) custom-call(f32[10,8,256]{2,1,0:T(8,128)S(1)} %copy-done, f32[3,8,256]{2,1,0:T(8,128)S(1)} %copy-done.1), custom_call_target="tpu_custom_call" | custom-call | tf_op jit(solution)/shard_map/alone/pallas_call | solution.py:479
  38.3 1.1 %beside.2.sums_in = f32[3,512,128]{2,1,0:T(8,128)S(1)} custom-call(f32[3,22,8,256]{3,2,1,0:T(8,128)S(1)} %pad_maximum_fusion.full, f32[3,8,256]{2,1,0:T(8,128)S(1)} %get-tuple-element.18.state, f32[4,512,128]{2,1,0:T(8,128)S(1)} %get-tuple-element.19.refs_0_.own_columns, f32[3,512,128]{2,1,0:T(8,128)S(1)} %get-tuple-element.20.refs_1_), custom_call_target="tpu_custom_call" | custom-call | tf_op jit(solution)/shard_map/beside/pallas_call | solution.py:490
  39.4 0.0 collective-permute-done.4
  39.5 8.0 %step.1 = (f32[2,4,256]{2,1,0:T(4,128)S(1)}, f32[3,8,256]{2,1,0:T(8,128)S(1)}, f32[9,32,256]{2,1,0:T(8,128)S(1)}, f32[9,32,256]{2,1,0:T(8,128)S(1)}) custom-call(f32[5,22,8,256]{3,2,1,0:T(8,128)S(1)} %constant_dynamic-update-slice_fusion.full, f32[3,8,256]{2,1,0:T(8,128)S(1)} %get-tuple-element.18.state, ...), custom_call_target="tpu_custom_call" | custom-call | tf_op jit(solution)/shard_map/step/pallas_call | solution.py:534
  47.5 8.1 %collective-permute-start.5 = (f32[2,4,256]{2,1,0:T(4,128)S(1)}, f32[2,4,256]{2,1,0:T(4,128)S(1)}, u32[]{:S(2)}, u32[]{:S(2)}) collective-permute-start(f32[2,4,256]{2,1,0:T(4,128)S(1)} %get-tuple-element.23.refs_0_), channel_id=1, source_target_pairs={{8,16},{12,20},{16,8},{20,12},{24,32},{28,36},{32,24},{36,28},{40,... | collective-permute-start | bytes 24584 | tf_op jit(solution)/shard_map/ppermute | solution.py:429
  55.6 1.9 %collective-permute-start.6 = (f32[2,4,256]{2,1,0:T(4,128)S(1)}, f32[2,4,256]{2,1,0:T(4,128)S(1)}, u32[]{:S(2)}, u32[]{:S(2)}) collective-permute-start(f32[2,4,256]{2,1,0:T(4,128)S(1)} %get-tuple-element.23.refs_0_), channel_id=1, source_target_pairs={{0,8},{4,12},{8,0},{12,4},{16,24},{20,28},{24,16},{28,20},{32,40},... | collective-permute-start | bytes 24584 | tf_op jit(solution)/shard_map/ppermute | solution.py:429
  57.6 1.3 %collective-permute-done.5 = f32[2,4,256]{2,1,0:T(4,128)S(1)} collective-permute-done((f32[2,4,256]{2,1,0:T(4,128)S(1)}, f32[2,4,256]{2,1,0:T(4,128)S(1)}, u32[]{:S(2)}, u32[]{:S(2)}) %collective-permute-start.5) | collective-permute-done | bytes 8224 | tf_op jit(solution)/shard_map/ppermute | solution.py:429
  58.9 1.2 %collective-permute-done.6 = f32[2,4,256]{2,1,0:T(4,128)S(1)} collective-permute-done((f32[2,4,256]{2,1,0:T(4,128)S(1)}, f32[2,4,256]{2,1,0:T(4,128)S(1)}, u32[]{:S(2)}, u32[]{:S(2)}) %collective-permute-start.6) | collective-permute-done | bytes 8224 | tf_op jit(solution)/shard_map/ppermute | solution.py:429
  60.1 1.9 %collective-permute-start.7 = (f32[3,2,4,256]{3,2,1,0:T(4,128)S(1)}, f32[3,2,4,256]{3,2,1,0:T(4,128)S(1)}, u32[]{:S(2)}, u32[]{:S(2)}) collective-permute-start(f32[3,2,4,256]{3,2,1,0:T(4,128)S(1)} %get-tuple-element.46), channel_id=1, source_target_pairs={{1,2},{2,1},{5,6},{6,5},{9,10},{10,9},{13,14},{14,13},{17,18},{18,... | collective-permute-start | bytes 73736 | tf_op jit(solution)/shard_map/ppermute | solution.py:429
  62.0 1.9 %collective-permute-start.8 = (f32[3,2,4,256]{3,2,1,0:T(4,128)S(1)}, f32[3,2,4,256]{3,2,1,0:T(4,128)S(1)}, u32[]{:S(2)}, u32[]{:S(2)}) collective-permute-start(f32[3,2,4,256]{3,2,1,0:T(4,128)S(1)} %get-tuple-element.46), channel_id=1, source_target_pairs={{0,1},{1,0},{2,3},{3,2},{4,5},{5,4},{6,7},{7,6},{8,9},{9,8},{10,11... | collective-permute-start | bytes 73736 | tf_op jit(solution)/shard_map/ppermute | solution.py:429
  63.9 0.7 collective-permute-done.7
  64.6 1.9 %collective-permute-done.8 = f32[3,2,4,256]{3,2,1,0:T(4,128)S(1)} collective-permute-done((f32[3,2,4,256]{3,2,1,0:T(4,128)S(1)}, f32[3,2,4,256]{3,2,1,0:T(4,128)S(1)}, u32[]{:S(2)}, u32[]{:S(2)}) %collective-permute-start.8) | collective-permute-done | bytes 24608 | tf_op jit(solution)/shard_map/ppermute | solution.py:429
  66.6 3.9 %collective-permute-start.9 = (f32[2,3,2,4,256]{4,3,2,1,0:T(4,128)S(1)}, f32[2,3,2,4,256]{4,3,2,1,0:T(4,128)S(1)}, u32[]{:S(2)}, u32[]{:S(2)}) collective-permute-start(f32[2,3,2,4,256]{4,3,2,1,0:T(4,128)S(1)} %pad_maximum_fusion.10), channel_id=1, source_target_pairs={{0,4},{4,0},{8,12},{12,8},{16,20},{20,16},{24,28},{28,24},{32,36},... | collective-permute-start | bytes 147464 | tf_op jit(solution)/shard_map/ppermute | solution.py:429
  70.6 2.4 %alone.3 = (f32[4,512,128]{2,1,0:T(8,128)S(1)}, f32[3,512,128]{2,1,0:T(8,128)S(1)}, f32[2,5,32,256]{3,2,1,0:T(8,128)S(1)}) custom-call(f32[10,8,256]{2,1,0:T(8,128)S(1)} %copy-done, f32[3,8,256]{2,1,0:T(8,128)S(1)} %get-tuple-element.22.state, f32[2,4,256]{2,1,0:T(4,128)S(1)} %get-tuple-element.23.refs_0_), custom_call_target="tpu_custom_call" | custom-call | tf_op jit(solution)/shard_map/alone/pallas_call | solution.py:479
  73.0 1.1 %beside.3.sums_in = f32[3,512,128]{2,1,0:T(8,128)S(1)} custom-call(f32[3,22,8,256]{3,2,1,0:T(8,128)S(1)} %pad_maximum_fusion.full, f32[3,8,256]{2,1,0:T(8,128)S(1)} %get-tuple-element.22.state, f32[3,3,2,4,256]{4,3,2,1,0:T(4,128)S(1)} %pad_maximum_fusion.8.refs_0_, f32[4,512,128]{2,1,0:T(8,128)S(1)} %get-tuple-element.24.refs_1_.own_columns, ...), custom_call_target="tpu_custom_call" | custom-call | tf_op jit(solution)/shard_map/beside/pallas_call | solution.py:490
  74.1 0.0 collective-permute-done.9
  74.2 8.0 %step_last.1 = (f32[3,1,1,512]{3,2,1,0:T(1,128)}, f32[3,1,1,512]{3,2,1,0:T(1,128)}, f32[4,16,256]{2,1,0:T(8,128)}) custom-call(f32[5,22,8,256]{3,2,1,0:T(8,128)S(1)} %constant_dynamic-update-slice_fusion.full, f32[3,8,256]{2,1,0:T(8,128)S(1)} %get-tuple-element.22.state, f32[4,512,128]{2,1,0:T(8,128)S(1)} %get-tuple-element.24.refs_1_.own_columns, ...), custom_call_target="tpu_custom_call" | custom-call | tf_op jit(solution)/shard_map/step_last/pallas_call | solution.py:550
  (29 shorter events, 0.5 us)
Async XLA Ops:
  2.9 15.1 %collective-permute-start = (f32[10,8,256]{2,1,0:T(8,128)}, f32[10,8,256]{2,1,0:T(8,128)S(1)}, u32[]{:S(2)}, u32[]{:S(2)}) collective-permute-start(f32[10,8,256]{2,1,0:T(8,128)} %get-tuple-element.16.sent), channel_id=1, source_target_pairs={{8,16},{12,20},{16,8},{20,12},{24,32},{28,36},{32,24},{36,28},{40,... | collective-permute-start | bytes 245768 | tf_op jit(solution)/shard_map/ppermute | solution.py:429
  15.6 5.4 %collective-permute-start.1 = (f32[10,8,256]{2,1,0:T(8,128)}, f32[10,8,256]{2,1,0:T(8,128)S(1)}, u32[]{:S(2)}, u32[]{:S(2)}) collective-permute-start(f32[10,8,256]{2,1,0:T(8,128)} %get-tuple-element.16.sent), channel_id=1, source_target_pairs={{0,8},{4,12},{8,0},{12,4},{16,24},{20,28},{24,16},{28,20},{32,40},... | collective-permute-start | bytes 245768 | tf_op jit(solution)/shard_map/ppermute | solution.py:429
  17.5 3.4 %copy-start = (f32[10,8,256]{2,1,0:T(8,128)S(1)}, f32[10,8,256]{2,1,0:T(8,128)}, u32[]{:S(2)}) copy-start(f32[10,8,256]{2,1,0:T(8,128)} %get-tuple-element.16.sent) | copy-start | bytes 245764
  21.1 5.9 %collective-permute-start.2 = (f32[3,6,8,256]{3,2,1,0:T(8,128)S(1)}, f32[3,6,8,256]{3,2,1,0:T(8,128)S(1)}, u32[]{:S(2)}, u32[]{:S(2)}) collective-permute-start(f32[3,6,8,256]{3,2,1,0:T(8,128)S(1)} %get-tuple-element.43), channel_id=1, source_target_pairs={{1,2},{2,1},{5,6},{6,5},{9,10},{10,9},{13,14},{14,13},{17,18},{18,... | collective-permute-start | bytes 442376 | tf_op jit(solution)/shard_map/ppermute | solution.py:429
  24.2 5.9 %collective-permute-start.3 = (f32[3,6,8,256]{3,2,1,0:T(8,128)S(1)}, f32[3,6,8,256]{3,2,1,0:T(8,128)S(1)}, u32[]{:S(2)}, u32[]{:S(2)}) collective-permute-start(f32[3,6,8,256]{3,2,1,0:T(8,128)S(1)} %get-tuple-element.44), channel_id=1, source_target_pairs={{0,1},{1,0},{2,3},{3,2},{4,5},{5,4},{6,7},{7,6},{8,9},{9,8},{10,11... | collective-permute-start | bytes 442376 | tf_op jit(solution)/shard_map/ppermute | solution.py:429
  30.3 5.5 %copy-start.1 = (f32[3,8,256]{2,1,0:T(8,128)S(1)}, f32[3,8,256]{2,1,0:T(8,128)}, u32[]{:S(2)}) copy-start(f32[3,8,256]{2,1,0:T(8,128)} %get-tuple-element.17.state) | copy-start | bytes 73732
  30.3 9.0 %collective-permute-start.4 = (f32[2,22,8,256]{3,2,1,0:T(8,128)S(1)}, f32[2,22,8,256]{3,2,1,0:T(8,128)S(1)}, u32[]{:S(2)}, u32[]{:S(2)}) collective-permute-start(f32[2,22,8,256]{3,2,1,0:T(8,128)S(1)} %pad_maximum_fusion.2), channel_id=1, source_target_pairs={{0,4},{4,0},{8,12},{12,8},{16,20},{20,16},{24,28},{28,24},{32,36},... | collective-permute-start | bytes 1081352 | tf_op jit(solution)/shard_map/ppermute | solution.py:429
  47.5 11.4 %collective-permute-start.5 = (f32[2,4,256]{2,1,0:T(4,128)S(1)}, f32[2,4,256]{2,1,0:T(4,128)S(1)}, u32[]{:S(2)}, u32[]{:S(2)}) collective-permute-start(f32[2,4,256]{2,1,0:T(4,128)S(1)} %get-tuple-element.23.refs_0_), channel_id=1, source_target_pairs={{8,16},{12,20},{16,8},{20,12},{24,32},{28,36},{32,24},{36,28},{40,... | collective-permute-start | bytes 24584 | tf_op jit(solution)/shard_map/ppermute | solution.py:429
  55.6 4.4 %collective-permute-start.6 = (f32[2,4,256]{2,1,0:T(4,128)S(1)}, f32[2,4,256]{2,1,0:T(4,128)S(1)}, u32[]{:S(2)}, u32[]{:S(2)}) collective-permute-start(f32[2,4,256]{2,1,0:T(4,128)S(1)} %get-tuple-element.23.refs_0_), channel_id=1, source_target_pairs={{0,8},{4,12},{8,0},{12,4},{16,24},{20,28},{24,16},{28,20},{32,40},... | collective-permute-start | bytes 24584 | tf_op jit(solution)/shard_map/ppermute | solution.py:429
  60.1 4.6 %collective-permute-start.7 = (f32[3,2,4,256]{3,2,1,0:T(4,128)S(1)}, f32[3,2,4,256]{3,2,1,0:T(4,128)S(1)}, u32[]{:S(2)}, u32[]{:S(2)}) collective-permute-start(f32[3,2,4,256]{3,2,1,0:T(4,128)S(1)} %get-tuple-element.46), channel_id=1, source_target_pairs={{1,2},{2,1},{5,6},{6,5},{9,10},{10,9},{13,14},{14,13},{17,18},{18,... | collective-permute-start | bytes 73736 | tf_op jit(solution)/shard_map/ppermute | solution.py:429
  62.0 4.6 %collective-permute-start.8 = (f32[3,2,4,256]{3,2,1,0:T(4,128)S(1)}, f32[3,2,4,256]{3,2,1,0:T(4,128)S(1)}, u32[]{:S(2)}, u32[]{:S(2)}) collective-permute-start(f32[3,2,4,256]{3,2,1,0:T(4,128)S(1)} %get-tuple-element.46), channel_id=1, source_target_pairs={{0,1},{1,0},{2,3},{3,2},{4,5},{5,4},{6,7},{7,6},{8,9},{9,8},{10,11... | collective-permute-start | bytes 73736 | tf_op jit(solution)/shard_map/ppermute | solution.py:429
  66.6 7.5 %collective-permute-start.9 = (f32[2,3,2,4,256]{4,3,2,1,0:T(4,128)S(1)}, f32[2,3,2,4,256]{4,3,2,1,0:T(4,128)S(1)}, u32[]{:S(2)}, u32[]{:S(2)}) collective-permute-start(f32[2,3,2,4,256]{4,3,2,1,0:T(4,128)S(1)} %pad_maximum_fusion.10), channel_id=1, source_target_pairs={{0,4},{4,0},{8,12},{12,8},{16,20},{20,16},{24,28},{28,24},{32,36},... | collective-permute-start | bytes 147464 | tf_op jit(solution)/shard_map/ppermute | solution.py:429

commit v5 on v4

--- a/solution.py
+++ b/solution.py
@@ -88,11 +88,18 @@
     return (position >= 0.0) & (position < place[3])
 
 
-def prep_kernel(counts, table, fraction, velocity, anchor, kinds, target, sent, state):
+def prep_kernel(counts, *refs):
+    inputs, (sent, state), held, sems = refs[:6], refs[6:8], refs[8:14], refs[14]
+    copies = [pltpu.make_async_copy(*pair, sems.at[i]) for i, pair in enumerate(zip(inputs, held))]
+    for copy in copies:
+        copy.start()
+    table, fraction, velocity, anchor, kinds, target = held
     info = (lax.axis_index("cells"), lax.axis_index("grp"), counts[0, 0])
     for row, value in enumerate(info):
         state[2, row : row + 1, :] = jnp.full((1, 256), value, jnp.int32).astype(jnp.float32)
     state[2, 3:8, :] = jnp.zeros((5, 256), jnp.float32)
+    for copy in copies:
+        copy.wait()
     for half in range(2):
         lanes = pl.ds(half * 256, 256)
         kind = kinds[0, :, lanes]
@@ -459,13 +466,21 @@
     flags = ((cell // 2) % 2 == 0, group % 2 == 0, cell % 2 == 0)
     extent = (4.0 * cells, 16.0 * groups_count)
 
+    raw = [
+        pltpu.with_memory_space_constraint(value, pltpu.HBM)
+        for value in (type_table, fraction, velocity, anchor, atom_types, target)
+    ]
     own, state = pl.pallas_call(
         prep_kernel,
         out_shape=(shape(10, 8, 256), shape(3, 8, 256)),
-        in_specs=[SMEM, SMEM, VMEM, VMEM, VMEM, VMEM, VMEM],
+        in_specs=[SMEM] + [pl.BlockSpec(memory_space=pltpu.HBM)] * 6,
         out_specs=(VMEM, VMEM),
+        scratch_shapes=[pltpu.SMEM(type_table.shape, jnp.float32)]
+        + [pltpu.VMEM(value.shape, value.dtype) for value in raw[1:]]
+        + [pltpu.SemaphoreType.DMA((6,))],
         name="prep",
-    )(counts, type_table, fraction, velocity, anchor, atom_types, target)
+        compiler_params=pltpu.CompilerParams(vmem_limit_bytes=24 << 20),
+    )(counts, *raw)
 
     table = shape(4, 512, LANES)
     totals = shape(3, 512, LANES)

time: 82.7 us -> 81.8 us (0.989)
  no operation moved by 1% of the time
where the time goes in v5:
time: 81.8 us; the launch traced here: 81.4 us
  starting transfers between devices  42.9 us (52%)
  Pallas kernels  24 us (29%)
  waiting for transfers between devices  12.3 us (15%)
  between operations  1.65 us (2%)
    ppermute x10, starting transfers between devices, send(): return lax.ppermute(value, *groups[link])  42.9 us
    ppermute x10, waiting for transfers between devices, send(): return lax.ppermute(value, *groups[link])  12.3 us
    pallas_call x1, Pallas kernels, per_device(): pl.pallas_call(functools.partial(step_kernel, False, extent), out_shape=(...  8.03 us
    pallas_call x1, Pallas kernels, per_device(): pl.pallas_call(functools.partial(step_kernel, True, extent), out_shape=(s...  8.01 us
    pallas_call x2, Pallas kernels, alone(): pl.pallas_call(functools.partial(own_kernel, turn > 0, extent), out_shape...  4.86 us
    pallas_call x2, Pallas kernels, beside(): pl.pallas_call(functools.partial(column_kernel, turn > 0), out_shape=tota...  2.17 us
  transfers between devices with their start and end apart: 10, of which 8 were waited for; matrix products, arithmetic and copies ran while one was open for 0% of the time, Pallas kernels for 9%

profile of v5, /device:TPU:121, one launch (start us, length us, event | category | flops | bytes accessed | tf_op | source)
XLA Modules:
  0.0 81.4 jit_solution(5991987695258014561)
XLA Ops:
  1.3 1.0 %prep.1 = (f32[10,8,256]{2,1,0:T(8,128)S(1)}, f32[3,8,256]{2,1,0:T(8,128)S(1)}) custom-call(s32[1,1]{1,0:T(1,128)S(6)} %copy.27.counts, f32[3,8]{1,0:T(4,128)} %refs_0_.1, f32[3,1,1,512]{3,2,1,0:T(1,128)} %refs_1_.1, f32[3,1,1,512]{3,2,1,0:T(1,128)} %refs_2_.1, s32[3,1,1,512]{3,2,1,0:T(1,128)} %refs_3_.1, s32[1,1,512]{2,1,0:T(1,128)} %refs_4_.1, ...), custom_call_target="tpu_custom_call" | custom-call | tf_op jit(solution)/shard_map/prep/pallas_call | solution.py:473
  2.3 12.7 %collective-permute-start = (f32[10,8,256]{2,1,0:T(8,128)S(1)}, f32[10,8,256]{2,1,0:T(8,128)S(1)}, u32[]{:S(2)}, u32[]{:S(2)}) collective-permute-start(f32[10,8,256]{2,1,0:T(8,128)S(1)} %get-tuple-element.16.sent), channel_id=1, source_target_pairs={{8,16},{12,20},{16,8},{20,12},{24,32},{28,36},{32,24},{36,28},{40,... | collective-permute-start | bytes 245768 | tf_op jit(solution)/shard_map/ppermute | solution.py:436
  15.0 1.9 %collective-permute-start.1 = (f32[10,8,256]{2,1,0:T(8,128)S(1)}, f32[10,8,256]{2,1,0:T(8,128)S(1)}, u32[]{:S(2)}, u32[]{:S(2)}) collective-permute-start(f32[10,8,256]{2,1,0:T(8,128)S(1)} %get-tuple-element.16.sent), channel_id=1, source_target_pairs={{0,8},{4,12},{8,0},{12,4},{16,24},{20,28},{24,16},{28,20},{32,40},... | collective-permute-start | bytes 245768 | tf_op jit(solution)/shard_map/ppermute | solution.py:436
  17.0 0.2 collective-permute-done
  17.1 3.1 %collective-permute-done.1 = f32[10,8,256]{2,1,0:T(8,128)S(1)} collective-permute-done((f32[10,8,256]{2,1,0:T(8,128)S(1)}, f32[10,8,256]{2,1,0:T(8,128)S(1)}, u32[]{:S(2)}, u32[]{:S(2)}) %collective-permute-start.1) | collective-permute-done | bytes 81952 | tf_op jit(solution)/shard_map/ppermute | solution.py:436
  20.3 3.1 %collective-permute-start.2 = (f32[3,6,8,256]{3,2,1,0:T(8,128)S(1)}, f32[3,6,8,256]{3,2,1,0:T(8,128)S(1)}, u32[]{:S(2)}, u32[]{:S(2)}) collective-permute-start(f32[3,6,8,256]{3,2,1,0:T(8,128)S(1)} %get-tuple-element.43), channel_id=1, source_target_pairs={{1,2},{2,1},{5,6},{6,5},{9,10},{10,9},{13,14},{14,13},{17,18},{18,... | collective-permute-start | bytes 442376 | tf_op jit(solution)/shard_map/ppermute | solution.py:436
  23.4 1.9 %collective-permute-start.3 = (f32[3,6,8,256]{3,2,1,0:T(8,128)S(1)}, f32[3,6,8,256]{3,2,1,0:T(8,128)S(1)}, u32[]{:S(2)}, u32[]{:S(2)}) collective-permute-start(f32[3,6,8,256]{3,2,1,0:T(8,128)S(1)} %get-tuple-element.44), channel_id=1, source_target_pairs={{0,1},{1,0},{2,3},{3,2},{4,5},{5,4},{6,7},{7,6},{8,9},{9,8},{10,11... | collective-permute-start | bytes 442376 | tf_op jit(solution)/shard_map/ppermute | solution.py:436
  25.4 0.8 %collective-permute-done.2 = f32[3,6,8,256]{3,2,1,0:T(8,128)S(1)} collective-permute-done((f32[3,6,8,256]{3,2,1,0:T(8,128)S(1)}, f32[3,6,8,256]{3,2,1,0:T(8,128)S(1)}, u32[]{:S(2)}, u32[]{:S(2)}) %collective-permute-start.2) | collective-permute-done | bytes 147488 | tf_op jit(solution)/shard_map/ppermute | solution.py:436
  26.2 3.1 %collective-permute-done.3 = f32[3,6,8,256]{3,2,1,0:T(8,128)S(1)} collective-permute-done((f32[3,6,8,256]{3,2,1,0:T(8,128)S(1)}, f32[3,6,8,256]{3,2,1,0:T(8,128)S(1)}, u32[]{:S(2)}, u32[]{:S(2)}) %collective-permute-start.3) | collective-permute-done | bytes 147488 | tf_op jit(solution)/shard_map/ppermute | solution.py:436
  29.5 5.4 %collective-permute-start.4 = (f32[2,22,8,256]{3,2,1,0:T(8,128)S(1)}, f32[2,22,8,256]{3,2,1,0:T(8,128)S(1)}, u32[]{:S(2)}, u32[]{:S(2)}) collective-permute-start(f32[2,22,8,256]{3,2,1,0:T(8,128)S(1)} %pad_maximum_fusion.2), channel_id=1, source_target_pairs={{0,4},{4,0},{8,12},{12,8},{16,20},{20,16},{24,28},{28,24},{32,36},... | collective-permute-start | bytes 1081352 | tf_op jit(solution)/shard_map/ppermute | solution.py:436
  35.0 2.4 %alone.2 = (f32[3,8,256]{2,1,0:T(8,128)S(1)}, f32[4,512,128]{2,1,0:T(8,128)S(1)}, f32[3,512,128]{2,1,0:T(8,128)S(1)}, f32[2,5,32,256]{3,2,1,0:T(8,128)S(1)}) custom-call(f32[10,8,256]{2,1,0:T(8,128)S(1)} %get-tuple-element.16.sent, f32[3,8,256]{2,1,0:T(8,128)S(1)} %get-tuple-element.17.state), custom_call_target="tpu_custom_call" | custom-call | tf_op jit(solution)/shard_map/alone/pallas_call | solution.py:494
  37.4 1.1 %beside.2.sums_in = f32[3,512,128]{2,1,0:T(8,128)S(1)} custom-call(f32[3,22,8,256]{3,2,1,0:T(8,128)S(1)} %pad_maximum_fusion.full, f32[3,8,256]{2,1,0:T(8,128)S(1)} %get-tuple-element.18.state, f32[4,512,128]{2,1,0:T(8,128)S(1)} %get-tuple-element.19.refs_0_.own_columns, f32[3,512,128]{2,1,0:T(8,128)S(1)} %get-tuple-element.20.refs_1_), custom_call_target="tpu_custom_call" | custom-call | tf_op jit(solution)/shard_map/beside/pallas_call | solution.py:505
  38.5 0.0 collective-permute-done.4
  38.6 8.0 %step.1 = (f32[2,4,256]{2,1,0:T(4,128)S(1)}, f32[3,8,256]{2,1,0:T(8,128)S(1)}, f32[9,32,256]{2,1,0:T(8,128)S(1)}, f32[9,32,256]{2,1,0:T(8,128)S(1)}) custom-call(f32[5,22,8,256]{3,2,1,0:T(8,128)S(1)} %constant_dynamic-update-slice_fusion.full, f32[3,8,256]{2,1,0:T(8,128)S(1)} %get-tuple-element.18.state, ...), custom_call_target="tpu_custom_call" | custom-call | tf_op jit(solution)/shard_map/step/pallas_call | solution.py:549
  46.7 8.1 %collective-permute-start.5 = (f32[2,4,256]{2,1,0:T(4,128)S(1)}, f32[2,4,256]{2,1,0:T(4,128)S(1)}, u32[]{:S(2)}, u32[]{:S(2)}) collective-permute-start(f32[2,4,256]{2,1,0:T(4,128)S(1)} %get-tuple-element.23.refs_0_), channel_id=1, source_target_pairs={{8,16},{12,20},{16,8},{20,12},{24,32},{28,36},{32,24},{36,28},{40,... | collective-permute-start | bytes 24584 | tf_op jit(solution)/shard_map/ppermute | solution.py:436
  54.8 1.9 %collective-permute-start.6 = (f32[2,4,256]{2,1,0:T(4,128)S(1)}, f32[2,4,256]{2,1,0:T(4,128)S(1)}, u32[]{:S(2)}, u32[]{:S(2)}) collective-permute-start(f32[2,4,256]{2,1,0:T(4,128)S(1)} %get-tuple-element.23.refs_0_), channel_id=1, source_target_pairs={{0,8},{4,12},{8,0},{12,4},{16,24},{20,28},{24,16},{28,20},{32,40},... | collective-permute-start | bytes 24584 | tf_op jit(solution)/shard_map/ppermute | solution.py:436
  56.7 1.3 %collective-permute-done.5 = f32[2,4,256]{2,1,0:T(4,128)S(1)} collective-permute-done((f32[2,4,256]{2,1,0:T(4,128)S(1)}, f32[2,4,256]{2,1,0:T(4,128)S(1)}, u32[]{:S(2)}, u32[]{:S(2)}) %collective-permute-start.5) | collective-permute-done | bytes 8224 | tf_op jit(solution)/shard_map/ppermute | solution.py:436
  58.0 1.2 %collective-permute-done.6 = f32[2,4,256]{2,1,0:T(4,128)S(1)} collective-permute-done((f32[2,4,256]{2,1,0:T(4,128)S(1)}, f32[2,4,256]{2,1,0:T(4,128)S(1)}, u32[]{:S(2)}, u32[]{:S(2)}) %collective-permute-start.6) | collective-permute-done | bytes 8224 | tf_op jit(solution)/shard_map/ppermute | solution.py:436
  59.2 1.9 %collective-permute-start.7 = (f32[3,2,4,256]{3,2,1,0:T(4,128)S(1)}, f32[3,2,4,256]{3,2,1,0:T(4,128)S(1)}, u32[]{:S(2)}, u32[]{:S(2)}) collective-permute-start(f32[3,2,4,256]{3,2,1,0:T(4,128)S(1)} %get-tuple-element.46), channel_id=1, source_target_pairs={{1,2},{2,1},{5,6},{6,5},{9,10},{10,9},{13,14},{14,13},{17,18},{18,... | collective-permute-start | bytes 73736 | tf_op jit(solution)/shard_map/ppermute | solution.py:436
  61.2 1.9 %collective-permute-start.8 = (f32[3,2,4,256]{3,2,1,0:T(4,128)S(1)}, f32[3,2,4,256]{3,2,1,0:T(4,128)S(1)}, u32[]{:S(2)}, u32[]{:S(2)}) collective-permute-start(f32[3,2,4,256]{3,2,1,0:T(4,128)S(1)} %get-tuple-element.46), channel_id=1, source_target_pairs={{0,1},{1,0},{2,3},{3,2},{4,5},{5,4},{6,7},{7,6},{8,9},{9,8},{10,11... | collective-permute-start | bytes 73736 | tf_op jit(solution)/shard_map/ppermute | solution.py:436
  63.1 0.7 collective-permute-done.7
  63.8 1.9 %collective-permute-done.8 = f32[3,2,4,256]{3,2,1,0:T(4,128)S(1)} collective-permute-done((f32[3,2,4,256]{3,2,1,0:T(4,128)S(1)}, f32[3,2,4,256]{3,2,1,0:T(4,128)S(1)}, u32[]{:S(2)}, u32[]{:S(2)}) %collective-permute-start.8) | collective-permute-done | bytes 24608 | tf_op jit(solution)/shard_map/ppermute | solution.py:436
  65.8 3.9 %collective-permute-start.9 = (f32[2,3,2,4,256]{4,3,2,1,0:T(4,128)S(1)}, f32[2,3,2,4,256]{4,3,2,1,0:T(4,128)S(1)}, u32[]{:S(2)}, u32[]{:S(2)}) collective-permute-start(f32[2,3,2,4,256]{4,3,2,1,0:T(4,128)S(1)} %pad_maximum_fusion.10), channel_id=1, source_target_pairs={{0,4},{4,0},{8,12},{12,8},{16,20},{20,16},{24,28},{28,24},{32,36},... | collective-permute-start | bytes 147464 | tf_op jit(solution)/shard_map/ppermute | solution.py:436
  69.8 2.4 %alone.3 = (f32[4,512,128]{2,1,0:T(8,128)S(1)}, f32[3,512,128]{2,1,0:T(8,128)S(1)}, f32[2,5,32,256]{3,2,1,0:T(8,128)S(1)}) custom-call(f32[10,8,256]{2,1,0:T(8,128)S(1)} %get-tuple-element.16.sent, f32[3,8,256]{2,1,0:T(8,128)S(1)} %get-tuple-element.22.state, f32[2,4,256]{2,1,0:T(4,128)S(1)} %get-tuple-element.23.refs_0_), custom_call_target="tpu_custom_call" | custom-call | tf_op jit(solution)/shard_map/alone/pallas_call | solution.py:494
  72.2 1.1 %beside.3.sums_in = f32[3,512,128]{2,1,0:T(8,128)S(1)} custom-call(f32[3,22,8,256]{3,2,1,0:T(8,128)S(1)} %pad_maximum_fusion.full, f32[3,8,256]{2,1,0:T(8,128)S(1)} %get-tuple-element.22.state, f32[3,3,2,4,256]{4,3,2,1,0:T(4,128)S(1)} %pad_maximum_fusion.8.refs_0_, f32[4,512,128]{2,1,0:T(8,128)S(1)} %get-tuple-element.24.refs_1_.own_columns, ...), custom_call_target="tpu_custom_call" | custom-call | tf_op jit(solution)/shard_map/beside/pallas_call | solution.py:505
  73.3 0.0 collective-permute-done.9
  73.4 8.0 %step_last.1 = (f32[3,1,1,512]{3,2,1,0:T(1,128)}, f32[3,1,1,512]{3,2,1,0:T(1,128)}, f32[4,16,256]{2,1,0:T(8,128)}) custom-call(f32[5,22,8,256]{3,2,1,0:T(8,128)S(1)} %constant_dynamic-update-slice_fusion.full, f32[3,8,256]{2,1,0:T(8,128)S(1)} %get-tuple-element.22.state, f32[4,512,128]{2,1,0:T(8,128)S(1)} %get-tuple-element.24.refs_1_.own_columns, ...), custom_call_target="tpu_custom_call" | custom-call | tf_op jit(solution)/shard_map/step_last/pallas_call | solution.py:565
  (29 shorter events, 0.5 us)
Async XLA Ops:
  2.3 14.9 %collective-permute-start = (f32[10,8,256]{2,1,0:T(8,128)S(1)}, f32[10,8,256]{2,1,0:T(8,128)S(1)}, u32[]{:S(2)}, u32[]{:S(2)}) collective-permute-start(f32[10,8,256]{2,1,0:T(8,128)S(1)} %get-tuple-element.16.sent), channel_id=1, source_target_pairs={{8,16},{12,20},{16,8},{20,12},{24,32},{28,36},{32,24},{36,28},{40,... | collective-permute-start | bytes 245768 | tf_op jit(solution)/shard_map/ppermute | solution.py:436
  15.0 5.2 %collective-permute-start.1 = (f32[10,8,256]{2,1,0:T(8,128)S(1)}, f32[10,8,256]{2,1,0:T(8,128)S(1)}, u32[]{:S(2)}, u32[]{:S(2)}) collective-permute-start(f32[10,8,256]{2,1,0:T(8,128)S(1)} %get-tuple-element.16.sent), channel_id=1, source_target_pairs={{0,8},{4,12},{8,0},{12,4},{16,24},{20,28},{24,16},{28,20},{32,40},... | collective-permute-start | bytes 245768 | tf_op jit(solution)/shard_map/ppermute | solution.py:436
  20.3 5.9 %collective-permute-start.2 = (f32[3,6,8,256]{3,2,1,0:T(8,128)S(1)}, f32[3,6,8,256]{3,2,1,0:T(8,128)S(1)}, u32[]{:S(2)}, u32[]{:S(2)}) collective-permute-start(f32[3,6,8,256]{3,2,1,0:T(8,128)S(1)} %get-tuple-element.43), channel_id=1, source_target_pairs={{1,2},{2,1},{5,6},{6,5},{9,10},{10,9},{13,14},{14,13},{17,18},{18,... | collective-permute-start | bytes 442376 | tf_op jit(solution)/shard_map/ppermute | solution.py:436
  23.4 5.9 %collective-permute-start.3 = (f32[3,6,8,256]{3,2,1,0:T(8,128)S(1)}, f32[3,6,8,256]{3,2,1,0:T(8,128)S(1)}, u32[]{:S(2)}, u32[]{:S(2)}) collective-permute-start(f32[3,6,8,256]{3,2,1,0:T(8,128)S(1)} %get-tuple-element.44), channel_id=1, source_target_pairs={{0,1},{1,0},{2,3},{3,2},{4,5},{5,4},{6,7},{7,6},{8,9},{9,8},{10,11... | collective-permute-start | bytes 442376 | tf_op jit(solution)/shard_map/ppermute | solution.py:436
  29.5 9.0 %collective-permute-start.4 = (f32[2,22,8,256]{3,2,1,0:T(8,128)S(1)}, f32[2,22,8,256]{3,2,1,0:T(8,128)S(1)}, u32[]{:S(2)}, u32[]{:S(2)}) collective-permute-start(f32[2,22,8,256]{3,2,1,0:T(8,128)S(1)} %pad_maximum_fusion.2), channel_id=1, source_target_pairs={{0,4},{4,0},{8,12},{12,8},{16,20},{20,16},{24,28},{28,24},{32,36},... | collective-permute-start | bytes 1081352 | tf_op jit(solution)/shard_map/ppermute | solution.py:436
  46.7 11.4 %collective-permute-start.5 = (f32[2,4,256]{2,1,0:T(4,128)S(1)}, f32[2,4,256]{2,1,0:T(4,128)S(1)}, u32[]{:S(2)}, u32[]{:S(2)}) collective-permute-start(f32[2,4,256]{2,1,0:T(4,128)S(1)} %get-tuple-element.23.refs_0_), channel_id=1, source_target_pairs={{8,16},{12,20},{16,8},{20,12},{24,32},{28,36},{32,24},{36,28},{40,... | collective-permute-start | bytes 24584 | tf_op jit(solution)/shard_map/ppermute | solution.py:436
  54.8 4.4 %collective-permute-start.6 = (f32[2,4,256]{2,1,0:T(4,128)S(1)}, f32[2,4,256]{2,1,0:T(4,128)S(1)}, u32[]{:S(2)}, u32[]{:S(2)}) collective-permute-start(f32[2,4,256]{2,1,0:T(4,128)S(1)} %get-tuple-element.23.refs_0_), channel_id=1, source_target_pairs={{0,8},{4,12},{8,0},{12,4},{16,24},{20,28},{24,16},{28,20},{32,40},... | collective-permute-start | bytes 24584 | tf_op jit(solution)/shard_map/ppermute | solution.py:436
  59.2 4.6 %collective-permute-start.7 = (f32[3,2,4,256]{3,2,1,0:T(4,128)S(1)}, f32[3,2,4,256]{3,2,1,0:T(4,128)S(1)}, u32[]{:S(2)}, u32[]{:S(2)}) collective-permute-start(f32[3,2,4,256]{3,2,1,0:T(4,128)S(1)} %get-tuple-element.46), channel_id=1, source_target_pairs={{1,2},{2,1},{5,6},{6,5},{9,10},{10,9},{13,14},{14,13},{17,18},{18,... | collective-permute-start | bytes 73736 | tf_op jit(solution)/shard_map/ppermute | solution.py:436
  61.2 4.6 %collective-permute-start.8 = (f32[3,2,4,256]{3,2,1,0:T(4,128)S(1)}, f32[3,2,4,256]{3,2,1,0:T(4,128)S(1)}, u32[]{:S(2)}, u32[]{:S(2)}) collective-permute-start(f32[3,2,4,256]{3,2,1,0:T(4,128)S(1)} %get-tuple-element.46), channel_id=1, source_target_pairs={{0,1},{1,0},{2,3},{3,2},{4,5},{5,4},{6,7},{7,6},{8,9},{9,8},{10,11... | collective-permute-start | bytes 73736 | tf_op jit(solution)/shard_map/ppermute | solution.py:436
  65.8 7.5 %collective-permute-start.9 = (f32[2,3,2,4,256]{4,3,2,1,0:T(4,128)S(1)}, f32[2,3,2,4,256]{4,3,2,1,0:T(4,128)S(1)}, u32[]{:S(2)}, u32[]{:S(2)}) collective-permute-start(f32[2,3,2,4,256]{4,3,2,1,0:T(4,128)S(1)} %pad_maximum_fusion.10), channel_id=1, source_target_pairs={{0,4},{4,0},{8,12},{12,8},{16,20},{20,16},{24,28},{28,24},{32,36},... | collective-permute-start | bytes 147464 | tf_op jit(solution)/shard_map/ppermute | solution.py:436
